TPU v7x, 512 devices: a whole 4x8x8 slice. The times are simulated.
512 devices in a mesh: lon: 64 (over y_lo, z, core), lat: 8 (over y_hi, x).
Axes of the slice: x: 4, y: 8 (y_hi: 2, y_lo: 4; y = y_hi * 4 + y_lo), z: 8, core: 2. Of those that a mesh axis runs over, the one named last changes fastest.
Arguments:
- final_adjoint: float32 [2, 38, 64, 8192], P(None, None, 'lat', 'lon'), may hold values from -6 to 6
- store: bfloat16 [4, 38, 16, 8, 8192], P(None, None, None, 'lat', 'lon'), may hold values from -6 to 6
- holder_offset: int32 [2, 8, 64], replicated, may hold values from 0 to 7
- holder_slot: int32 [2, 8, 64], replicated, may hold values from 0 to 15, as said below
- bottom_level: int32 [64, 8192], P('lat', 'lon'), may hold values from 0 to 38
- mix_class: int32 [37, 64, 8192], P(None, 'lat', 'lon'), may hold values from 0 to 7
- mix_table: float32 [8], replicated, may hold values from 0.02 to 0.4
Outputs:
- tracer_adjoint: float32 [2, 38, 64, 8192], P(None, None, 'lat', 'lon')
- velocity_adjoint: float32 [2, 38, 64, 8192], P(None, None, 'lat', 'lon')
Inputs may be any that keep to these rules, and one draw needn't show every extreme that they name: `holder_slot`: for every longitude tile, the 16 entries over all steps and bands are all different.
All inputs are finite; a program needn't handle non-finite values.
Results may differ from a plain program's by a relative error of at most 0.0014.
Values may be sent and summed in bfloat16 or wider, within the bound.
No kernel may reach another device: no remote copies, remote signals or barrier semaphores. Data moves between devices by JAX's collectives and lax.ppermute only.
A program may use at most 64 MiB of HBM per device.

v0:
```python
import jax
import jax.numpy as jnp
from jax import lax
from jax.sharding import PartitionSpec as P

STEPS = 2


ADVECT_HALF = 0.125
DIFFUSE = 0.1


def from_partner(block, axis, bit):
    count = lax.axis_size(axis)
    route = []
    for low in range(count):
        high = low | 1 << bit
        if high != low and high < count:
            route += [(low, high), (high, low)]
    return lax.ppermute(block, axis, route)


def with_halo(value, sides, width):
    for axis, dim in sides:
        devices, length = (lax.axis_size(axis), value.shape[dim])
        up = [(i, (i + 1) % devices) for i in range(devices)]
        down = [(j, i) for i, j in up]
        last = lax.slice_in_dim(value, length - width, length, axis=dim)
        first = lax.slice_in_dim(value, 0, width, axis=dim)
        before = lax.ppermute(last, axis, up)
        after = lax.ppermute(first, axis, down)
        value = jnp.concatenate([before, value, after], axis=dim)
    return value


def transpose_step(
    masked,
    east,
    west,
    north,
    south,
    tracer,
    tracer_east,
    tracer_north,
    zonal,
    zonal_west,
    meridional,
    meridional_south,
    south_open,
    kappa_below,
    kappa_above,
):
    below = jnp.concatenate([masked[:, 1:], jnp.zeros_like(masked[:, :1])], axis=1)
    above = jnp.concatenate([jnp.zeros_like(masked[:, :1]), masked[:, :-1]], axis=1)
    advect = (
        zonal * (east - masked)
        + zonal_west * (masked - west)
        + meridional * (north - masked)
        + meridional_south * (masked - south)
    )
    spread = east - masked + (west - masked) + (north - masked) + south_open * (south - masked)
    mixing = kappa_below * (below - masked) + kappa_above * (above - masked)
    result = masked + ADVECT_HALF * advect + DIFFUSE * spread + mixing
    zonal_grad = ADVECT_HALF * jnp.sum((tracer + tracer_east) * (east - masked), axis=0)
    merid_grad = ADVECT_HALF * jnp.sum((tracer + tracer_north) * (north - masked), axis=0)
    return (result, zonal_grad, merid_grad)


def fold_rows(row_block, field_kind):
    moved = row_block
    levels_bits = lax.axis_size("lon").bit_length() - 1
    for bit_index in range(levels_bits):
        if field_kind == "adjoint":
            moved = from_partner(moved.astype(jnp.bfloat16), "lon", bit_index).astype(moved.dtype)
        else:
            moved = from_partner(moved, "lon", bit_index)
    return jnp.flip(moved, axis=-1)


def shards(final_adjoint, store, holder_offset, holder_slot, bottom_level, mix_class, mix_table):
    band_index = lax.axis_index("lat")
    tile_index = lax.axis_index("lon")
    bands = lax.axis_size("lat")
    levels = final_adjoint.shape[1]
    tile_height = final_adjoint.shape[2]
    tile_width = final_adjoint.shape[3]
    top_band = band_index == bands - 1
    ocean_mask = (jnp.arange(levels, dtype=jnp.int32)[:, None, None] < bottom_level[None]).astype(
        jnp.float32
    )
    kappa = jnp.zeros(mix_class.shape, jnp.float32)
    for class_index in range(mix_table.shape[0]):
        kappa = kappa + mix_table[class_index] * (mix_class == class_index).astype(jnp.float32)
    zero_level = jnp.zeros((1, tile_height, tile_width), jnp.float32)
    kappa_below = jnp.concatenate([kappa, zero_level], axis=0)
    kappa_above = jnp.concatenate([zero_level, kappa], axis=0)
    global_rows = band_index * tile_height + jnp.arange(tile_height, dtype=jnp.int32)
    south_open = (global_rows > 0).astype(jnp.float32)[:, None]
    slot_table = lax.dynamic_index_in_dim(holder_slot, tile_index, axis=2, keepdims=False)
    offset_column = lax.dynamic_index_in_dim(holder_offset, tile_index, axis=2, keepdims=False)
    offset_steps = lax.dynamic_index_in_dim(offset_column, band_index, axis=1, keepdims=False)

    def sides(extended, mirrored):
        east = extended[..., 1:-1, 2:]
        west = extended[..., 1:-1, :-2]
        south = extended[..., :-2, 1:-1]
        north = extended[..., 2:, 1:-1]
        north = north.at[..., -1, :].set(jnp.where(top_band, mirrored, north[..., -1, :]))
        return (east, west, north, south)

    adjoint = final_adjoint
    zonal_total = jnp.zeros((levels, tile_height, tile_width), jnp.float32)
    merid_total = jnp.zeros((levels, tile_height, tile_width), jnp.float32)
    for step_index in range(STEPS - 1, -1, -1):
        request = jnp.take(store, slot_table[step_index], axis=2)
        received = lax.all_to_all(request, "lat", split_axis=2, concat_axis=2, tiled=True)
        order = (jnp.arange(bands, dtype=jnp.int32) + offset_steps[step_index]) % bands
        ordered = jnp.take(received, order, axis=2)
        trajectory = ordered.reshape(received.shape[0], received.shape[1], tile_height, tile_width)
        extended_state = with_halo(trajectory, (("lon", 3), ("lat", 2)), 1)
        top_state = jnp.stack([trajectory[0, :, -1], trajectory[1, :, -1], trajectory[3, :, -1]])
        mirror_state = fold_rows(top_state, "trajectory").astype(jnp.float32)
        masked = ocean_mask * adjoint
        extended_adjoint = with_halo(masked, (("lon", 3), ("lat", 2)), 1)
        mirror_adjoint = fold_rows(masked[:, :, -1, :], "adjoint")
        state_wide = extended_state.astype(jnp.float32)
        tracer = trajectory[0:2].astype(jnp.float32)
        zonal = trajectory[2].astype(jnp.float32)
        meridional = trajectory[3].astype(jnp.float32)
        tracer_east, tracer_west, tracer_north, tracer_south = sides(
            state_wide[0:2], mirror_state[0:2]
        )
        zonal_west = state_wide[2, :, 1:-1, :-2]
        meridional_south = state_wide[3, :, :-2, 1:-1] * south_open
        fold_velocity = jnp.where(top_band, mirror_state[2], 0.0)
        meridional_net = meridional.at[:, -1, :].set(meridional[:, -1, :] - fold_velocity)
        east, west, north, south = sides(extended_adjoint, mirror_adjoint)
        adjoint, zonal_grad, merid_grad = transpose_step(
            masked,
            east,
            west,
            north,
            south,
            tracer,
            tracer_east,
            tracer_north,
            zonal,
            zonal_west,
            meridional_net,
            meridional_south,
            south_open,
            kappa_below,
            kappa_above,
        )
        zonal_total = zonal_total + zonal_grad
        merid_total = merid_total + merid_grad
    return (adjoint, jnp.stack([zonal_total, merid_total]))


def solution(mesh):
    return jax.shard_map(
        shards,
        mesh=mesh,
        in_specs=(
            P(None, None, "lat", "lon"),
            P(None, None, None, "lat", "lon"),
            P(),
            P(),
            P("lat", "lon"),
            P(None, "lat", "lon"),
            P(),
        ),
        out_specs=(P(None, None, "lat", "lon"), P(None, None, "lat", "lon")),
        check_vma=False,
    )
```

profile of v0, /device:TPU:6, one launch (start us, length us, event | category | flops | bytes accessed | tf_op | source)
XLA Modules:
  0.0 261.9 jit_solution(3631502479113437797)
XLA Ops:
  4.9 10.2 %all-to-all-start = ((bf16[4,38,8,1,128]{4,0,1,3,2:T(4,128)(2,1)}), bf16[4,38,8,1,128]{4,0,1,3,2:T(4,128)(2,1)S(1)}, u32[]{:S(2)}, u32[]{:S(2)}) async-start(bf16[4,38,8,1,128]{4,0,1,3,2:T(4,128)(2,1)} %fusion.40), calls=%async_computation | async-start | bytes 622592 | tf_op jit(solution)/shard_map/all_to_all | solution.py:116
  15.9 10.2 %collective-permute-start = (f32[2,38,8,1]{3,2,1,0:T(8,128)S(1)}, f32[2,38,8,1]{3,2,1,0:T(8,128)S(1)}, u32[]{:S(2)}, u32[]{:S(2)}) collective-permute-start(f32[2,38,8,1]{3,2,1,0:T(8,128)S(1)} %get-tuple-element.132), channel_id=1, source_target_pairs={{8,0},{16,8},{24,16},{32,24},{40,32},{48,40},{56,48},{64,56},{72,6... | collective-permute-start | bytes 7304 | tf_op jit(solution)/shard_map/ppermute | solution.py:31
  35.2 5.1 %select_add_fusion = f32[37,8,128]{2,1,0:T(8,128)S(1)} fusion(s32[37,8,128]{2,1,0:T(8,128)S(1)} %copy-done.26, f32[]{:T(128)} %bitcast.28, f32[]{:T(128)} %bitcast.27, f32[]{:T(128)} %bitcast.26, f32[]{:T(128)} %bitcast.25, f32[]{:T(128)} %bitcast.24, f32[]{:T(128)} %bitcast.23, f32[]{:T(128)} %bitcast.22, f32[]{:T(128)} %bitcast.21), kind=kLoop, calls=%fused_computation.98 | loop fusion | flops 871424 | bytes 303136 | tf_op jit(solution)/shard_map/add | solution.py:93
  44.6 3.1 %collective-permute-done.14 = bf16[2,38,128]{2,0,1:T(2,128)(2,1)S(1)} collective-permute-done((bf16[2,38,128]{2,0,1:T(2,128)(2,1)S(1)}, bf16[2,38,128]{2,0,1:T(2,128)(2,1)S(1)}, u32[]{:S(2)}, u32[]{:S(2)}) %collective-permute-start.14) | collective-permute-done | bytes 19488 | tf_op jit(solution)/shard_map/ppermute | solution.py:20
  50.2 4.0 %collective-permute-done.15 = bf16[2,38,128]{2,0,1:T(2,128)(2,1)S(1)} collective-permute-done((bf16[2,38,128]{2,0,1:T(2,128)(2,1)S(1)}, bf16[2,38,128]{2,0,1:T(2,128)(2,1)S(1)}, u32[]{:S(2)}, u32[]{:S(2)}) %collective-permute-start.15) | collective-permute-done | bytes 19488 | tf_op jit(solution)/shard_map/ppermute | solution.py:20
  54.2 4.7 %collective-permute-start.16 = (bf16[2,38,128]{2,0,1:T(2,128)(2,1)S(1)}, bf16[2,38,128]{2,0,1:T(2,128)(2,1)S(1)}, u32[]{:S(2)}, u32[]{:S(2)}) collective-permute-start(bf16[2,38,128]{2,0,1:T(2,128)(2,1)S(1)} %collective-permute-done.15), channel_id=1, source_target_pairs={{0,64},{64,0},{8,72},{72,8},{16,80},{80,16},{24,88},{88,24},{32,96... | collective-permute-start | bytes 58376 | tf_op jit(solution)/shard_map/ppermute | solution.py:20
  63.8 3.0 %collective-permute-start.17 = (bf16[2,38,128]{2,0,1:T(2,128)(2,1)S(1)}, bf16[2,38,128]{2,0,1:T(2,128)(2,1)S(1)}, u32[]{:S(2)}, u32[]{:S(2)}) collective-permute-start(bf16[2,38,128]{2,0,1:T(2,128)(2,1)S(1)} %collective-permute-done.16), channel_id=1, source_target_pairs={{0,128},{128,0},{8,136},{136,8},{16,144},{144,16},{24,152},{152,24... | collective-permute-start | bytes 58376 | tf_op jit(solution)/shard_map/ppermute | solution.py:20
  66.8 7.3 %collective-permute-start.19 = (f32[2,38,1,130]{3,2,1,0:T(1,128)S(1)}, f32[2,38,1,130]{3,2,1,0:T(1,128)}, u32[]{:S(2)}, u32[]{:S(2)}) collective-permute-start(f32[2,38,1,130]{3,2,1,0:T(1,128)S(1)} %get-tuple-element.113), channel_id=1, source_target_pairs={{0,1},{1,2},{2,3},{3,4},{4,5},{5,6},{6,7},{7,0},{8,9},{9,10},{10,1... | collective-permute-start | bytes 118568 | tf_op jit(solution)/shard_map/ppermute | solution.py:30
  74.1 4.4 %collective-permute-start.18 = (bf16[2,38,128]{2,0,1:T(2,128)(2,1)S(1)}, bf16[2,38,128]{2,0,1:T(2,128)(2,1)S(1)}, u32[]{:S(2)}, u32[]{:S(2)}) collective-permute-start(bf16[2,38,128]{2,0,1:T(2,128)(2,1)S(1)} %collective-permute-done.17), channel_id=1, source_target_pairs={{0,256},{256,0},{8,264},{264,8},{16,272},{272,16},{24,280},{280,24... | collective-permute-start | bytes 58376 | tf_op jit(solution)/shard_map/ppermute | solution.py:20
  81.8 9.2 %all-to-all-start.1 = ((bf16[4,38,8,1,128]{4,0,1,3,2:T(4,128)(2,1)}), bf16[4,38,8,1,128]{4,0,1,3,2:T(4,128)(2,1)S(1)}, u32[]{:S(2)}, u32[]{:S(2)}) async-start(bf16[4,38,8,1,128]{4,0,1,3,2:T(4,128)(2,1)} %fusion.39), calls=%async_computation.1 | async-start | bytes 622592 | tf_op jit(solution)/shard_map/all_to_all | solution.py:116
  93.0 8.4 %all-to-all-done.1 = bf16[4,38,8,1,128]{4,0,1,3,2:T(4,128)(2,1)S(1)} async-done(((bf16[4,38,8,1,128]{4,0,1,3,2:T(4,128)(2,1)}), bf16[4,38,8,1,128]{4,0,1,3,2:T(4,128)(2,1)S(1)}, u32[]{:S(2)}, u32[]{:S(2)}) %all-to-all-start.1) | async-done | bytes 311328 | tf_op jit(solution)/shard_map/all_to_all | solution.py:116
  105.0 7.5 %collective-permute-start.22 = (bf16[4,38,8,1]{3,2,1,0:T(8,128)(2,1)S(1)}, bf16[4,38,8,1]{3,2,1,0:T(8,128)(2,1)S(1)}, u32[]{:S(2)}, u32[]{:S(2)}) collective-permute-start(bf16[4,38,8,1]{3,2,1,0:T(8,128)(2,1)S(1)} %get-tuple-element.120), channel_id=1, source_target_pairs={{8,0},{16,8},{24,16},{32,24},{40,32},{48,40},{56,48},{64,56},{72,6... | collective-permute-start | bytes 7304 | tf_op jit(solution)/shard_map/ppermute | solution.py:31
  114.5 7.5 %collective-permute-start.2 = (bf16[4,38,8,1]{3,2,1,0:T(8,128)(2,1)}, bf16[4,38,8,1]{3,2,1,0:T(8,128)(2,1)S(1)}, u32[]{:S(2)}, u32[]{:S(2)}) collective-permute-start(bf16[4,38,8,1]{3,2,1,0:T(8,128)(2,1)} %get-tuple-element.131), channel_id=1, source_target_pairs={{8,0},{16,8},{24,16},{32,24},{40,32},{48,40},{56,48},{64,56},{72,6... | collective-permute-start | bytes 7304 | tf_op jit(solution)/shard_map/ppermute | solution.py:31
  135.4 8.9 %collective-permute-start.3 = (bf16[4,38,1,130]{3,2,1,0:T(2,128)(2,1)S(1)}, bf16[4,38,1,130]{3,2,1,0:T(2,128)(2,1)S(1)}, u32[]{:S(2)}, u32[]{:S(2)}) collective-permute-start(bf16[4,38,1,130]{3,2,1,0:T(2,128)(2,1)S(1)} %get-tuple-element.110), channel_id=1, source_target_pairs={{0,1},{1,2},{2,3},{3,4},{4,5},{5,6},{6,7},{7,0},{8,9},{9,10},{10,1... | collective-permute-start | bytes 118568 | tf_op jit(solution)/shard_map/ppermute | solution.py:30
  148.2 3.9 %collective-permute-start.27 = (bf16[3,38,128]{2,0,1:T(4,128)(2,1)S(1)}, bf16[3,38,128]{2,0,1:T(4,128)(2,1)S(1)}, u32[]{:S(2)}, u32[]{:S(2)}) collective-permute-start(bf16[3,38,128]{2,0,1:T(4,128)(2,1)S(1)} %collective-permute-done.26), channel_id=1, source_target_pairs={{0,16},{16,0},{8,24},{24,8},{32,48},{48,32},{40,56},{56,40},{64,80... | collective-permute-start | bytes 87560 | tf_op jit(solution)/shard_map/ppermute | solution.py:20
  153.3 6.6 %collective-permute-done.4 = bf16[4,38,1,130]{3,2,1,0:T(2,128)(2,1)S(1)} collective-permute-done((bf16[4,38,1,130]{3,2,1,0:T(2,128)(2,1)S(1)}, bf16[4,38,1,130]{3,2,1,0:T(2,128)(2,1)S(1)}, u32[]{:S(2)}, u32[]{:S(2)}) %collective-permute-start.4) | collective-permute-done | bytes 39552 | tf_op jit(solution)/shard_map/ppermute | solution.py:31
  164.6 4.8 %collective-permute-start.28 = (bf16[3,38,128]{2,0,1:T(4,128)(2,1)S(1)}, bf16[3,38,128]{2,0,1:T(4,128)(2,1)S(1)}, u32[]{:S(2)}, u32[]{:S(2)}) collective-permute-start(bf16[3,38,128]{2,0,1:T(4,128)(2,1)S(1)} %collective-permute-done.27), channel_id=1, source_target_pairs={{0,32},{32,0},{8,40},{40,8},{16,48},{48,16},{24,56},{56,24},{64,96... | collective-permute-start | bytes 87560 | tf_op jit(solution)/shard_map/ppermute | solution.py:20
  172.1 7.8 %collective-permute-start.29 = (bf16[3,38,128]{2,0,1:T(4,128)(2,1)S(1)}, bf16[3,38,128]{2,0,1:T(4,128)(2,1)S(1)}, u32[]{:S(2)}, u32[]{:S(2)}) collective-permute-start(bf16[3,38,128]{2,0,1:T(4,128)(2,1)S(1)} %collective-permute-done.28), channel_id=1, source_target_pairs={{0,64},{64,0},{8,72},{72,8},{16,80},{80,16},{24,88},{88,24},{32,96... | collective-permute-start | bytes 87560 | tf_op jit(solution)/shard_map/ppermute | solution.py:20
  182.0 3.9 %collective-permute-start.30 = (bf16[3,38,128]{2,0,1:T(4,128)(2,1)S(1)}, bf16[3,38,128]{2,0,1:T(4,128)(2,1)}, u32[]{:S(2)}, u32[]{:S(2)}) collective-permute-start(bf16[3,38,128]{2,0,1:T(4,128)(2,1)S(1)} %collective-permute-done.29), channel_id=1, source_target_pairs={{0,128},{128,0},{8,136},{136,8},{16,144},{144,16},{24,152},{152,24... | collective-permute-start | bytes 87560 | tf_op jit(solution)/shard_map/ppermute | solution.py:20
  188.9 4.6 %collective-permute-start.31 = (bf16[3,38,128]{2,0,1:T(4,128)(2,1)}, bf16[3,38,128]{2,0,1:T(4,128)(2,1)}, u32[]{:S(2)}, u32[]{:S(2)}) collective-permute-start(bf16[3,38,128]{2,0,1:T(4,128)(2,1)} %collective-permute-done.30), channel_id=1, source_target_pairs={{0,256},{256,0},{8,264},{264,8},{16,272},{272,16},{24,280},{280,24... | collective-permute-start | bytes 87560 | tf_op jit(solution)/shard_map/ppermute | solution.py:20
  202.0 4.0 %collective-permute-start.20 = (f32[2,38,8,1]{3,2,1,0:T(8,128)}, f32[2,38,8,1]{3,2,1,0:T(8,128)S(1)}, u32[]{:S(2)}, u32[]{:S(2)}) collective-permute-start(f32[2,38,8,1]{3,2,1,0:T(8,128)} %get-tuple-element.121), channel_id=1, source_target_pairs={{8,0},{16,8},{24,16},{32,24},{40,32},{48,40},{56,48},{64,56},{72,6... | collective-permute-start | bytes 7304 | tf_op jit(solution)/shard_map/ppermute | solution.py:31
  210.6 3.3 %collective-permute-done.34 = bf16[2,38,128]{2,0,1:T(2,128)(2,1)} collective-permute-done((bf16[2,38,128]{2,0,1:T(2,128)(2,1)}, bf16[2,38,128]{2,0,1:T(2,128)(2,1)}, u32[]{:S(2)}, u32[]{:S(2)}) %collective-permute-start.34) | collective-permute-done | bytes 19488 | tf_op jit(solution)/shard_map/ppermute | solution.py:20
  220.8 4.3 %collective-permute-start.36 = (bf16[2,38,128]{2,0,1:T(2,128)(2,1)}, bf16[2,38,128]{2,0,1:T(2,128)(2,1)S(1)}, u32[]{:S(2)}, u32[]{:S(2)}) collective-permute-start(bf16[2,38,128]{2,0,1:T(2,128)(2,1)} %collective-permute-done.35), channel_id=1, source_target_pairs={{0,64},{64,0},{8,72},{72,8},{16,80},{80,16},{24,88},{88,24},{32,96... | collective-permute-start | bytes 58376 | tf_op jit(solution)/shard_map/ppermute | solution.py:20
  239.0 9.9 %collective-permute-start.39 = (f32[2,38,1,130]{3,2,1,0:T(1,128)}, f32[2,38,1,130]{3,2,1,0:T(1,128)}, u32[]{:S(2)}, u32[]{:S(2)}) collective-permute-start(f32[2,38,1,130]{3,2,1,0:T(1,128)} %get-tuple-element.109), channel_id=1, source_target_pairs={{0,1},{1,2},{2,3},{3,4},{4,5},{5,6},{6,7},{7,0},{8,9},{9,10},{10,1... | collective-permute-start | bytes 118568 | tf_op jit(solution)/shard_map/ppermute | solution.py:30
  (213 shorter events, 113.5 us)
Async XLA Ops:
  4.9 76.3 %all-to-all-start = ((bf16[4,38,8,1,128]{4,0,1,3,2:T(4,128)(2,1)}), bf16[4,38,8,1,128]{4,0,1,3,2:T(4,128)(2,1)S(1)}, u32[]{:S(2)}, u32[]{:S(2)}) async-start(bf16[4,38,8,1,128]{4,0,1,3,2:T(4,128)(2,1)} %fusion.40), calls=%async_computation | async-start | bytes 622592 | tf_op jit(solution)/shard_map/all_to_all | solution.py:116
  15.9 43.0 %collective-permute-start = (f32[2,38,8,1]{3,2,1,0:T(8,128)S(1)}, f32[2,38,8,1]{3,2,1,0:T(8,128)S(1)}, u32[]{:S(2)}, u32[]{:S(2)}) collective-permute-start(f32[2,38,8,1]{3,2,1,0:T(8,128)S(1)} %get-tuple-element.132), channel_id=1, source_target_pairs={{8,0},{16,8},{24,16},{32,24},{40,32},{48,40},{56,48},{64,56},{72,6... | collective-permute-start | bytes 7304 | tf_op jit(solution)/shard_map/ppermute | solution.py:31
  26.1 32.9 %collective-permute-start.5 = (f32[2,38,8,1]{3,2,1,0:T(8,128)S(1)}, f32[2,38,8,1]{3,2,1,0:T(8,128)S(1)}, u32[]{:S(2)}, u32[]{:S(2)}) collective-permute-start(f32[2,38,8,1]{3,2,1,0:T(8,128)S(1)} %get-tuple-element.133), channel_id=1, source_target_pairs={{0,8},{8,16},{16,24},{24,32},{32,40},{40,48},{48,56},{56,64},{64,7... | collective-permute-start | bytes 7304 | tf_op jit(solution)/shard_map/ppermute | solution.py:30
  28.1 13.9 %collective-permute-start.13 = (bf16[2,38,128]{2,0,1:T(2,128)(2,1)S(1)}, bf16[2,38,128]{2,0,1:T(2,128)(2,1)S(1)}, u32[]{:S(2)}, u32[]{:S(2)}) collective-permute-start(bf16[2,38,128]{2,0,1:T(2,128)(2,1)S(1)} %bitcast.147), channel_id=1, source_target_pairs={{0,8},{8,0},{16,24},{24,16},{32,40},{40,32},{48,56},{56,48},{64,72... | collective-permute-start | bytes 58376 | tf_op jit(solution)/shard_map/ppermute | solution.py:20
  59.5 19.0 %collective-permute-start.12 = (f32[2,38,1,130]{3,2,1,0:T(1,128)S(1)}, f32[2,38,1,130]{3,2,1,0:T(1,128)S(1)}, u32[]{:S(2)}, u32[]{:S(2)}) collective-permute-start(f32[2,38,1,130]{3,2,1,0:T(1,128)S(1)} %get-tuple-element.112), channel_id=1, source_target_pairs={{1,0},{2,1},{3,2},{4,3},{5,4},{6,5},{7,6},{0,7},{9,8},{10,9},{11,1... | collective-permute-start | bytes 118568 | tf_op jit(solution)/shard_map/ppermute | solution.py:31
  66.8 127.2 %collective-permute-start.19 = (f32[2,38,1,130]{3,2,1,0:T(1,128)S(1)}, f32[2,38,1,130]{3,2,1,0:T(1,128)}, u32[]{:S(2)}, u32[]{:S(2)}) collective-permute-start(f32[2,38,1,130]{3,2,1,0:T(1,128)S(1)} %get-tuple-element.113), channel_id=1, source_target_pairs={{0,1},{1,2},{2,3},{3,4},{4,5},{5,6},{6,7},{7,0},{8,9},{9,10},{10,1... | collective-permute-start | bytes 118568 | tf_op jit(solution)/shard_map/ppermute | solution.py:30
  81.8 19.6 %all-to-all-start.1 = ((bf16[4,38,8,1,128]{4,0,1,3,2:T(4,128)(2,1)}), bf16[4,38,8,1,128]{4,0,1,3,2:T(4,128)(2,1)S(1)}, u32[]{:S(2)}, u32[]{:S(2)}) async-start(bf16[4,38,8,1,128]{4,0,1,3,2:T(4,128)(2,1)} %fusion.39), calls=%async_computation.1 | async-start | bytes 622592 | tf_op jit(solution)/shard_map/all_to_all | solution.py:116
  103.0 20.6 %collective-permute-start.21 = (bf16[4,38,8,1]{3,2,1,0:T(8,128)(2,1)S(1)}, bf16[4,38,8,1]{3,2,1,0:T(8,128)(2,1)S(1)}, u32[]{:S(2)}, u32[]{:S(2)}) collective-permute-start(bf16[4,38,8,1]{3,2,1,0:T(8,128)(2,1)S(1)} %get-tuple-element.119), channel_id=1, source_target_pairs={{0,8},{8,16},{16,24},{24,32},{32,40},{40,48},{48,56},{56,64},{64,7... | collective-permute-start | bytes 7304 | tf_op jit(solution)/shard_map/ppermute | solution.py:30
  105.0 20.6 %collective-permute-start.22 = (bf16[4,38,8,1]{3,2,1,0:T(8,128)(2,1)S(1)}, bf16[4,38,8,1]{3,2,1,0:T(8,128)(2,1)S(1)}, u32[]{:S(2)}, u32[]{:S(2)}) collective-permute-start(bf16[4,38,8,1]{3,2,1,0:T(8,128)(2,1)S(1)} %get-tuple-element.120), channel_id=1, source_target_pairs={{8,0},{16,8},{24,16},{32,24},{40,32},{48,40},{56,48},{64,56},{72,6... | collective-permute-start | bytes 7304 | tf_op jit(solution)/shard_map/ppermute | solution.py:31
  112.5 16.2 %collective-permute-start.1 = (bf16[4,38,8,1]{3,2,1,0:T(8,128)(2,1)S(1)}, bf16[4,38,8,1]{3,2,1,0:T(8,128)(2,1)S(1)}, u32[]{:S(2)}, u32[]{:S(2)}) collective-permute-start(bf16[4,38,8,1]{3,2,1,0:T(8,128)(2,1)S(1)} %get-tuple-element.130), channel_id=1, source_target_pairs={{0,8},{8,16},{16,24},{24,32},{32,40},{40,48},{48,56},{56,64},{64,7... | collective-permute-start | bytes 7304 | tf_op jit(solution)/shard_map/ppermute | solution.py:30
  114.5 17.2 %collective-permute-start.2 = (bf16[4,38,8,1]{3,2,1,0:T(8,128)(2,1)}, bf16[4,38,8,1]{3,2,1,0:T(8,128)(2,1)S(1)}, u32[]{:S(2)}, u32[]{:S(2)}) collective-permute-start(bf16[4,38,8,1]{3,2,1,0:T(8,128)(2,1)} %get-tuple-element.131), channel_id=1, source_target_pairs={{8,0},{16,8},{24,16},{32,24},{40,32},{48,40},{56,48},{64,56},{72,6... | collective-permute-start | bytes 7304 | tf_op jit(solution)/shard_map/ppermute | solution.py:31
  125.6 18.8 %collective-permute-start.26 = (bf16[3,38,128]{2,0,1:T(4,128)(2,1)S(1)}, bf16[3,38,128]{2,0,1:T(4,128)(2,1)S(1)}, u32[]{:S(2)}, u32[]{:S(2)}) collective-permute-start(bf16[3,38,128]{2,0,1:T(4,128)(2,1)S(1)} %pad_maximum_fusion.38), channel_id=1, source_target_pairs={{0,8},{8,0},{16,24},{24,16},{32,40},{40,32},{48,56},{56,48},{64,72... | collective-permute-start | bytes 87560 | tf_op jit(solution)/shard_map/ppermute | solution.py:20
  128.8 17.5 %collective-permute-start.23 = (bf16[4,38,1,130]{3,2,1,0:T(2,128)(2,1)S(1)}, bf16[4,38,1,130]{3,2,1,0:T(2,128)(2,1)S(1)}, u32[]{:S(2)}, u32[]{:S(2)}) collective-permute-start(bf16[4,38,1,130]{3,2,1,0:T(2,128)(2,1)S(1)} %get-tuple-element.106), channel_id=1, source_target_pairs={{0,1},{1,2},{2,3},{3,4},{4,5},{5,6},{6,7},{7,0},{8,9},{9,10},{10,1... | collective-permute-start | bytes 118568 | tf_op jit(solution)/shard_map/ppermute | solution.py:30
  131.7 16.5 %collective-permute-start.24 = (bf16[4,38,1,130]{3,2,1,0:T(2,128)(2,1)S(1)}, bf16[4,38,1,130]{3,2,1,0:T(2,128)(2,1)S(1)}, u32[]{:S(2)}, u32[]{:S(2)}) collective-permute-start(bf16[4,38,1,130]{3,2,1,0:T(2,128)(2,1)S(1)} %get-tuple-element.107), channel_id=1, source_target_pairs={{1,0},{2,1},{3,2},{4,3},{5,4},{6,5},{7,6},{0,7},{9,8},{10,9},{11,1... | collective-permute-start | bytes 118568 | tf_op jit(solution)/shard_map/ppermute | solution.py:31
  135.4 17.9 %collective-permute-start.3 = (bf16[4,38,1,130]{3,2,1,0:T(2,128)(2,1)S(1)}, bf16[4,38,1,130]{3,2,1,0:T(2,128)(2,1)S(1)}, u32[]{:S(2)}, u32[]{:S(2)}) collective-permute-start(bf16[4,38,1,130]{3,2,1,0:T(2,128)(2,1)S(1)} %get-tuple-element.110), channel_id=1, source_target_pairs={{0,1},{1,2},{2,3},{3,4},{4,5},{5,6},{6,7},{7,0},{8,9},{9,10},{10,1... | collective-permute-start | bytes 118568 | tf_op jit(solution)/shard_map/ppermute | solution.py:30
  144.4 15.5 %collective-permute-start.4 = (bf16[4,38,1,130]{3,2,1,0:T(2,128)(2,1)S(1)}, bf16[4,38,1,130]{3,2,1,0:T(2,128)(2,1)S(1)}, u32[]{:S(2)}, u32[]{:S(2)}) collective-permute-start(bf16[4,38,1,130]{3,2,1,0:T(2,128)(2,1)S(1)} %get-tuple-element.111), channel_id=1, source_target_pairs={{1,0},{2,1},{3,2},{4,3},{5,4},{6,5},{7,6},{0,7},{9,8},{10,9},{11,1... | collective-permute-start | bytes 118568 | tf_op jit(solution)/shard_map/ppermute | solution.py:31
  146.3 15.6 %collective-permute-start.7 = (bf16[3,38,128]{2,0,1:T(4,128)(2,1)S(1)}, bf16[3,38,128]{2,0,1:T(4,128)(2,1)S(1)}, u32[]{:S(2)}, u32[]{:S(2)}) collective-permute-start(bf16[3,38,128]{2,0,1:T(4,128)(2,1)S(1)} %collective-permute-done.6), channel_id=1, source_target_pairs={{0,16},{16,0},{8,24},{24,8},{32,48},{48,32},{40,56},{56,40},{64,80... | collective-permute-start | bytes 87560 | tf_op jit(solution)/shard_map/ppermute | solution.py:20
  148.2 16.3 %collective-permute-start.27 = (bf16[3,38,128]{2,0,1:T(4,128)(2,1)S(1)}, bf16[3,38,128]{2,0,1:T(4,128)(2,1)S(1)}, u32[]{:S(2)}, u32[]{:S(2)}) collective-permute-start(bf16[3,38,128]{2,0,1:T(4,128)(2,1)S(1)} %collective-permute-done.26), channel_id=1, source_target_pairs={{0,16},{16,0},{8,24},{24,8},{32,48},{48,32},{40,56},{56,40},{64,80... | collective-permute-start | bytes 87560 | tf_op jit(solution)/shard_map/ppermute | solution.py:20
  188.9 12.2 %collective-permute-start.31 = (bf16[3,38,128]{2,0,1:T(4,128)(2,1)}, bf16[3,38,128]{2,0,1:T(4,128)(2,1)}, u32[]{:S(2)}, u32[]{:S(2)}) collective-permute-start(bf16[3,38,128]{2,0,1:T(4,128)(2,1)} %collective-permute-done.30), channel_id=1, source_target_pairs={{0,256},{256,0},{8,264},{264,8},{16,272},{272,16},{24,280},{280,24... | collective-permute-start | bytes 87560 | tf_op jit(solution)/shard_map/ppermute | solution.py:20
  202.0 23.0 %collective-permute-start.20 = (f32[2,38,8,1]{3,2,1,0:T(8,128)}, f32[2,38,8,1]{3,2,1,0:T(8,128)S(1)}, u32[]{:S(2)}, u32[]{:S(2)}) collective-permute-start(f32[2,38,8,1]{3,2,1,0:T(8,128)} %get-tuple-element.121), channel_id=1, source_target_pairs={{8,0},{16,8},{24,16},{32,24},{40,32},{48,40},{56,48},{64,56},{72,6... | collective-permute-start | bytes 7304 | tf_op jit(solution)/shard_map/ppermute | solution.py:31
  206.0 19.1 %collective-permute-start.25 = (f32[2,38,8,1]{3,2,1,0:T(8,128)}, f32[2,38,8,1]{3,2,1,0:T(8,128)}, u32[]{:S(2)}, u32[]{:S(2)}) collective-permute-start(f32[2,38,8,1]{3,2,1,0:T(8,128)} %get-tuple-element.122), channel_id=1, source_target_pairs={{0,8},{8,16},{16,24},{24,32},{32,40},{40,48},{48,56},{56,64},{64,7... | collective-permute-start | bytes 7304 | tf_op jit(solution)/shard_map/ppermute | solution.py:30
  227.4 24.1 %collective-permute-start.32 = (f32[2,38,1,130]{3,2,1,0:T(1,128)}, f32[2,38,1,130]{3,2,1,0:T(1,128)S(1)}, u32[]{:S(2)}, u32[]{:S(2)}) collective-permute-start(f32[2,38,1,130]{3,2,1,0:T(1,128)} %get-tuple-element.108), channel_id=1, source_target_pairs={{1,0},{2,1},{3,2},{4,3},{5,4},{6,5},{7,6},{0,7},{9,8},{10,9},{11,1... | collective-permute-start | bytes 118568 | tf_op jit(solution)/shard_map/ppermute | solution.py:31
  230.9 18.1 %collective-permute-start.37 = (bf16[2,38,128]{2,0,1:T(2,128)(2,1)S(1)}, bf16[2,38,128]{2,0,1:T(2,128)(2,1)}, u32[]{:S(2)}, u32[]{:S(2)}) collective-permute-start(bf16[2,38,128]{2,0,1:T(2,128)(2,1)S(1)} %collective-permute-done.36), channel_id=1, source_target_pairs={{0,128},{128,0},{8,136},{136,8},{16,144},{144,16},{24,152},{152,24... | collective-permute-start | bytes 58376 | tf_op jit(solution)/shard_map/ppermute | solution.py:20
  239.0 19.9 %collective-permute-start.39 = (f32[2,38,1,130]{3,2,1,0:T(1,128)}, f32[2,38,1,130]{3,2,1,0:T(1,128)}, u32[]{:S(2)}, u32[]{:S(2)}) collective-permute-start(f32[2,38,1,130]{3,2,1,0:T(1,128)} %get-tuple-element.109), channel_id=1, source_target_pairs={{0,1},{1,2},{2,3},{3,4},{4,5},{5,6},{6,7},{7,0},{8,9},{9,10},{10,1... | collective-permute-start | bytes 118568 | tf_op jit(solution)/shard_map/ppermute | solution.py:30
  (48 other events, 356.2 us)
where the time goes:
time: 264 us; the launch traced here: 262 us
  starting transfers between devices  167 us (63%)
  waiting for transfers between devices  35.3 us (13%)
  other arithmetic  31.8 us (12%)
  local copies, waits for them, and re-layouts  26 us (10%)
    ppermute x24, starting transfers between devices, from_partner(): return lax.ppermute(block, axis, route)  72.1 us
    ppermute x8, starting transfers between devices, with_halo(): after = lax.ppermute(first, axis, down)  38.9 us
    ppermute x8, starting transfers between devices, with_halo(): before = lax.ppermute(last, axis, up)  36.7 us
    ppermute x24, waiting for transfers between devices, from_partner(): return lax.ppermute(block, axis, route)  20.2 us
    all_to_all x2, starting transfers between devices, shards(): lax.all_to_all(request, 'lat', split_axis=2, concat_axis=2, tiled=True)  19.3 us
    all_to_all x2, waiting for transfers between devices, shards(): lax.all_to_all(request, 'lat', split_axis=2, concat_axis=2, tiled=True)  8.44 us
    unnamed x64, local copies, waits for them, and re-layouts  7.48 us
    ppermute x8, waiting for transfers between devices, with_halo(): after = lax.ppermute(first, axis, down)  6.61 us
  transfers between devices with their start and end apart: 42, of which 10 were waited for; matrix products, arithmetic and copies ran while one was open for 18% of the time, Pallas kernels for 0%

commit v1 on v0

v1 whole, which is shorter than its diff:
```python
import functools

import jax
import jax.numpy as jnp
from jax import lax
from jax.experimental import pallas as pl
from jax.experimental.pallas import tpu as pltpu
from jax.sharding import PartitionSpec as P

STEP_ORDER = (1, 0)
FIELDS = 4
ADVECT_HALF = 0.125
DIFFUSE = 0.1

ROWS = 8
LANES = 128

EDGE_STATE = (0, 256)
EDGE_MASKED = 512
EDGE_PART = 640
EDGE_LANES = 768


class Layout:
    def __init__(self, levels):
        self.tracer = (0, 3 * levels)
        self.merid = (2 * levels, 5 * levels)
        self.masked = 6 * levels
        self.part = 8 * levels
        self.corner = 10 * levels
        self.bottom = 11 * levels
        self.rows = (11 * levels + 1 + 15) // 16 * 16


def shift(block, amount, axis):
    return pltpu.roll(block, amount % block.shape[axis], axis)


def lanes_of(shape):
    return lax.broadcasted_iota(jnp.int32, shape, 1)


def rows_of(shape):
    return lax.broadcasted_iota(jnp.int32, shape, 0)


def strided(ref, start, count):
    return ref[pl.ds(start, count, stride=ROWS), :]


def request_kernel(slot_ref, store_ref, out_ref, wide_ref):
    tile = lax.axis_index("lon")
    bands, steps, pieces, lanes = out_ref.shape
    slots = store_ref.shape[0] // pieces
    wide_ref[...] = store_ref[...].astype(jnp.float32)
    for band in range(bands):
        for at, step in enumerate(STEP_ORDER):
            slot = slot_ref[step, band, tile]
            rows = wide_ref[pl.ds(slot, pieces, stride=slots), :]
            out_ref[band, at] = rows.astype(jnp.bfloat16)


def prepare_kernel(table_ref, adjoint_ref, bottom_ref, mix_ref, masked_ref, base_ref, kappa_ref):
    levels = adjoint_ref.shape[0] // (2 * ROWS)
    bottom = bottom_ref[...]
    edge = jnp.zeros((ROWS, LANES), jnp.float32)
    kappa_ref[0:ROWS] = edge
    kappa_ref[levels * ROWS : (levels + 1) * ROWS] = edge
    for level in range(levels - 1):
        classes = mix_ref[level * ROWS : (level + 1) * ROWS]
        kappa = jnp.full((ROWS, LANES), table_ref[0], jnp.float32)
        for index in range(1, table_ref.shape[0]):
            kappa = jnp.where(classes == index, table_ref[index], kappa)
        kappa_ref[(level + 1) * ROWS : (level + 2) * ROWS] = kappa
    for tracer in range(2):
        start = tracer * levels * ROWS
        for level in range(levels):
            here = slice(start + level * ROWS, start + (level + 1) * ROWS)
            masked_ref[here] = jnp.where(level < bottom, adjoint_ref[here], 0.0)
        for level in range(levels):
            base_ref[start + level * ROWS : start + (level + 1) * ROWS] = mixed(
                masked_ref, kappa_ref, start, level, levels
            )


def mixed(masked_ref, kappa_ref, start, level, levels):
    def at(index):
        return masked_ref[start + index * ROWS : start + (index + 1) * ROWS]

    masked = at(level)
    below = at(level + 1) if level + 1 < levels else jnp.zeros_like(masked)
    above = at(level - 1) if level > 0 else jnp.zeros_like(masked)
    kappa_above = kappa_ref[level * ROWS : (level + 1) * ROWS]
    kappa_below = kappa_ref[(level + 1) * ROWS : (level + 2) * ROWS]
    return masked + kappa_below * (below - masked) + kappa_above * (above - masked)


def edges_kernel(
    offset_ref,
    piece_ref,
    masked_ref,
    base_ref,
    bottom_ref,
    state_ref,
    to_west_ref,
    to_east_ref,
    top_ref,
    bot_ref,
    part_ref,
    column_ref,
):
    tile = lax.axis_index("lon")
    band = lax.axis_index("lat")
    levels = masked_ref.shape[0] // (2 * ROWS)
    pieces = FIELDS * levels
    holders = piece_ref.shape[0]
    lane = lanes_of((ROWS, LANES))
    sources = []
    for at, step in enumerate(STEP_ORDER):
        offset = offset_ref[step, band, tile]
        chunks = []
        for row in range(ROWS):
            chunk = piece_ref[lax.rem(row + offset, holders), at]
            state_ref[pl.ds(at * pieces * ROWS + row, pieces, stride=ROWS), :] = chunk.astype(
                jnp.float32
            )
            chunks.append(chunk)
        sources.append((EDGE_STATE[at], jnp.concatenate(chunks, axis=1)))
    for level in range(levels):
        zonal = state_ref[(2 * levels + level) * ROWS : (2 * levels + level + 1) * ROWS]
        east_factor = ADVECT_HALF * zonal + DIFFUSE
        west_factor = ADVECT_HALF * shift(zonal, 1, 1) - DIFFUSE
        for tracer in range(2):
            here = slice((tracer * levels + level) * ROWS, (tracer * levels + level + 1) * ROWS)
            masked = masked_ref[here]
            face = jnp.where(
                lane < LANES // 2,
                east_factor * (shift(masked, -1, 1) - masked),
                west_factor * (masked - shift(masked, 1, 1)),
            )
            part_ref[here] = base_ref[here] + face
    for start, ref in ((EDGE_MASKED, masked_ref), (EDGE_PART, part_ref)):
        columns = [strided(ref, row, 2 * levels).astype(jnp.bfloat16) for row in range(ROWS)]
        sources.append((start, jnp.concatenate(columns, axis=1)))
    place = (ROWS * LANES, LANES)
    from_row, from_lane = rows_of(place) // LANES, rows_of(place) % LANES
    chosen = ((from_lane == 0) & (lanes_of(place) == from_row)) | (
        (from_lane == LANES - 1) & (lanes_of(place) == from_row + ROWS)
    )
    pick = jnp.where(chosen, 1.0, 0.0).astype(jnp.bfloat16)
    column_ref[...] = jnp.zeros_like(column_ref)
    for start, source in sources:
        column_ref[start : start + source.shape[0]] = jnp.dot(
            source, pick, preferred_element_type=jnp.float32
        )
    edge = jnp.transpose(column_ref[...])
    bottom = bottom_ref[...].astype(jnp.float32)
    spot = lanes_of((ROWS, EDGE_LANES)) == EDGE_MASKED + 2 * levels
    to_west_ref[...] = jnp.where(spot, bottom[:, 0:1], edge[0:ROWS]).astype(jnp.bfloat16)
    to_east_ref[...] = jnp.where(spot, bottom[:, LANES - 1 :], edge[ROWS : 2 * ROWS]).astype(
        jnp.bfloat16
    )
    layout = Layout(levels)
    wide = lanes_of((levels, LANES))
    for row, inner, draft_ref in ((ROWS - 1, ROWS - 2, top_ref), (0, 1, bot_ref)):
        for at in range(2):
            begin = at * pieces * ROWS
            draft_ref[layout.tracer[at] : layout.tracer[at] + 2 * levels] = strided(
                state_ref, begin + row, 2 * levels
            )
            draft_ref[layout.merid[at] : layout.merid[at] + levels] = strided(
                state_ref, begin + 3 * levels * ROWS + row, levels
            )
        zonal = strided(state_ref, 2 * levels * ROWS + row, levels)
        merid = strided(state_ref, 3 * levels * ROWS + min(row, inner), levels)
        east_factor = ADVECT_HALF * zonal + DIFFUSE
        west_factor = ADVECT_HALF * shift(zonal, 1, 1) - DIFFUSE
        for tracer in range(2):
            begin = tracer * levels * ROWS
            masked = strided(masked_ref, begin + row, levels)
            next_row = strided(masked_ref, begin + inner, levels)
            if row > inner:
                along = (ADVECT_HALF * merid - DIFFUSE) * (masked - next_row)
            else:
                along = (ADVECT_HALF * merid + DIFFUSE) * (next_row - masked)
            east = east_factor * (shift(masked, -1, 1) - masked)
            west = west_factor * (masked - shift(masked, 1, 1))
            part = strided(base_ref, begin + row, levels) + along
            part = part + jnp.where(wide < LANES - 1, east, 0.0) + jnp.where(wide > 0, west, 0.0)
            at_masked = layout.masked + tracer * levels
            at_part = layout.part + tracer * levels
            draft_ref[at_masked : at_masked + levels] = masked
            draft_ref[at_part : at_part + levels] = part
        draft_ref[layout.corner : layout.corner + levels] = zonal
        draft_ref[layout.bottom : layout.rows] = jnp.broadcast_to(
            bottom[row : row + 1], (layout.rows - layout.bottom, LANES)
        )


def complete_kernel(
    levels,
    west_ref,
    east_ref,
    top_draft_ref,
    bot_draft_ref,
    first_ref,
    second_ref,
    edge_ref,
    column_ref,
    top_ref,
    bot_ref,
):
    layout = Layout(levels)
    low_half = lax.axis_index("lon") < lax.axis_size("lon") // 2
    top_ref[...] = top_draft_ref[...]
    bot_ref[...] = bot_draft_ref[...]
    edge_ref[...] = jnp.zeros_like(edge_ref)
    edge_ref[0:ROWS] = west_ref[...].astype(jnp.float32)
    edge_ref[ROWS : 2 * ROWS] = east_ref[...].astype(jnp.float32)
    column_ref[...] = jnp.transpose(edge_ref[...])
    lane = lanes_of((levels, LANES))

    def pair(start, row):
        block = column_ref[start : start + levels]
        return block[:, row : row + 1], block[:, ROWS + row : ROWS + row + 1]

    for row, draft_ref in ((ROWS - 1, top_ref), (0, bot_ref)):
        zonal = draft_ref[layout.corner : layout.corner + levels]
        zonal_west, _ = pair(EDGE_STATE[0] + 2 * levels, row)
        merid_west, merid_east = pair(EDGE_STATE[0] + 3 * levels, row)
        east_factor = ADVECT_HALF * zonal + DIFFUSE
        west_factor = ADVECT_HALF * zonal_west - DIFFUSE
        corner = jnp.where((lane == 32) | (lane == 96), merid_west, 0.0)
        corner = jnp.where((lane == 31) | (lane == 95), merid_east, corner)
        for tracer in range(2):
            west, east = pair(EDGE_MASKED + tracer * levels, row)
            at_masked = layout.masked + tracer * levels
            at_part = layout.part + tracer * levels
            masked = draft_ref[at_masked : at_masked + levels]
            face = jnp.where(lane == LANES - 1, east_factor * (east - masked), 0.0)
            face = jnp.where(lane == 0, west_factor * (masked - west), face)
            draft_ref[at_part : at_part + levels] = draft_ref[at_part : at_part + levels] + face
            corner = jnp.where(lane == (0, LANES // 2)[tracer], west, corner)
            corner = jnp.where(lane == (LANES - 1, LANES // 2 - 1)[tracer], east, corner)
        draft_ref[layout.corner : layout.corner + levels] = corner

    @pl.when(low_half)
    def _():
        first_ref[...] = top_ref[...].astype(jnp.bfloat16)
        second_ref[...] = bot_ref[...].astype(jnp.bfloat16)

    @pl.when(jnp.logical_not(low_half))
    def _():
        first_ref[...] = bot_ref[...].astype(jnp.bfloat16)
        second_ref[...] = top_ref[...].astype(jnp.bfloat16)


def steps_kernel(
    first_ref,
    second_ref,
    west_ref,
    east_ref,
    state_ref,
    masked_ref,
    base_ref,
    kappa_ref,
    bottom_ref,
    adjoint_ref,
    velocity_ref,
    north_ref,
    south_ref,
    corner_ref,
    next_ref,
    side_ref,
    ring_ref,
):
    levels = masked_ref.shape[0] // (2 * ROWS)
    layout = Layout(levels)
    band = lax.axis_index("lat")
    low_half = lax.axis_index("lon") < lax.axis_size("lon") // 2
    top_band = (band == lax.axis_size("lat") - 1).astype(jnp.int32)
    folded = top_band.astype(jnp.float32)
    square = (LANES, LANES)
    from_lane = rows_of(square)
    turned = from_lane + top_band * (LANES - 1 - 2 * from_lane)
    turn = jnp.where(lanes_of(square) == turned, 1.0, 0.0).astype(jnp.bfloat16)

    @pl.when(low_half)
    def _():
        north_ref[...] = jnp.dot(second_ref[...], turn, preferred_element_type=jnp.float32)
        south_ref[...] = first_ref[...].astype(jnp.float32)

    @pl.when(jnp.logical_not(low_half))
    def _():
        north_ref[...] = jnp.dot(first_ref[...], turn, preferred_element_type=jnp.float32)
        south_ref[...] = second_ref[...].astype(jnp.float32)

    for at in range(2):
        here = slice(layout.merid[at], layout.merid[at] + levels)
        north_ref[here] = north_ref[here] * folded
    for side, (ref, scale) in enumerate(((north_ref, folded), (south_ref, None))):
        packed = ref[layout.corner : layout.corner + levels]
        merid = shift(packed, 96, 1)
        merid = merid if scale is None else merid * scale
        for item, block in enumerate((packed, shift(packed, LANES // 2, 1), merid)):
            begin = (side * 3 + item) * levels
            corner_ref[begin : begin + levels] = block

    tile_shape = (ROWS, LANES)
    lane = lanes_of(tile_shape)
    row = rows_of(tile_shape)
    first_lane, last_lane = lane == 0, lane == LANES - 1
    bottom_row, top_row = row == 0, row == ROWS - 1
    closed = (band == 0).astype(jnp.int32)
    open_south = jnp.where(row >= closed, DIFFUSE, 0.0)
    bottom = bottom_ref[...]

    def spread(ref, index):
        return jnp.broadcast_to(ref[:, index : index + 1].astype(jnp.float32), tile_shape)

    def line(ref, index):
        return jnp.broadcast_to(ref[index : index + 1], tile_shape)

    def tile_of(ref, index):
        return ref[index * ROWS : (index + 1) * ROWS]

    side_bottom = jnp.where(
        first_lane,
        spread(west_ref, EDGE_MASKED + 2 * levels),
        spread(east_ref, EDGE_MASKED + 2 * levels),
    )

    def factors(at, level):
        begin = at * FIELDS * levels
        zonal = tile_of(state_ref, begin + 2 * levels + level)
        merid = tile_of(state_ref, begin + 3 * levels + level)
        zonal_west = jnp.where(
            first_lane,
            spread(west_ref, EDGE_STATE[at] + 2 * levels + level),
            shift(zonal, 1, 1),
        )
        merid_south = jnp.where(
            bottom_row, line(south_ref, layout.merid[at] + level), shift(merid, 1, 0)
        )
        merid_net = merid - jnp.where(top_row, line(north_ref, layout.merid[at] + level), 0.0)
        return (
            ADVECT_HALF * zonal,
            ADVECT_HALF * zonal_west,
            ADVECT_HALF * merid_net + DIFFUSE,
            ADVECT_HALF * merid_south - open_south,
        )

    def gradients(at, level, tracer, east, north):
        field = tile_of(state_ref, (at * FIELDS + tracer) * levels + level)
        field_east = jnp.where(
            last_lane,
            spread(east_ref, EDGE_STATE[at] + tracer * levels + level),
            shift(field, -1, 1),
        )
        field_north = jnp.where(
            top_row, line(north_ref, layout.tracer[at] + tracer * levels + level), shift(field, -1, 0)
        )
        return (field + field_east) * east, (field + field_north) * north

    level_of = rows_of((levels, LANES))
    for tracer in range(2):
        start = tracer * levels * ROWS
        at_masked = slice(layout.masked + tracer * levels, layout.masked + (tracer + 1) * levels)
        at_part = slice(layout.part + tracer * levels, layout.part + (tracer + 1) * levels)
        at_merid = slice(layout.merid[0], layout.merid[0] + levels)
        merid = strided(state_ref, 3 * levels * ROWS + ROWS - 1, levels)
        masked = strided(masked_ref, start + ROWS - 1, levels)
        face = (ADVECT_HALF * (north_ref[at_merid] - merid) + DIFFUSE) * (
            masked - north_ref[at_masked]
        )
        wet = level_of.astype(jnp.float32) < north_ref[layout.bottom : layout.bottom + 1]
        ring_ref[tracer * levels : (tracer + 1) * levels] = jnp.where(
            wet, north_ref[at_part] + face, 0.0
        )
        masked = strided(masked_ref, start, levels)
        face = (ADVECT_HALF * south_ref[at_merid] + DIFFUSE) * (masked - south_ref[at_masked])
        wet = level_of.astype(jnp.float32) < south_ref[layout.bottom : layout.bottom + 1]
        ring_ref[(2 + tracer) * levels : (3 + tracer) * levels] = jnp.where(
            wet, south_ref[at_part] + face, 0.0
        )

    for level in range(levels):
        zonal, zonal_west, north_factor, south_factor = factors(0, level)
        side_merid = jnp.where(
            first_lane,
            spread(west_ref, EDGE_STATE[0] + 3 * levels + level),
            spread(east_ref, EDGE_STATE[0] + 3 * levels + level),
        )
        side_north = side_merid - jnp.where(top_row, line(corner_ref, 2 * levels + level), 0.0)
        side_south = jnp.where(bottom_row, line(corner_ref, 5 * levels + level), shift(side_merid, 1, 0))
        side_north = ADVECT_HALF * side_north + DIFFUSE
        side_south = ADVECT_HALF * side_south - open_south
        zonal_total = jnp.zeros(tile_shape, jnp.float32)
        merid_total = jnp.zeros(tile_shape, jnp.float32)
        for tracer in range(2):
            index = tracer * levels + level
            masked = tile_of(masked_ref, index)
            west = spread(west_ref, EDGE_MASKED + index)
            east = spread(east_ref, EDGE_MASKED + index)
            side = jnp.where(first_lane, west, east)
            to_east = jnp.where(last_lane, east, shift(masked, -1, 1)) - masked
            to_west = masked - jnp.where(first_lane, west, shift(masked, 1, 1))
            to_north = (
                jnp.where(top_row, line(north_ref, layout.masked + index), shift(masked, -1, 0))
                - masked
            )
            to_south = masked - jnp.where(
                bottom_row, line(south_ref, layout.masked + index), shift(masked, 1, 0)
            )
            result = (
                tile_of(base_ref, index)
                + (zonal + DIFFUSE) * to_east
                + (zonal_west - DIFFUSE) * to_west
                + north_factor * to_north
                + south_factor * to_south
            )
            next_ref[index * ROWS : (index + 1) * ROWS] = jnp.where(level < bottom, result, 0.0)
            zonal_grad, merid_grad = gradients(0, level, tracer, to_east, to_north)
            zonal_total = zonal_total + zonal_grad
            merid_total = merid_total + merid_grad
            face = jnp.where(
                first_lane,
                (zonal_west + DIFFUSE) * (masked - side),
                (zonal - DIFFUSE) * (side - masked),
            )
            part = jnp.where(
                first_lane, spread(west_ref, EDGE_PART + index), spread(east_ref, EDGE_PART + index)
            )
            upper = jnp.where(top_row, line(corner_ref, index), shift(side, -1, 0)) - side
            lower = side - jnp.where(
                bottom_row, line(corner_ref, 3 * levels + index), shift(side, 1, 0)
            )
            result = part + face + side_north * upper + side_south * lower
            side_ref[index * ROWS : (index + 1) * ROWS] = jnp.where(
                side_bottom > level, result, 0.0
            )
        velocity_ref[level * ROWS : (level + 1) * ROWS] = ADVECT_HALF * zonal_total
        velocity_ref[(levels + level) * ROWS : (levels + level + 1) * ROWS] = (
            ADVECT_HALF * merid_total
        )

    for level in range(levels):
        zonal, zonal_west, north_factor, south_factor = factors(1, level)
        zonal_total = jnp.zeros(tile_shape, jnp.float32)
        merid_total = jnp.zeros(tile_shape, jnp.float32)
        for tracer in range(2):
            index = tracer * levels + level
            masked = tile_of(next_ref, index)
            side = tile_of(side_ref, index)
            to_east = jnp.where(last_lane, side, shift(masked, -1, 1)) - masked
            to_west = masked - jnp.where(first_lane, side, shift(masked, 1, 1))
            to_north = jnp.where(top_row, line(ring_ref, index), shift(masked, -1, 0)) - masked
            to_south = masked - jnp.where(
                bottom_row, line(ring_ref, 2 * levels + index), shift(masked, 1, 0)
            )
            adjoint_ref[index * ROWS : (index + 1) * ROWS] = (
                mixed(next_ref, kappa_ref, tracer * levels * ROWS, level, levels)
                + (zonal + DIFFUSE) * to_east
                + (zonal_west - DIFFUSE) * to_west
                + north_factor * to_north
                + south_factor * to_south
            )
            zonal_grad, merid_grad = gradients(1, level, tracer, to_east, to_north)
            zonal_total = zonal_total + zonal_grad
            merid_total = merid_total + merid_grad
        for total, begin in ((zonal_total, 0), (merid_total, levels)):
            here = slice((begin + level) * ROWS, (begin + level + 1) * ROWS)
            velocity_ref[here] = velocity_ref[here] + ADVECT_HALF * total


def line_routes(tiles, bands):
    def at(tile, band):
        return tile * bands + band

    upward = []
    for tile in range(tiles // 2):
        mirror = tiles - 1 - tile
        for band in range(bands - 1):
            upward.append((at(tile, band), at(tile, band + 1)))
            upward.append((at(mirror, band + 1), at(mirror, band)))
        upward.append((at(tile, bands - 1), at(mirror, bands - 1)))
    return upward, [(target, source) for source, target in upward]


def call(kernel, outputs, scratch, scalars, arrays):
    vmem = pl.BlockSpec(memory_space=pltpu.VMEM)
    smem = pl.BlockSpec(memory_space=pltpu.SMEM)
    return pl.pallas_call(
        kernel,
        out_shape=[jax.ShapeDtypeStruct(shape, dtype) for shape, dtype in outputs],
        in_specs=[smem] * len(scalars) + [vmem] * len(arrays),
        out_specs=[vmem] * len(outputs),
        scratch_shapes=[pltpu.VMEM(shape, jnp.float32) for shape in scratch],
        compiler_params=pltpu.CompilerParams(vmem_limit_bytes=32 * 1024 * 1024),
    )(*scalars, *arrays)


def shards(final_adjoint, store, holder_offset, holder_slot, bottom_level, mix_class, mix_table):
    bands = lax.axis_size("lat")
    tiles = lax.axis_size("lon")
    levels = final_adjoint.shape[1]
    slots = store.shape[2]
    steps = len(STEP_ORDER)
    pieces = FIELDS * levels
    full = levels * ROWS
    layout = Layout(levels)
    narrow, wide = jnp.bfloat16, jnp.float32
    (request,) = call(
        request_kernel,
        [((bands, steps, pieces, LANES), narrow)],
        [(pieces * slots, LANES)],
        [holder_slot],
        [store.reshape(pieces * slots, LANES)],
    )
    received = lax.all_to_all(request, "lat", split_axis=0, concat_axis=0, tiled=True)
    masked, base, kappa = call(
        prepare_kernel,
        [((2 * full, LANES), wide), ((2 * full, LANES), wide), ((full + ROWS, LANES), wide)],
        [],
        [mix_table],
        [
            final_adjoint.reshape(2 * full, LANES),
            bottom_level,
            mix_class.reshape((levels - 1) * ROWS, LANES),
        ],
    )
    state, to_west, to_east, top, bot = call(
        edges_kernel,
        [
            ((steps * FIELDS * full, LANES), wide),
            ((ROWS, EDGE_LANES), narrow),
            ((ROWS, EDGE_LANES), narrow),
            ((layout.rows, LANES), wide),
            ((layout.rows, LANES), wide),
        ],
        [(2 * full, LANES), (EDGE_LANES, LANES)],
        [holder_offset],
        [received, masked, base, bottom_level],
    )
    eastward = [(tile, (tile + 1) % tiles) for tile in range(tiles)]
    westward = [(target, source) for source, target in eastward]
    west = lax.ppermute(to_east, "lon", eastward)
    east = lax.ppermute(to_west, "lon", westward)
    first, second = call(
        functools.partial(complete_kernel, levels),
        [((layout.rows, LANES), narrow), ((layout.rows, LANES), narrow)],
        [(LANES, EDGE_LANES), (EDGE_LANES, LANES), (layout.rows, LANES), (layout.rows, LANES)],
        [],
        [west, east, top, bot],
    )
    upward, downward = line_routes(tiles, bands)
    first = lax.ppermute(first, ("lon", "lat"), upward)
    second = lax.ppermute(second, ("lon", "lat"), downward)
    adjoint, velocity = call(
        steps_kernel,
        [((2 * full, LANES), wide), ((2 * full, LANES), wide)],
        [
            (layout.rows, LANES),
            (layout.rows, LANES),
            (6 * levels, LANES),
            (2 * full, LANES),
            (2 * full, LANES),
            (4 * levels, LANES),
        ],
        [],
        [first, second, west, east, state, masked, base, kappa, bottom_level],
    )
    shape = (2, levels, ROWS, LANES)
    return adjoint.reshape(shape), velocity.reshape(shape)


def solution(mesh):
    return jax.shard_map(
        shards,
        mesh=mesh,
        in_specs=(
            P(None, None, "lat", "lon"),
            P(None, None, None, "lat", "lon"),
            P(),
            P(),
            P("lat", "lon"),
            P(None, "lat", "lon"),
            P(),
        ),
        out_specs=(P(None, None, "lat", "lon"), P(None, None, "lat", "lon")),
        check_vma=False,
    )
```

time: 264 us -> 69.8 us (0.26)
  the two profiles are of different devices: /device:TPU:6 before, /device:TPU:48 now
where the time goes in v1:
time: 69.8 us; the launch traced here: 69.4 us
  starting transfers between devices  32.8 us (47%)
  waiting for transfers between devices  26.9 us (39%)
  Pallas kernels  7.21 us (10%)
  local copies, waits for them, and re-layouts  1.78 us (3%)
  between operations  0.73 us (1%)
    all_to_all x1, waiting for transfers between devices, shards(): lax.all_to_all(request, 'lat', split_axis=0, concat_axis=0, tiled=True)  14.8 us
    ppermute x1, waiting for transfers between devices, shards(): second = lax.ppermute(second, ('lon', 'lat'), downward)  10.4 us
    ppermute x1, starting transfers between devices, shards(): east = lax.ppermute(to_west, 'lon', westward)  10.2 us
    all_to_all x1, starting transfers between devices, shards(): lax.all_to_all(request, 'lat', split_axis=0, concat_axis=0, tiled=True)  9.67 us
    ppermute x1, starting transfers between devices, shards(): first = lax.ppermute(first, ('lon', 'lat'), upward)  8.99 us
    pallas_call x5, Pallas kernels, call(): pl.pallas_call(kernel, out_shape=[jax.ShapeDtypeStruct(shape, dtype) for...  7.21 us
    ppermute x1, starting transfers between devices, shards(): west = lax.ppermute(to_east, 'lon', eastward)  1.94 us
    ppermute x1, starting transfers between devices, shards(): second = lax.ppermute(second, ('lon', 'lat'), downward)  1.92 us
  transfers between devices with their start and end apart: 5, of which 4 were waited for; matrix products, arithmetic and copies ran while one was open for 0% of the time, Pallas kernels for 1%

profile of v1, /device:TPU:48, one launch (start us, length us, event | category | flops | bytes accessed | tf_op | source)
XLA Modules:
  0.0 69.4 jit_solution(6972228655607856028)
XLA Ops:
  0.6 0.0 copy-start
  0.6 1.1 %copy-done = bf16[4,38,16,1,128]{4,2,3,1,0:T(8,128)(2,1)S(1)} copy-done((bf16[4,38,16,1,128]{4,2,3,1,0:T(8,128)(2,1)S(1)}, bf16[4,38,16,1,128]{4,2,3,1,0:T(8,128)(2,1)}, u32[]{:S(2)}) %copy-start) | copy-done | bytes 622616
  1.7 0.7 %copy-done.4 = s32[2,8,64]{2,1,0:T(8,128)S(1)} copy-done((s32[2,8,64]{2,1,0:T(8,128)S(1)}, s32[2,8,64]{2,1,0:T(8,128)}, u32[]{:S(2)}) %copy-start.4) | copy-done | bytes 4120
  2.4 0.0 copy-start.5
  2.4 2.2 %shard_map.86 = bf16[8,2,152,128]{3,2,1,0:T(8,128)(2,1)} custom-call(s32[2,8,64]{2,1,0:T(8,128)S(1)} %copy-done.4, bf16[2432,128]{1,0:T(8,128)(2,1)S(1)} %bitcast.5), custom_call_target="tpu_custom_call" | custom-call | tf_op jit(solution)/shard_map/pallas_call | solution.py:493
  4.7 9.7 %all-to-all-start = ((bf16[8,2,152,128]{3,2,1,0:T(8,128)(2,1)}), bf16[8,2,152,128]{3,2,1,0:T(8,128)(2,1)S(1)}, u32[]{:S(2)}, u32[]{:S(2)}) async-start(bf16[8,2,152,128]{3,2,1,0:T(8,128)(2,1)} %shard_map.86), calls=%async_computation | async-start | bytes 1245184 | tf_op jit(solution)/shard_map/all_to_all | solution.py:520
  14.3 0.0 copy-done.1
  14.3 0.0 copy-done.2
  14.3 0.0 copy-done.3
  14.3 0.0 copy-done.6
  14.4 0.7 %shard_map.87 = (f32[608,128]{1,0:T(8,128)S(1)}, f32[608,128]{1,0:T(8,128)S(1)}, f32[312,128]{1,0:T(8,128)S(1)}) custom-call(f32[8]{0:T(128)S(1)} %copy-done.6, f32[608,128]{1,0:T(8,128)S(1)} %bitcast.6, s32[8,128]{1,0:T(8,128)S(1)} %copy-done.3, s32[296,128]{1,0:T(8,128)S(1)} %bitcast.7), custom_call_target="tpu_custom_call" | custom-call | tf_op jit(solution)/shard_map/pallas_call | solution.py:493
  15.1 14.8 %all-to-all-done.piece_ref = bf16[8,2,152,128]{3,2,1,0:T(8,128)(2,1)S(1)} async-done(((bf16[8,2,152,128]{3,2,1,0:T(8,128)(2,1)}), bf16[8,2,152,128]{3,2,1,0:T(8,128)(2,1)S(1)}, u32[]{:S(2)}, u32[]{:S(2)}) %all-to-all-start) | async-done | bytes 622624 | tf_op jit(solution)/shard_map/all_to_all | solution.py:520
  29.9 0.0 copy-done.5
  29.9 1.4 %shard_map.88 = (f32[2432,128]{1,0:T(8,128)S(1)}, bf16[8,768]{1,0:T(8,128)(2,1)S(1)}, bf16[8,768]{1,0:T(8,128)(2,1)S(1)}, f32[432,128]{1,0:T(8,128)S(1)}, f32[432,128]{1,0:T(8,128)S(1)}) custom-call(s32[2,8,64]{2,1,0:T(8,128)S(1)} %copy-done.5, bf16[8,2,152,128]{3,2,1,0:T(8,128)(2,1)S(1)} %all-to-all-done.piece_ref, ...), custom_call_target="tpu_custom_call" | custom-call | tf_op jit(solution)/shard_map/pallas_call | solution.py:493
  31.3 1.9 %collective-permute-start = (bf16[8,768]{1,0:T(8,128)(2,1)S(1)}, bf16[8,768]{1,0:T(8,128)(2,1)S(1)}, u32[]{:S(2)}, u32[]{:S(2)}) collective-permute-start(bf16[8,768]{1,0:T(8,128)(2,1)S(1)} %get-tuple-element.16), channel_id=1, source_target_pairs={{0,8},{8,16},{16,24},{24,32},{32,40},{40,48},{48,56},{56,64},{64,7... | collective-permute-start | bytes 36872 | tf_op jit(solution)/shard_map/ppermute | solution.py:547
  33.3 10.2 %collective-permute-start.1 = (bf16[8,768]{1,0:T(8,128)(2,1)S(1)}, bf16[8,768]{1,0:T(8,128)(2,1)S(1)}, u32[]{:S(2)}, u32[]{:S(2)}) collective-permute-start(bf16[8,768]{1,0:T(8,128)(2,1)S(1)} %get-tuple-element.17), channel_id=1, source_target_pairs={{8,0},{16,8},{24,16},{32,24},{40,32},{48,40},{56,48},{64,56},{72,6... | collective-permute-start | bytes 36872 | tf_op jit(solution)/shard_map/ppermute | solution.py:548
  43.5 0.0 collective-permute-done.west_ref
  43.5 1.4 %collective-permute-done.1.east_ref = bf16[8,768]{1,0:T(8,128)(2,1)S(1)} collective-permute-done((bf16[8,768]{1,0:T(8,128)(2,1)S(1)}, bf16[8,768]{1,0:T(8,128)(2,1)S(1)}, u32[]{:S(2)}, u32[]{:S(2)}) %collective-permute-start.1) | collective-permute-done | bytes 12320 | tf_op jit(solution)/shard_map/ppermute | solution.py:548
  44.9 0.3 shard_map.89
  45.2 9.0 %collective-permute-start.2 = (bf16[432,128]{1,0:T(8,128)(2,1)S(1)}, bf16[432,128]{1,0:T(8,128)(2,1)S(1)}, u32[]{:S(2)}, u32[]{:S(2)}) collective-permute-start(bf16[432,128]{1,0:T(8,128)(2,1)S(1)} %get-tuple-element.20), channel_id=1, source_target_pairs={{0,1},{505,504},{1,2},{506,505},{2,3},{507,506},{3,4},{508,507},{4... | collective-permute-start | bytes 331784 | tf_op jit(solution)/shard_map/ppermute | solution.py:557
  54.2 1.9 %collective-permute-start.3 = (bf16[432,128]{1,0:T(8,128)(2,1)S(1)}, bf16[432,128]{1,0:T(8,128)(2,1)S(1)}, u32[]{:S(2)}, u32[]{:S(2)}) collective-permute-start(bf16[432,128]{1,0:T(8,128)(2,1)S(1)} %get-tuple-element.21), channel_id=1, source_target_pairs={{1,0},{504,505},{2,1},{505,506},{3,2},{506,507},{4,3},{507,508},{5... | collective-permute-start | bytes 331784 | tf_op jit(solution)/shard_map/ppermute | solution.py:558
  56.2 0.4 collective-permute-done.2.first_ref
  56.5 10.4 %collective-permute-done.3.second_ref = bf16[432,128]{1,0:T(8,128)(2,1)S(1)} collective-permute-done((bf16[432,128]{1,0:T(8,128)(2,1)S(1)}, bf16[432,128]{1,0:T(8,128)(2,1)S(1)}, u32[]{:S(2)}, u32[]{:S(2)}) %collective-permute-start.3) | collective-permute-done | bytes 110624 | tf_op jit(solution)/shard_map/ppermute | solution.py:558
  66.9 2.5 %shard_map.90 = (f32[608,128]{1,0:T(8,128)}, f32[608,128]{1,0:T(8,128)}) custom-call(bf16[432,128]{1,0:T(8,128)(2,1)S(1)} %collective-permute-done.2.first_ref, bf16[432,128]{1,0:T(8,128)(2,1)S(1)} %collective-permute-done.3.second_ref, bf16[8,768]{1,0:T(8,128)(2,1)S(1)} %collective-permute-done.west_ref, ...), custom_call_target="tpu_custom_call" | custom-call | tf_op jit(solution)/shard_map/pallas_call | solution.py:493
  (5 shorter events, 0.0 us)
Async XLA Ops:
  0.6 1.1 %copy-start = (bf16[4,38,16,1,128]{4,2,3,1,0:T(8,128)(2,1)S(1)}, bf16[4,38,16,1,128]{4,2,3,1,0:T(8,128)(2,1)}, u32[]{:S(2)}) copy-start(bf16[4,38,16,1,128]{4,2,3,1,0:T(8,128)(2,1)} %param.8) | copy-start | bytes 1867780
  1.7 0.7 %copy-start.4 = (s32[2,8,64]{2,1,0:T(8,128)S(1)}, s32[2,8,64]{2,1,0:T(8,128)}, u32[]{:S(2)}) copy-start(s32[2,8,64]{2,1,0:T(8,128)} %slot_ref.1) | copy-start | bytes 12292
  2.4 11.9 %copy-start.1 = (f32[2,38,8,128]{3,2,1,0:T(8,128)S(1)}, f32[2,38,8,128]{3,2,1,0:T(8,128)}, u32[]{:S(2)}) copy-start(f32[2,38,8,128]{3,2,1,0:T(8,128)} %param.7) | copy-start | bytes 933892
  2.4 11.9 %copy-start.2 = (s32[37,8,128]{2,1,0:T(8,128)S(1)}, s32[37,8,128]{2,1,0:T(8,128)}, u32[]{:S(2)}) copy-start(s32[37,8,128]{2,1,0:T(8,128)} %param.12) | copy-start | bytes 454660
  2.4 11.9 %copy-start.3 = (s32[8,128]{1,0:T(8,128)S(1)}, s32[8,128]{1,0:T(8,128)}, u32[]{:S(2)}) copy-start(s32[8,128]{1,0:T(8,128)} %bottom_ref.5) | copy-start | bytes 12292
  2.4 11.9 %copy-start.6 = (f32[8]{0:T(128)S(1)}, f32[8]{0:T(128)}, u32[]{:S(2)}) copy-start(f32[8]{0:T(128)} %table_ref.1) | copy-start | bytes 100
  2.4 27.5 %copy-start.5 = (s32[2,8,64]{2,1,0:T(8,128)S(1)}, s32[2,8,64]{2,1,0:T(8,128)}, u32[]{:S(2)}) copy-start(s32[2,8,64]{2,1,0:T(8,128)} %offset_ref.1) | copy-start | bytes 12292
  4.7 25.2 %all-to-all-start = ((bf16[8,2,152,128]{3,2,1,0:T(8,128)(2,1)}), bf16[8,2,152,128]{3,2,1,0:T(8,128)(2,1)S(1)}, u32[]{:S(2)}, u32[]{:S(2)}) async-start(bf16[8,2,152,128]{3,2,1,0:T(8,128)(2,1)} %shard_map.86), calls=%async_computation | async-start | bytes 1245184 | tf_op jit(solution)/shard_map/all_to_all | solution.py:520
  31.3 12.2 %collective-permute-start = (bf16[8,768]{1,0:T(8,128)(2,1)S(1)}, bf16[8,768]{1,0:T(8,128)(2,1)S(1)}, u32[]{:S(2)}, u32[]{:S(2)}) collective-permute-start(bf16[8,768]{1,0:T(8,128)(2,1)S(1)} %get-tuple-element.16), channel_id=1, source_target_pairs={{0,8},{8,16},{16,24},{24,32},{32,40},{40,48},{48,56},{56,64},{64,7... | collective-permute-start | bytes 36872 | tf_op jit(solution)/shard_map/ppermute | solution.py:547
  33.3 11.6 %collective-permute-start.1 = (bf16[8,768]{1,0:T(8,128)(2,1)S(1)}, bf16[8,768]{1,0:T(8,128)(2,1)S(1)}, u32[]{:S(2)}, u32[]{:S(2)}) collective-permute-start(bf16[8,768]{1,0:T(8,128)(2,1)S(1)} %get-tuple-element.17), channel_id=1, source_target_pairs={{8,0},{16,8},{24,16},{32,24},{40,32},{48,40},{56,48},{64,56},{72,6... | collective-permute-start | bytes 36872 | tf_op jit(solution)/shard_map/ppermute | solution.py:548
  45.2 11.3 %collective-permute-start.2 = (bf16[432,128]{1,0:T(8,128)(2,1)S(1)}, bf16[432,128]{1,0:T(8,128)(2,1)S(1)}, u32[]{:S(2)}, u32[]{:S(2)}) collective-permute-start(bf16[432,128]{1,0:T(8,128)(2,1)S(1)} %get-tuple-element.20), channel_id=1, source_target_pairs={{0,1},{505,504},{1,2},{506,505},{2,3},{507,506},{3,4},{508,507},{4... | collective-permute-start | bytes 331784 | tf_op jit(solution)/shard_map/ppermute | solution.py:557
  54.2 12.7 %collective-permute-start.3 = (bf16[432,128]{1,0:T(8,128)(2,1)S(1)}, bf16[432,128]{1,0:T(8,128)(2,1)S(1)}, u32[]{:S(2)}, u32[]{:S(2)}) collective-permute-start(bf16[432,128]{1,0:T(8,128)(2,1)S(1)} %get-tuple-element.21), channel_id=1, source_target_pairs={{1,0},{504,505},{2,1},{505,506},{3,2},{506,507},{4,3},{507,508},{5... | collective-permute-start | bytes 331784 | tf_op jit(solution)/shard_map/ppermute | solution.py:558

commit v2 on v1

--- a/solution.py
+++ b/solution.py
@@ -102,8 +102,8 @@
     base_ref,
     bottom_ref,
     state_ref,
-    to_west_ref,
-    to_east_ref,
+    inner_ref,
+    outer_ref,
     top_ref,
     bot_ref,
     part_ref,
@@ -156,10 +156,19 @@
     edge = jnp.transpose(column_ref[...])
     bottom = bottom_ref[...].astype(jnp.float32)
     spot = lanes_of((ROWS, EDGE_LANES)) == EDGE_MASKED + 2 * levels
-    to_west_ref[...] = jnp.where(spot, bottom[:, 0:1], edge[0:ROWS]).astype(jnp.bfloat16)
-    to_east_ref[...] = jnp.where(spot, bottom[:, LANES - 1 :], edge[ROWS : 2 * ROWS]).astype(
-        jnp.bfloat16
-    )
+    to_west = jnp.where(spot, bottom[:, 0:1], edge[0:ROWS]).astype(jnp.bfloat16)
+    to_east = jnp.where(spot, bottom[:, LANES - 1 :], edge[ROWS : 2 * ROWS]).astype(jnp.bfloat16)
+
+    @pl.when(lax.rem(tile, 2) == 0)
+    def _():
+        inner_ref[...] = to_east
+        outer_ref[...] = to_west
+
+    @pl.when(lax.rem(tile, 2) == 1)
+    def _():
+        inner_ref[...] = to_west
+        outer_ref[...] = to_east
+
     layout = Layout(levels)
     wide = lanes_of((levels, LANES))
     for row, inner, draft_ref in ((ROWS - 1, ROWS - 2, top_ref), (0, 1, bot_ref)):
@@ -199,19 +208,33 @@
 
 def complete_kernel(
     levels,
+    inner_ref,
+    outer_ref,
+    top_draft_ref,
+    bot_draft_ref,
+    near_ref,
+    far_ref,
     west_ref,
     east_ref,
-    top_draft_ref,
-    bot_draft_ref,
-    first_ref,
-    second_ref,
     edge_ref,
     column_ref,
     top_ref,
     bot_ref,
 ):
     layout = Layout(levels)
-    low_half = lax.axis_index("lon") < lax.axis_size("lon") // 2
+    odd_tile = lax.rem(lax.axis_index("lon"), 2) == 1
+    odd_band = lax.rem(lax.axis_index("lat"), 2) == 1
+
+    @pl.when(odd_tile)
+    def _():
+        west_ref[...] = inner_ref[...]
+        east_ref[...] = outer_ref[...]
+
+    @pl.when(jnp.logical_not(odd_tile))
+    def _():
+        west_ref[...] = outer_ref[...]
+        east_ref[...] = inner_ref[...]
+
     top_ref[...] = top_draft_ref[...]
     bot_ref[...] = bot_draft_ref[...]
     edge_ref[...] = jnp.zeros_like(edge_ref)
@@ -244,20 +267,20 @@
             corner = jnp.where(lane == (LANES - 1, LANES // 2 - 1)[tracer], east, corner)
         draft_ref[layout.corner : layout.corner + levels] = corner
 
-    @pl.when(low_half)
-    def _():
-        first_ref[...] = top_ref[...].astype(jnp.bfloat16)
-        second_ref[...] = bot_ref[...].astype(jnp.bfloat16)
-
-    @pl.when(jnp.logical_not(low_half))
-    def _():
-        first_ref[...] = bot_ref[...].astype(jnp.bfloat16)
-        second_ref[...] = top_ref[...].astype(jnp.bfloat16)
+    @pl.when(odd_band)
+    def _():
+        near_ref[...] = bot_ref[...].astype(jnp.bfloat16)
+        far_ref[...] = top_ref[...].astype(jnp.bfloat16)
+
+    @pl.when(jnp.logical_not(odd_band))
+    def _():
+        near_ref[...] = top_ref[...].astype(jnp.bfloat16)
+        far_ref[...] = bot_ref[...].astype(jnp.bfloat16)
 
 
 def steps_kernel(
-    first_ref,
-    second_ref,
+    near_ref,
+    far_ref,
     west_ref,
     east_ref,
     state_ref,
@@ -277,7 +300,7 @@
     levels = masked_ref.shape[0] // (2 * ROWS)
     layout = Layout(levels)
     band = lax.axis_index("lat")
-    low_half = lax.axis_index("lon") < lax.axis_size("lon") // 2
+    odd_band = lax.rem(band, 2) == 1
     top_band = (band == lax.axis_size("lat") - 1).astype(jnp.int32)
     folded = top_band.astype(jnp.float32)
     square = (LANES, LANES)
@@ -285,15 +308,15 @@
     turned = from_lane + top_band * (LANES - 1 - 2 * from_lane)
     turn = jnp.where(lanes_of(square) == turned, 1.0, 0.0).astype(jnp.bfloat16)
 
-    @pl.when(low_half)
-    def _():
-        north_ref[...] = jnp.dot(second_ref[...], turn, preferred_element_type=jnp.float32)
-        south_ref[...] = first_ref[...].astype(jnp.float32)
-
-    @pl.when(jnp.logical_not(low_half))
-    def _():
-        north_ref[...] = jnp.dot(first_ref[...], turn, preferred_element_type=jnp.float32)
-        south_ref[...] = second_ref[...].astype(jnp.float32)
+    @pl.when(odd_band)
+    def _():
+        north_ref[...] = jnp.dot(far_ref[...], turn, preferred_element_type=jnp.float32)
+        south_ref[...] = near_ref[...].astype(jnp.float32)
+
+    @pl.when(jnp.logical_not(odd_band))
+    def _():
+        north_ref[...] = jnp.dot(near_ref[...], turn, preferred_element_type=jnp.float32)
+        south_ref[...] = far_ref[...].astype(jnp.float32)
 
     for at in range(2):
         here = slice(layout.merid[at], layout.merid[at] + levels)
@@ -473,18 +496,25 @@
             velocity_ref[here] = velocity_ref[here] + ADVECT_HALF * total
 
 
+def swaps(pairs):
+    return [pair for low, high in pairs for pair in ((low, high), (high, low))]
+
+
+def ring_routes(tiles):
+    inner = swaps((tile, tile + 1) for tile in range(0, tiles, 2))
+    outer = swaps((tile, (tile + 1) % tiles) for tile in range(1, tiles, 2))
+    return inner, outer
+
+
 def line_routes(tiles, bands):
-    def at(tile, band):
-        return tile * bands + band
-
-    upward = []
-    for tile in range(tiles // 2):
-        mirror = tiles - 1 - tile
-        for band in range(bands - 1):
-            upward.append((at(tile, band), at(tile, band + 1)))
-            upward.append((at(mirror, band + 1), at(mirror, band)))
-        upward.append((at(tile, bands - 1), at(mirror, bands - 1)))
-    return upward, [(target, source) for source, target in upward]
+    near, far = [], []
+    for tile in range(tiles):
+        start = tile * bands
+        near += [(start + band, start + band + 1) for band in range(0, bands, 2)]
+        far += [(start + band, start + band + 1) for band in range(1, bands - 1, 2)]
+        if tile < tiles // 2:
+            far.append((start + bands - 1, (tiles - tile) * bands - 1))
+    return swaps(near), swaps(far)
 
 
 def call(kernel, outputs, scratch, scalars, arrays):
@@ -529,7 +559,7 @@
             mix_class.reshape((levels - 1) * ROWS, LANES),
         ],
     )
-    state, to_west, to_east, top, bot = call(
+    state, inner, outer, top, bot = call(
         edges_kernel,
         [
             ((steps * FIELDS * full, LANES), wide),
@@ -542,20 +572,24 @@
         [holder_offset],
         [received, masked, base, bottom_level],
     )
-    eastward = [(tile, (tile + 1) % tiles) for tile in range(tiles)]
-    westward = [(target, source) for source, target in eastward]
-    west = lax.ppermute(to_east, "lon", eastward)
-    east = lax.ppermute(to_west, "lon", westward)
-    first, second = call(
+    inner_routes, outer_routes = ring_routes(tiles)
+    near_routes, far_routes = line_routes(tiles, bands)
+    inner = lax.ppermute(inner, "lon", inner_routes)
+    outer = lax.ppermute(outer, "lon", outer_routes)
+    near, far, west, east = call(
         functools.partial(complete_kernel, levels),
-        [((layout.rows, LANES), narrow), ((layout.rows, LANES), narrow)],
+        [
+            ((layout.rows, LANES), narrow),
+            ((layout.rows, LANES), narrow),
+            ((ROWS, EDGE_LANES), narrow),
+            ((ROWS, EDGE_LANES), narrow),
+        ],
         [(LANES, EDGE_LANES), (EDGE_LANES, LANES), (layout.rows, LANES), (layout.rows, LANES)],
         [],
-        [west, east, top, bot],
-    )
-    upward, downward = line_routes(tiles, bands)
-    first = lax.ppermute(first, ("lon", "lat"), upward)
-    second = lax.ppermute(second, ("lon", "lat"), downward)
+        [inner, outer, top, bot],
+    )
+    near = lax.ppermute(near, ("lon", "lat"), near_routes)
+    far = lax.ppermute(far, ("lon", "lat"), far_routes)
     adjoint, velocity = call(
         steps_kernel,
         [((2 * full, LANES), wide), ((2 * full, LANES), wide)],
@@ -568,7 +602,7 @@
             (4 * levels, LANES),
         ],
         [],
-        [first, second, west, east, state, masked, base, kappa, bottom_level],
+        [near, far, west, east, state, masked, base, kappa, bottom_level],
     )
     shape = (2, levels, ROWS, LANES)
     return adjoint.reshape(shape), velocity.reshape(shape)

time: 69.8 us -> 67.3 us (0.964)
  the two profiles are of different devices: /device:TPU:48 before, /device:TPU:22 now
where the time goes in v2:
time: 67.3 us; the launch traced here: 66.9 us
  waiting for transfers between devices  29.3 us (44%)
  starting transfers between devices  27.8 us (41%)
  Pallas kernels  7.28 us (11%)
  local copies, waits for them, and re-layouts  1.78 us (3%)
  between operations  0.74 us (1%)
    all_to_all x1, waiting for transfers between devices, shards(): lax.all_to_all(request, 'lat', split_axis=0, concat_axis=0, tiled=True)  18.3 us
    ppermute x1, starting transfers between devices, shards(): outer = lax.ppermute(outer, 'lon', outer_routes)  12 us
    ppermute x1, waiting for transfers between devices, shards(): far = lax.ppermute(far, ('lon', 'lat'), far_routes)  8.66 us
    all_to_all x1, starting transfers between devices, shards(): lax.all_to_all(request, 'lat', split_axis=0, concat_axis=0, tiled=True)  8.24 us
    pallas_call x5, Pallas kernels, call(): pl.pallas_call(kernel, out_shape=[jax.ShapeDtypeStruct(shape, dtype) for...  7.28 us
    ppermute x1, starting transfers between devices, shards(): far = lax.ppermute(far, ('lon', 'lat'), far_routes)  3.07 us
    ppermute x1, starting transfers between devices, shards(): near = lax.ppermute(near, ('lon', 'lat'), near_routes)  2.64 us
    ppermute x1, starting transfers between devices, shards(): inner = lax.ppermute(inner, 'lon', inner_routes)  1.92 us
  transfers between devices with their start and end apart: 5, of which 4 were waited for; matrix products, arithmetic and copies ran while one was open for 0% of the time, Pallas kernels for 1%

profile of v2, /device:TPU:22, one launch (start us, length us, event | category | flops | bytes accessed | tf_op | source)
XLA Modules:
  0.0 66.9 jit_solution(7109855360336703999)
XLA Ops:
  0.6 0.0 copy-start
  0.6 1.1 %copy-done = bf16[4,38,16,1,128]{4,2,3,1,0:T(8,128)(2,1)S(1)} copy-done((bf16[4,38,16,1,128]{4,2,3,1,0:T(8,128)(2,1)S(1)}, bf16[4,38,16,1,128]{4,2,3,1,0:T(8,128)(2,1)}, u32[]{:S(2)}) %copy-start) | copy-done | bytes 622616
  1.7 0.7 %copy-done.4 = s32[2,8,64]{2,1,0:T(8,128)S(1)} copy-done((s32[2,8,64]{2,1,0:T(8,128)S(1)}, s32[2,8,64]{2,1,0:T(8,128)}, u32[]{:S(2)}) %copy-start.4) | copy-done | bytes 4120
  2.4 0.0 copy-start.5
  2.4 2.2 %shard_map.86 = bf16[8,2,152,128]{3,2,1,0:T(8,128)(2,1)} custom-call(s32[2,8,64]{2,1,0:T(8,128)S(1)} %copy-done.4, bf16[2432,128]{1,0:T(8,128)(2,1)S(1)} %bitcast.5), custom_call_target="tpu_custom_call" | custom-call | tf_op jit(solution)/shard_map/pallas_call | solution.py:523
  4.7 8.2 %all-to-all-start = ((bf16[8,2,152,128]{3,2,1,0:T(8,128)(2,1)}), bf16[8,2,152,128]{3,2,1,0:T(8,128)(2,1)S(1)}, u32[]{:S(2)}, u32[]{:S(2)}) async-start(bf16[8,2,152,128]{3,2,1,0:T(8,128)(2,1)} %shard_map.86), calls=%async_computation | async-start | bytes 1245184 | tf_op jit(solution)/shard_map/all_to_all | solution.py:550
  12.9 0.0 copy-done.1
  12.9 0.0 copy-done.2
  12.9 0.0 copy-done.3
  12.9 0.0 copy-done.6
  12.9 0.7 %shard_map.87 = (f32[608,128]{1,0:T(8,128)S(1)}, f32[608,128]{1,0:T(8,128)S(1)}, f32[312,128]{1,0:T(8,128)S(1)}) custom-call(f32[8]{0:T(128)S(1)} %copy-done.6, f32[608,128]{1,0:T(8,128)S(1)} %bitcast.6, s32[8,128]{1,0:T(8,128)S(1)} %copy-done.3, s32[296,128]{1,0:T(8,128)S(1)} %bitcast.7), custom_call_target="tpu_custom_call" | custom-call | tf_op jit(solution)/shard_map/pallas_call | solution.py:523
  13.6 18.3 %all-to-all-done.piece_ref = bf16[8,2,152,128]{3,2,1,0:T(8,128)(2,1)S(1)} async-done(((bf16[8,2,152,128]{3,2,1,0:T(8,128)(2,1)}), bf16[8,2,152,128]{3,2,1,0:T(8,128)(2,1)S(1)}, u32[]{:S(2)}, u32[]{:S(2)}) %all-to-all-start) | async-done | bytes 622624 | tf_op jit(solution)/shard_map/all_to_all | solution.py:550
  31.9 0.0 copy-done.5
  31.9 1.5 %shard_map.88 = (f32[2432,128]{1,0:T(8,128)S(1)}, bf16[8,768]{1,0:T(8,128)(2,1)S(1)}, bf16[8,768]{1,0:T(8,128)(2,1)S(1)}, f32[432,128]{1,0:T(8,128)S(1)}, f32[432,128]{1,0:T(8,128)S(1)}) custom-call(s32[2,8,64]{2,1,0:T(8,128)S(1)} %copy-done.5, bf16[8,2,152,128]{3,2,1,0:T(8,128)(2,1)S(1)} %all-to-all-done.piece_ref, ...), custom_call_target="tpu_custom_call" | custom-call | tf_op jit(solution)/shard_map/pallas_call | solution.py:523
  33.5 1.9 %collective-permute-start = (bf16[8,768]{1,0:T(8,128)(2,1)S(1)}, bf16[8,768]{1,0:T(8,128)(2,1)S(1)}, u32[]{:S(2)}, u32[]{:S(2)}) collective-permute-start(bf16[8,768]{1,0:T(8,128)(2,1)S(1)} %get-tuple-element.18), channel_id=1, source_target_pairs={{0,8},{8,0},{16,24},{24,16},{32,40},{40,32},{48,56},{56,48},{64,72... | collective-permute-start | bytes 36872 | tf_op jit(solution)/shard_map/ppermute | solution.py:577
  35.4 12.0 %collective-permute-start.1 = (bf16[8,768]{1,0:T(8,128)(2,1)S(1)}, bf16[8,768]{1,0:T(8,128)(2,1)S(1)}, u32[]{:S(2)}, u32[]{:S(2)}) collective-permute-start(bf16[8,768]{1,0:T(8,128)(2,1)S(1)} %get-tuple-element.19), channel_id=1, source_target_pairs={{8,16},{16,8},{24,32},{32,24},{40,48},{48,40},{56,64},{64,56},{72,... | collective-permute-start | bytes 36872 | tf_op jit(solution)/shard_map/ppermute | solution.py:578
  47.3 0.0 collective-permute-done.inner_ref
  47.4 1.4 %collective-permute-done.1.outer_ref = bf16[8,768]{1,0:T(8,128)(2,1)S(1)} collective-permute-done((bf16[8,768]{1,0:T(8,128)(2,1)S(1)}, bf16[8,768]{1,0:T(8,128)(2,1)S(1)}, u32[]{:S(2)}, u32[]{:S(2)}) %collective-permute-start.1) | collective-permute-done | bytes 12320 | tf_op jit(solution)/shard_map/ppermute | solution.py:578
  48.7 0.3 shard_map.89
  49.1 2.6 %collective-permute-start.2 = (bf16[432,128]{1,0:T(8,128)(2,1)S(1)}, bf16[432,128]{1,0:T(8,128)(2,1)S(1)}, u32[]{:S(2)}, u32[]{:S(2)}) collective-permute-start(bf16[432,128]{1,0:T(8,128)(2,1)S(1)} %get-tuple-element.22), channel_id=1, source_target_pairs={{0,1},{1,0},{2,3},{3,2},{4,5},{5,4},{6,7},{7,6},{8,9},{9,8},{10,11... | collective-permute-start | bytes 331784 | tf_op jit(solution)/shard_map/ppermute | solution.py:591
  51.7 3.1 %collective-permute-start.3 = (bf16[432,128]{1,0:T(8,128)(2,1)S(1)}, bf16[432,128]{1,0:T(8,128)(2,1)S(1)}, u32[]{:S(2)}, u32[]{:S(2)}) collective-permute-start(bf16[432,128]{1,0:T(8,128)(2,1)S(1)} %get-tuple-element.23), channel_id=1, source_target_pairs={{1,2},{2,1},{3,4},{4,3},{5,6},{6,5},{7,511},{511,7},{9,10},{10,9},... | collective-permute-start | bytes 331784 | tf_op jit(solution)/shard_map/ppermute | solution.py:592
  54.8 0.9 %collective-permute-done.2.near_ref = bf16[432,128]{1,0:T(8,128)(2,1)S(1)} collective-permute-done((bf16[432,128]{1,0:T(8,128)(2,1)S(1)}, bf16[432,128]{1,0:T(8,128)(2,1)S(1)}, u32[]{:S(2)}, u32[]{:S(2)}) %collective-permute-start.2) | collective-permute-done | bytes 110624 | tf_op jit(solution)/shard_map/ppermute | solution.py:591
  55.7 8.7 %collective-permute-done.3.far_ref = bf16[432,128]{1,0:T(8,128)(2,1)S(1)} collective-permute-done((bf16[432,128]{1,0:T(8,128)(2,1)S(1)}, bf16[432,128]{1,0:T(8,128)(2,1)S(1)}, u32[]{:S(2)}, u32[]{:S(2)}) %collective-permute-start.3) | collective-permute-done | bytes 110624 | tf_op jit(solution)/shard_map/ppermute | solution.py:592
  64.4 2.5 %shard_map.90 = (f32[608,128]{1,0:T(8,128)}, f32[608,128]{1,0:T(8,128)}) custom-call(bf16[432,128]{1,0:T(8,128)(2,1)S(1)} %collective-permute-done.2.near_ref, bf16[432,128]{1,0:T(8,128)(2,1)S(1)} %collective-permute-done.3.far_ref, bf16[8,768]{1,0:T(8,128)(2,1)S(1)} %get-tuple-element.24.west_ref, bf16[8,768]{1,0:T(8,128)(2,1)S(1)} %get-tuple-element.25.east_ref, ...), custom_call_target="tpu_custom_call" | custom-call | tf_op jit(solution)/shard_map/pallas_call | solution.py:523
  (5 shorter events, 0.0 us)
Async XLA Ops:
  0.6 1.1 %copy-start = (bf16[4,38,16,1,128]{4,2,3,1,0:T(8,128)(2,1)S(1)}, bf16[4,38,16,1,128]{4,2,3,1,0:T(8,128)(2,1)}, u32[]{:S(2)}) copy-start(bf16[4,38,16,1,128]{4,2,3,1,0:T(8,128)(2,1)} %param.8) | copy-start | bytes 1867780
  1.7 0.7 %copy-start.4 = (s32[2,8,64]{2,1,0:T(8,128)S(1)}, s32[2,8,64]{2,1,0:T(8,128)}, u32[]{:S(2)}) copy-start(s32[2,8,64]{2,1,0:T(8,128)} %slot_ref.1) | copy-start | bytes 12292
  2.4 10.5 %copy-start.1 = (f32[2,38,8,128]{3,2,1,0:T(8,128)S(1)}, f32[2,38,8,128]{3,2,1,0:T(8,128)}, u32[]{:S(2)}) copy-start(f32[2,38,8,128]{3,2,1,0:T(8,128)} %param.7) | copy-start | bytes 933892
  2.4 10.5 %copy-start.2 = (s32[37,8,128]{2,1,0:T(8,128)S(1)}, s32[37,8,128]{2,1,0:T(8,128)}, u32[]{:S(2)}) copy-start(s32[37,8,128]{2,1,0:T(8,128)} %param.12) | copy-start | bytes 454660
  2.4 10.5 %copy-start.3 = (s32[8,128]{1,0:T(8,128)S(1)}, s32[8,128]{1,0:T(8,128)}, u32[]{:S(2)}) copy-start(s32[8,128]{1,0:T(8,128)} %bottom_ref.5) | copy-start | bytes 12292
  2.4 10.5 %copy-start.6 = (f32[8]{0:T(128)S(1)}, f32[8]{0:T(128)}, u32[]{:S(2)}) copy-start(f32[8]{0:T(128)} %table_ref.1) | copy-start | bytes 100
  2.4 29.5 %copy-start.5 = (s32[2,8,64]{2,1,0:T(8,128)S(1)}, s32[2,8,64]{2,1,0:T(8,128)}, u32[]{:S(2)}) copy-start(s32[2,8,64]{2,1,0:T(8,128)} %offset_ref.1) | copy-start | bytes 12292
  4.7 27.3 %all-to-all-start = ((bf16[8,2,152,128]{3,2,1,0:T(8,128)(2,1)}), bf16[8,2,152,128]{3,2,1,0:T(8,128)(2,1)S(1)}, u32[]{:S(2)}, u32[]{:S(2)}) async-start(bf16[8,2,152,128]{3,2,1,0:T(8,128)(2,1)} %shard_map.86), calls=%async_computation | async-start | bytes 1245184 | tf_op jit(solution)/shard_map/all_to_all | solution.py:550
  33.5 13.9 %collective-permute-start = (bf16[8,768]{1,0:T(8,128)(2,1)S(1)}, bf16[8,768]{1,0:T(8,128)(2,1)S(1)}, u32[]{:S(2)}, u32[]{:S(2)}) collective-permute-start(bf16[8,768]{1,0:T(8,128)(2,1)S(1)} %get-tuple-element.18), channel_id=1, source_target_pairs={{0,8},{8,0},{16,24},{24,16},{32,40},{40,32},{48,56},{56,48},{64,72... | collective-permute-start | bytes 36872 | tf_op jit(solution)/shard_map/ppermute | solution.py:577
  35.4 13.4 %collective-permute-start.1 = (bf16[8,768]{1,0:T(8,128)(2,1)S(1)}, bf16[8,768]{1,0:T(8,128)(2,1)S(1)}, u32[]{:S(2)}, u32[]{:S(2)}) collective-permute-start(bf16[8,768]{1,0:T(8,128)(2,1)S(1)} %get-tuple-element.19), channel_id=1, source_target_pairs={{8,16},{16,8},{24,32},{32,24},{40,48},{48,40},{56,64},{64,56},{72,... | collective-permute-start | bytes 36872 | tf_op jit(solution)/shard_map/ppermute | solution.py:578
  49.1 6.6 %collective-permute-start.2 = (bf16[432,128]{1,0:T(8,128)(2,1)S(1)}, bf16[432,128]{1,0:T(8,128)(2,1)S(1)}, u32[]{:S(2)}, u32[]{:S(2)}) collective-permute-start(bf16[432,128]{1,0:T(8,128)(2,1)S(1)} %get-tuple-element.22), channel_id=1, source_target_pairs={{0,1},{1,0},{2,3},{3,2},{4,5},{5,4},{6,7},{7,6},{8,9},{9,8},{10,11... | collective-permute-start | bytes 331784 | tf_op jit(solution)/shard_map/ppermute | solution.py:591
  51.7 12.7 %collective-permute-start.3 = (bf16[432,128]{1,0:T(8,128)(2,1)S(1)}, bf16[432,128]{1,0:T(8,128)(2,1)S(1)}, u32[]{:S(2)}, u32[]{:S(2)}) collective-permute-start(bf16[432,128]{1,0:T(8,128)(2,1)S(1)} %get-tuple-element.23), channel_id=1, source_target_pairs={{1,2},{2,1},{3,4},{4,3},{5,6},{6,5},{7,511},{511,7},{9,10},{10,9},... | collective-permute-start | bytes 331784 | tf_op jit(solution)/shard_map/ppermute | solution.py:592

commit v3 on v2

--- a/solution.py
+++ b/solution.py
@@ -58,6 +58,60 @@
             slot = slot_ref[step, band, tile]
             rows = wide_ref[pl.ds(slot, pieces, stride=slots), :]
             out_ref[band, at] = rows.astype(jnp.bfloat16)
+
+
+def columns_kernel(
+    slot_ref, store_ref, masked_ref, base_ref, bottom_ref, mail_ref, wide_ref, column_ref, row_ref
+):
+    tile = lax.axis_index("lon")
+    odd = lax.rem(tile, 2)
+    half, height, _ = mail_ref.shape
+    half = half // 2
+    slots = store_ref.shape[0] // (masked_ref.shape[0] // ROWS * 2)
+    pieces = store_ref.shape[0] // slots
+    rows = masked_ref.shape[0] // ROWS
+    edge_lane = odd * (LANES - 1)
+    next_lane = edge_lane + 1 - 2 * odd
+
+    def picks(count):
+        place = (count * LANES, LANES)
+        source, lane = rows_of(place) // LANES, rows_of(place) % LANES
+        chosen = ((lane == edge_lane) & (lanes_of(place) == source)) | (
+            (lane == next_lane) & (lanes_of(place) == source + count)
+        )
+        return jnp.where(chosen, 1.0, 0.0).astype(jnp.bfloat16)
+
+    wide_ref[...] = store_ref[...].astype(jnp.float32)
+    column_ref[...] = jnp.zeros_like(column_ref)
+    stored = [
+        wide_ref[pl.ds(slot, pieces, stride=slots), :].astype(jnp.bfloat16) for slot in range(slots)
+    ]
+    column_ref[0:pieces] = jnp.dot(
+        jnp.concatenate(stored, axis=1), picks(slots), preferred_element_type=jnp.float32
+    )
+    row_ref[...] = jnp.transpose(column_ref[...])
+    column_ref[...] = jnp.zeros_like(column_ref)
+    pick = picks(ROWS)
+    for start, ref in ((0, masked_ref), (LANES, base_ref)):
+        blocks = [strided(ref, row, rows).astype(jnp.bfloat16) for row in range(ROWS)]
+        column_ref[start : start + rows] = jnp.dot(
+            jnp.concatenate(blocks, axis=1), pick, preferred_element_type=jnp.float32
+        )
+    level_rows = jnp.transpose(column_ref[...])[0 : 2 * ROWS]
+    bottom = bottom_ref[...].astype(jnp.float32)
+    bottom = jnp.where(odd == 1, bottom[:, LANES - 1 :], bottom[:, 0:1])
+    spot = (lanes_of(level_rows.shape) == rows) & (rows_of(level_rows.shape) < ROWS)
+    bottom = jnp.concatenate([bottom, bottom], axis=0)
+    level_rows = jnp.where(spot, bottom, level_rows)
+    mail_ref[...] = jnp.zeros_like(mail_ref)
+    blank = jnp.zeros((ROWS - 3, level_rows.shape[1]), jnp.float32)
+    for band in range(half):
+        state = []
+        for step in STEP_ORDER:
+            state.append(row_ref[pl.ds(slot_ref[step, band, tile], 1), :])
+        state.append(row_ref[pl.ds(slots + slot_ref[STEP_ORDER[0], band, tile], 1), :])
+        letter = jnp.concatenate(state + [blank, level_rows], axis=0)
+        mail_ref[odd * half + band] = letter.astype(jnp.bfloat16)
 
 
 def prepare_kernel(table_ref, adjoint_ref, bottom_ref, mix_ref, masked_ref, base_ref, kappa_ref):
@@ -98,6 +152,7 @@
 def edges_kernel(
     offset_ref,
     piece_ref,
+    mail_ref,
     masked_ref,
     base_ref,
     bottom_ref,
@@ -108,6 +163,7 @@
     bot_ref,
     part_ref,
     column_ref,
+    letter_ref,
 ):
     tile = lax.axis_index("lon")
     band = lax.axis_index("lat")
@@ -159,16 +215,36 @@
     to_west = jnp.where(spot, bottom[:, 0:1], edge[0:ROWS]).astype(jnp.bfloat16)
     to_east = jnp.where(spot, bottom[:, LANES - 1 :], edge[ROWS : 2 * ROWS]).astype(jnp.bfloat16)
 
-    @pl.when(lax.rem(tile, 2) == 0)
+    odd = lax.rem(tile, 2)
+
+    @pl.when(odd == 0)
     def _():
         inner_ref[...] = to_east
-        outer_ref[...] = to_west
-
-    @pl.when(lax.rem(tile, 2) == 1)
+
+    @pl.when(odd == 1)
     def _():
         inner_ref[...] = to_west
-        outer_ref[...] = to_east
-
+
+    tiles = offset_ref.shape[2]
+    neighbour = lax.rem(tile + 2 * odd - 1 + tiles, tiles)
+    half = odd * holders
+    for at, step in enumerate(STEP_ORDER):
+        offset = offset_ref[step, band, neighbour]
+        for row in range(ROWS):
+            letter = mail_ref[half + lax.rem(row + offset, holders)].astype(jnp.float32)
+            letter_ref[at * ROWS + row : at * ROWS + row + 1] = letter[at : at + 1]
+            if at == 0:
+                letter_ref[2 * ROWS + row : 2 * ROWS + row + 1] = letter[2:3]
+    own = mail_ref[half + band].astype(jnp.float32)
+    edge_row, next_row = own[ROWS : 2 * ROWS], own[2 * ROWS : 3 * ROWS]
+    chosen = jnp.where(odd == 1, letter_ref[0:ROWS], letter_ref[2 * ROWS : 3 * ROWS])
+    lanes = lanes_of(chosen.shape)
+    zonal = jnp.where(lanes < levels, shift(chosen, -2 * levels, 1), shift(chosen, -levels, 1))
+    sign = (2 * odd - 1).astype(jnp.float32)
+    face = (ADVECT_HALF * zonal + sign * DIFFUSE) * (sign * (next_row - edge_row))
+    part = edge_row[:, LANES:] + face[:, 0:LANES]
+    outer = (letter_ref[0:ROWS], letter_ref[ROWS : 2 * ROWS], edge_row[:, 0:LANES], part)
+    outer_ref[...] = jnp.concatenate(outer, axis=1).astype(jnp.bfloat16)
     layout = Layout(levels)
     wide = lanes_of((levels, LANES))
     for row, inner, draft_ref in ((ROWS - 1, ROWS - 2, top_ref), (0, 1, bot_ref)):
@@ -500,12 +576,6 @@
     return [pair for low, high in pairs for pair in ((low, high), (high, low))]
 
 
-def ring_routes(tiles):
-    inner = swaps((tile, tile + 1) for tile in range(0, tiles, 2))
-    outer = swaps((tile, (tile + 1) % tiles) for tile in range(1, tiles, 2))
-    return inner, outer
-
-
 def line_routes(tiles, bands):
     near, far = [], []
     for tile in range(tiles):
@@ -559,6 +629,20 @@
             mix_class.reshape((levels - 1) * ROWS, LANES),
         ],
     )
+    (mail,) = call(
+        columns_kernel,
+        [((2 * bands, 3 * ROWS, 2 * LANES), narrow)],
+        [(pieces * slots, LANES), (2 * LANES, LANES), (LANES, 2 * LANES)],
+        [holder_slot],
+        [store.reshape(pieces * slots, LANES), masked, base, bottom_level],
+    )
+    groups = [
+        [tile * bands + band for tile in (low, (low + 1) % tiles) for band in range(bands)]
+        for low in range(1, tiles, 2)
+    ]
+    mail = lax.all_to_all(
+        mail, ("lon", "lat"), split_axis=0, concat_axis=0, tiled=True, axis_index_groups=groups
+    )
     state, inner, outer, top, bot = call(
         edges_kernel,
         [
@@ -568,14 +652,12 @@
             ((layout.rows, LANES), wide),
             ((layout.rows, LANES), wide),
         ],
-        [(2 * full, LANES), (EDGE_LANES, LANES)],
+        [(2 * full, LANES), (EDGE_LANES, LANES), (3 * ROWS, 2 * LANES)],
         [holder_offset],
-        [received, masked, base, bottom_level],
-    )
-    inner_routes, outer_routes = ring_routes(tiles)
+        [received, mail, masked, base, bottom_level],
+    )
     near_routes, far_routes = line_routes(tiles, bands)
-    inner = lax.ppermute(inner, "lon", inner_routes)
-    outer = lax.ppermute(outer, "lon", outer_routes)
+    inner = lax.ppermute(inner, "lon", swaps((tile, tile + 1) for tile in range(0, tiles, 2)))
     near, far, west, east = call(
         functools.partial(complete_kernel, levels),
         [

time: 67.3 us -> 81.6 us (1.21)
  blocking collectives: 0 us -> 21.8 us
  waiting for transfers between devices: 29.3 us -> 18.5 us
  local copies, waits for them, and re-layouts: 1.78 us -> 5.69 us
  starting transfers between devices: 27.8 us -> 25.1 us
  Pallas kernels: 7.28 us -> 9.09 us
    all_to_all x0 -> x1, blocking collectives: none -> 21.8 us  [shards(): lax.all_to_all(request, 'lat', split_axis=0, concat_axis=0, tiled=True)]
    ppermute x2 -> x1, starting transfers between devices: 13.9 us -> 1.92 us  [shards(): lax.ppermute(inner, 'lon', swaps(((tile, tile + 1) for tile in range(0, t...]
    all_to_all x1, waiting for transfers between devices: 18.3 us -> 6.71 us  [shards(): lax.all_to_all(mail, ('lon', 'lat'), split_axis=0, concat_axis=0, tiled=T...]
    all_to_all x1, starting transfers between devices: 8.24 us -> 16.7 us  [shards(): lax.all_to_all(mail, ('lon', 'lat'), split_axis=0, concat_axis=0, tiled=T...]
    unnamed x14 -> x22, local copies, waits for them, and re-layouts: 1.78 us -> 5.69 us
    pallas_call x5 -> x6, Pallas kernels: 7.28 us -> 9.09 us  [call(): pl.pallas_call(kernel, out_shape=[jax.ShapeDtypeStruct(shape, dtype) for...]
    ppermute x1, waiting for transfers between devices: 8.66 us -> 10.2 us  [shards(): far = lax.ppermute(far, ('lon', 'lat'), far_routes)]
    ppermute x1, starting transfers between devices: 3.07 us -> 4.14 us  [shards(): far = lax.ppermute(far, ('lon', 'lat'), far_routes)]
  transfers between devices with their start and end apart: 5 -> 4, of which waited for: 4 -> 4; matrix products, arithmetic and copies ran while one was open for 0% -> 0% of each run, Pallas kernels for 1% -> 2%
where the time goes in v3:
time: 81.6 us; the launch traced here: 81 us
  starting transfers between devices  25.1 us (31%)
  blocking collectives  21.8 us (27%)
  waiting for transfers between devices  18.5 us (23%)
  Pallas kernels  9.09 us (11%)
  local copies, waits for them, and re-layouts  5.69 us (7%)
    all_to_all x1, blocking collectives, shards(): lax.all_to_all(request, 'lat', split_axis=0, concat_axis=0, tiled=True)  21.8 us
    all_to_all x1, starting transfers between devices, shards(): lax.all_to_all(mail, ('lon', 'lat'), split_axis=0, concat_axis=0, tiled=T...  16.7 us
    ppermute x1, waiting for transfers between devices, shards(): far = lax.ppermute(far, ('lon', 'lat'), far_routes)  10.2 us
    pallas_call x6, Pallas kernels, call(): pl.pallas_call(kernel, out_shape=[jax.ShapeDtypeStruct(shape, dtype) for...  9.09 us
    all_to_all x1, waiting for transfers between devices, shards(): lax.all_to_all(mail, ('lon', 'lat'), split_axis=0, concat_axis=0, tiled=T...  6.71 us
    unnamed x22, local copies, waits for them, and re-layouts  5.69 us
    ppermute x1, starting transfers between devices, shards(): far = lax.ppermute(far, ('lon', 'lat'), far_routes)  4.14 us
    ppermute x1, starting transfers between devices, shards(): near = lax.ppermute(near, ('lon', 'lat'), near_routes)  2.35 us
  transfers between devices with their start and end apart: 4, of which 4 were waited for; matrix products, arithmetic and copies ran while one was open for 0% of the time, Pallas kernels for 2%

profile of v3, /device:TPU:22, one launch (start us, length us, event | category | flops | bytes accessed | tf_op | source)
XLA Modules:
  0.0 81.0 jit_solution(16024331900342346833)
XLA Ops:
  0.6 1.0 %copy-done.2 = f32[2,38,8,128]{3,2,1,0:T(8,128)S(1)} copy-done((f32[2,38,8,128]{3,2,1,0:T(8,128)S(1)}, f32[2,38,8,128]{3,2,1,0:T(8,128)}, u32[]{:S(2)}) %copy-start.2) | copy-done | bytes 311320
  1.6 0.9 %copy-done.3 = s32[37,8,128]{2,1,0:T(8,128)S(1)} copy-done((s32[37,8,128]{2,1,0:T(8,128)S(1)}, s32[37,8,128]{2,1,0:T(8,128)}, u32[]{:S(2)}) %copy-start.3) | copy-done | bytes 151576
  2.5 0.7 copy-done.4
  3.2 0.7 copy-done.10
  3.9 0.7 shard_map.87
  4.6 0.0 copy-start
  4.6 1.1 %copy-done = bf16[4,38,16,1,128]{4,2,3,1,0:T(8,128)(2,1)S(1)} copy-done((bf16[4,38,16,1,128]{4,2,3,1,0:T(8,128)(2,1)S(1)}, bf16[4,38,16,1,128]{4,2,3,1,0:T(8,128)(2,1)}, u32[]{:S(2)}) %copy-start) | copy-done | bytes 622616
  5.6 0.7 copy-done.5
  6.3 0.7 copy-done.7
  7.0 2.5 %shard_map.88 = bf16[16,24,256]{2,1,0:T(8,128)(2,1)} custom-call(s32[2,8,64]{2,1,0:T(8,128)S(1)} %copy-done.7, bf16[2432,128]{1,0:T(8,128)(2,1)S(1)} %bitcast.5, f32[608,128]{1,0:T(8,128)S(1)} %get-tuple-element.16.masked_ref, f32[608,128]{1,0:T(8,128)S(1)} %get-tuple-element.17.base_ref, s32[8,128]{1,0:T(8,128)S(1)} %copy-done.5), custom_call_target="tpu_custom_call" | custom-call | tf_op jit(solution)/shard_map/pallas_call | solution.py:593
  9.5 16.7 %all-to-all-start.1 = ((bf16[16,24,256]{2,1,0:T(8,128)(2,1)}), bf16[16,24,256]{2,1,0:T(8,128)(2,1)S(1)}, u32[]{:S(2)}, u32[]{:S(2)}) async-start(bf16[16,24,256]{2,1,0:T(8,128)(2,1)} %shard_map.88), calls=%async_computation.1 | async-start | bytes 393216 | tf_op jit(solution)/shard_map/all_to_all | solution.py:643
  26.2 0.0 copy-start.6
  26.2 1.4 %shard_map.86 = bf16[8,2,152,128]{3,2,1,0:T(8,128)(2,1)S(1)} custom-call(s32[2,8,64]{2,1,0:T(8,128)S(1)} %copy-done.8, bf16[2432,128]{1,0:T(8,128)(2,1)S(1)} %bitcast.6), custom_call_target="tpu_custom_call" | custom-call | tf_op jit(solution)/shard_map/pallas_call | solution.py:593
  27.6 6.7 %all-to-all-done.1.mail_ref = bf16[16,24,256]{2,1,0:T(8,128)(2,1)S(1)} async-done(((bf16[16,24,256]{2,1,0:T(8,128)(2,1)}), bf16[16,24,256]{2,1,0:T(8,128)(2,1)S(1)}, u32[]{:S(2)}, u32[]{:S(2)}) %all-to-all-start.1) | async-done | bytes 196640 | tf_op jit(solution)/shard_map/all_to_all | solution.py:643
  34.3 21.8 %all_to_all.10.piece_ref = bf16[8,2,152,128]{3,2,1,0:T(8,128)(2,1)S(1)} all-to-all(bf16[8,2,152,128]{3,2,1,0:T(8,128)(2,1)S(1)} %shard_map.86), channel_id=1, replica_groups=mesh['lon'=64,'lat'=8] {'lat'}, dimensions={0} | all-to-all | bytes 1245184 | tf_op jit(solution)/shard_map/all_to_all | solution.py:620
  56.1 1.6 %shard_map.89 = (f32[2432,128]{1,0:T(8,128)S(1)}, bf16[8,768]{1,0:T(8,128)(2,1)S(1)}, bf16[8,768]{1,0:T(8,128)(2,1)S(1)}, f32[432,128]{1,0:T(8,128)S(1)}, f32[432,128]{1,0:T(8,128)S(1)}) custom-call(s32[2,8,64]{2,1,0:T(8,128)S(1)} %copy-done.9, bf16[8,2,152,128]{3,2,1,0:T(8,128)(2,1)S(1)} %all_to_all.10.piece_ref, ...), custom_call_target="tpu_custom_call" | custom-call | tf_op jit(solution)/shard_map/pallas_call | solution.py:593
  57.7 1.9 %collective-permute-start = (bf16[8,768]{1,0:T(8,128)(2,1)S(1)}, bf16[8,768]{1,0:T(8,128)(2,1)S(1)}, u32[]{:S(2)}, u32[]{:S(2)}) collective-permute-start(bf16[8,768]{1,0:T(8,128)(2,1)S(1)} %get-tuple-element.18), channel_id=1, source_target_pairs={{0,8},{8,0},{16,24},{24,16},{32,40},{40,32},{48,56},{56,48},{64,72... | collective-permute-start | bytes 36872 | tf_op jit(solution)/shard_map/ppermute | solution.py:660
  59.6 1.1 %collective-permute-done.inner_ref = bf16[8,768]{1,0:T(8,128)(2,1)S(1)} collective-permute-done((bf16[8,768]{1,0:T(8,128)(2,1)S(1)}, bf16[8,768]{1,0:T(8,128)(2,1)S(1)}, u32[]{:S(2)}, u32[]{:S(2)}) %collective-permute-start) | collective-permute-done | bytes 12320 | tf_op jit(solution)/shard_map/ppermute | solution.py:660
  60.8 0.3 shard_map.90
  61.1 2.3 %collective-permute-start.1 = (bf16[432,128]{1,0:T(8,128)(2,1)S(1)}, bf16[432,128]{1,0:T(8,128)(2,1)S(1)}, u32[]{:S(2)}, u32[]{:S(2)}) collective-permute-start(bf16[432,128]{1,0:T(8,128)(2,1)S(1)} %get-tuple-element.22), channel_id=1, source_target_pairs={{0,1},{1,0},{2,3},{3,2},{4,5},{5,4},{6,7},{7,6},{8,9},{9,8},{10,11... | collective-permute-start | bytes 331784 | tf_op jit(solution)/shard_map/ppermute | solution.py:673
  63.5 4.1 %collective-permute-start.2 = (bf16[432,128]{1,0:T(8,128)(2,1)S(1)}, bf16[432,128]{1,0:T(8,128)(2,1)S(1)}, u32[]{:S(2)}, u32[]{:S(2)}) collective-permute-start(bf16[432,128]{1,0:T(8,128)(2,1)S(1)} %get-tuple-element.23), channel_id=1, source_target_pairs={{1,2},{2,1},{3,4},{4,3},{5,6},{6,5},{7,511},{511,7},{9,10},{10,9},... | collective-permute-start | bytes 331784 | tf_op jit(solution)/shard_map/ppermute | solution.py:674
  67.6 0.5 collective-permute-done.1.near_ref
  68.1 10.2 %collective-permute-done.2.far_ref = bf16[432,128]{1,0:T(8,128)(2,1)S(1)} collective-permute-done((bf16[432,128]{1,0:T(8,128)(2,1)S(1)}, bf16[432,128]{1,0:T(8,128)(2,1)S(1)}, u32[]{:S(2)}, u32[]{:S(2)}) %collective-permute-start.2) | collective-permute-done | bytes 110624 | tf_op jit(solution)/shard_map/ppermute | solution.py:674
  78.3 2.6 %shard_map.91 = (f32[608,128]{1,0:T(8,128)}, f32[608,128]{1,0:T(8,128)}) custom-call(bf16[432,128]{1,0:T(8,128)(2,1)S(1)} %collective-permute-done.1.near_ref, bf16[432,128]{1,0:T(8,128)(2,1)S(1)} %collective-permute-done.2.far_ref, bf16[8,768]{1,0:T(8,128)(2,1)S(1)} %get-tuple-element.24.west_ref, bf16[8,768]{1,0:T(8,128)(2,1)S(1)} %get-tuple-element.25.east_ref, ...), custom_call_target="tpu_custom_call" | custom-call | tf_op jit(solution)/shard_map/pallas_call | solution.py:593
  (13 shorter events, 0.0 us)
Async XLA Ops:
  0.6 1.0 %copy-start.2 = (f32[2,38,8,128]{3,2,1,0:T(8,128)S(1)}, f32[2,38,8,128]{3,2,1,0:T(8,128)}, u32[]{:S(2)}) copy-start(f32[2,38,8,128]{3,2,1,0:T(8,128)} %param.7) | copy-start | bytes 933892
  1.6 0.9 %copy-start.3 = (s32[37,8,128]{2,1,0:T(8,128)S(1)}, s32[37,8,128]{2,1,0:T(8,128)}, u32[]{:S(2)}) copy-start(s32[37,8,128]{2,1,0:T(8,128)} %param.12) | copy-start | bytes 454660
  2.5 0.7 copy-start.4
  3.2 0.7 copy-start.10
  3.9 22.3 %copy-start.8 = (s32[2,8,64]{2,1,0:T(8,128)S(1)}, s32[2,8,64]{2,1,0:T(8,128)}, u32[]{:S(2)}) copy-start(s32[2,8,64]{2,1,0:T(8,128)} %slot_ref.3) | copy-start | bytes 12292
  4.6 1.1 %copy-start = (bf16[4,38,16,1,128]{4,2,3,1,0:T(8,128)(2,1)S(1)}, bf16[4,38,16,1,128]{4,2,3,1,0:T(8,128)(2,1)}, u32[]{:S(2)}) copy-start(bf16[4,38,16,1,128]{4,2,3,1,0:T(8,128)(2,1)} %param.8) | copy-start | bytes 1867780
  5.6 0.7 copy-start.5
  6.3 0.7 copy-start.7
  7.0 19.2 %copy-start.1 = (bf16[4,38,16,1,128]{4,2,3,1,0:T(8,128)(2,1)S(1)}, bf16[4,38,16,1,128]{4,2,3,1,0:T(8,128)(2,1)}, u32[]{:S(2)}) copy-start(bf16[4,38,16,1,128]{4,2,3,1,0:T(8,128)(2,1)} %param.8) | copy-start | bytes 1867780
  9.5 24.8 %all-to-all-start.1 = ((bf16[16,24,256]{2,1,0:T(8,128)(2,1)}), bf16[16,24,256]{2,1,0:T(8,128)(2,1)S(1)}, u32[]{:S(2)}, u32[]{:S(2)}) async-start(bf16[16,24,256]{2,1,0:T(8,128)(2,1)} %shard_map.88), calls=%async_computation.1 | async-start | bytes 393216 | tf_op jit(solution)/shard_map/all_to_all | solution.py:643
  26.2 29.9 %copy-start.6 = (s32[8,128]{1,0:T(8,128)S(1)}, s32[8,128]{1,0:T(8,128)}, u32[]{:S(2)}) copy-start(s32[8,128]{1,0:T(8,128)} %bottom_ref.7) | copy-start | bytes 12292
  26.2 29.9 %copy-start.9 = (s32[2,8,64]{2,1,0:T(8,128)S(1)}, s32[2,8,64]{2,1,0:T(8,128)}, u32[]{:S(2)}) copy-start(s32[2,8,64]{2,1,0:T(8,128)} %offset_ref.1) | copy-start | bytes 12292
  57.7 3.1 %collective-permute-start = (bf16[8,768]{1,0:T(8,128)(2,1)S(1)}, bf16[8,768]{1,0:T(8,128)(2,1)S(1)}, u32[]{:S(2)}, u32[]{:S(2)}) collective-permute-start(bf16[8,768]{1,0:T(8,128)(2,1)S(1)} %get-tuple-element.18), channel_id=1, source_target_pairs={{0,8},{8,0},{16,24},{24,16},{32,40},{40,32},{48,56},{56,48},{64,72... | collective-permute-start | bytes 36872 | tf_op jit(solution)/shard_map/ppermute | solution.py:660
  61.1 7.0 %collective-permute-start.1 = (bf16[432,128]{1,0:T(8,128)(2,1)S(1)}, bf16[432,128]{1,0:T(8,128)(2,1)S(1)}, u32[]{:S(2)}, u32[]{:S(2)}) collective-permute-start(bf16[432,128]{1,0:T(8,128)(2,1)S(1)} %get-tuple-element.22), channel_id=1, source_target_pairs={{0,1},{1,0},{2,3},{3,2},{4,5},{5,4},{6,7},{7,6},{8,9},{9,8},{10,11... | collective-permute-start | bytes 331784 | tf_op jit(solution)/shard_map/ppermute | solution.py:673
  63.5 14.8 %collective-permute-start.2 = (bf16[432,128]{1,0:T(8,128)(2,1)S(1)}, bf16[432,128]{1,0:T(8,128)(2,1)S(1)}, u32[]{:S(2)}, u32[]{:S(2)}) collective-permute-start(bf16[432,128]{1,0:T(8,128)(2,1)S(1)} %get-tuple-element.23), channel_id=1, source_target_pairs={{1,2},{2,1},{3,4},{4,3},{5,6},{6,5},{7,511},{511,7},{9,10},{10,9},... | collective-permute-start | bytes 331784 | tf_op jit(solution)/shard_map/ppermute | solution.py:674

commit v4 on v2

v4 whole, which is shorter than its diff:
```python
import functools

import jax
import jax.numpy as jnp
from jax import lax
from jax.experimental import pallas as pl
from jax.experimental.pallas import tpu as pltpu
from jax.sharding import PartitionSpec as P

STEP_ORDER = (1, 0)
FIELDS = 4
ADVECT_HALF = 0.125
DIFFUSE = 0.1

ROWS = 8
LANES = 128

EDGE_STATE = (0, 256)
EDGE_MASKED = 512
EDGE_PART = 640
EDGE_LANES = 768


class Layout:
    def __init__(self, levels):
        self.tracer = (0, 3 * levels)
        self.merid = (2 * levels, 5 * levels)
        self.masked = 6 * levels
        self.part = 8 * levels
        self.corner = 10 * levels
        self.bottom = 11 * levels
        self.rows = (11 * levels + 1 + 15) // 16 * 16


def shift(block, amount, axis):
    return pltpu.roll(block, amount % block.shape[axis], axis)


def lanes_of(shape):
    return lax.broadcasted_iota(jnp.int32, shape, 1)


def rows_of(shape):
    return lax.broadcasted_iota(jnp.int32, shape, 0)


def strided(ref, start, count):
    return ref[pl.ds(start, count, stride=ROWS), :]


def request_kernel(
    slot_hbm, store_hbm, out_hbm, slot_ref, store_ref, wide_ref, pack_ref, slot_sem, in_sem, out_sem
):
    tile = lax.axis_index("lon")
    bands, steps, pieces, lanes = pack_ref.shape
    slots = store_ref.shape[0] // pieces
    length = store_ref.shape[0] // FIELDS
    table = pltpu.make_async_copy(slot_hbm, slot_ref, slot_sem)
    table.start()
    loads = []
    for field in range(FIELDS):
        here = pl.ds(field * length, length)
        load = pltpu.make_async_copy(store_hbm.at[here], store_ref.at[here], in_sem.at[field])
        load.start()
        loads.append(load)
    for field, load in enumerate(loads):
        load.wait()
        here = slice(field * length, (field + 1) * length)
        wide_ref[here] = store_ref[here].astype(jnp.float32)
    table.wait()
    stores = []
    for band in range(bands):
        for at, step in enumerate(STEP_ORDER):
            slot = slot_ref[step, band, tile]
            rows = wide_ref[pl.ds(slot, pieces, stride=slots), :]
            pack_ref[band, at] = rows.astype(jnp.bfloat16)
        store = pltpu.make_async_copy(pack_ref.at[band], out_hbm.at[band], out_sem.at[band])
        store.start()
        stores.append(store)
    for store in stores:
        store.wait()


def pick_columns():
    place = (ROWS * LANES, LANES)
    row, source = rows_of(place) // LANES, rows_of(place) % LANES
    order = lanes_of(place) - row
    chosen = (
        ((source == 0) & (order == 0))
        | ((source == LANES - 1) & (order == ROWS))
        | ((source == 1) & (order == 2 * ROWS))
        | ((source == LANES - 2) & (order == 3 * ROWS))
    )
    return jnp.where(chosen, 1.0, 0.0).astype(jnp.bfloat16)


def prepare_kernel(
    table_ref,
    adjoint_ref,
    bottom_ref,
    mix_ref,
    masked_ref,
    base_ref,
    kappa_ref,
    side_ref,
    pick_ref,
    column_ref,
):
    levels = adjoint_ref.shape[0] // (2 * ROWS)
    bottom = bottom_ref[...]
    edge = jnp.zeros((ROWS, LANES), jnp.float32)
    kappa_ref[0:ROWS] = edge
    kappa_ref[levels * ROWS : (levels + 1) * ROWS] = edge
    for level in range(levels - 1):
        classes = mix_ref[level * ROWS : (level + 1) * ROWS]
        kappa = jnp.full((ROWS, LANES), table_ref[0], jnp.float32)
        for index in range(1, table_ref.shape[0]):
            kappa = jnp.where(classes == index, table_ref[index], kappa)
        kappa_ref[(level + 1) * ROWS : (level + 2) * ROWS] = kappa
    for tracer in range(2):
        start = tracer * levels * ROWS
        for level in range(levels):
            here = slice(start + level * ROWS, start + (level + 1) * ROWS)
            masked_ref[here] = jnp.where(level < bottom, adjoint_ref[here], 0.0)
        for level in range(levels):
            base_ref[start + level * ROWS : start + (level + 1) * ROWS] = mixed(
                masked_ref, kappa_ref, start, level, levels
            )
    pick = pick_columns()
    pick_ref[...] = pick
    column_ref[...] = jnp.zeros_like(column_ref)
    rows = 2 * levels
    for start, ref in ((0, masked_ref), (LANES, base_ref)):
        blocks = [strided(ref, row, rows).astype(jnp.bfloat16) for row in range(ROWS)]
        column_ref[start : start + rows] = jnp.dot(
            jnp.concatenate(blocks, axis=1), pick, preferred_element_type=jnp.float32
        )
    side = jnp.transpose(column_ref[...])[0 : 4 * ROWS]
    spot = lanes_of((ROWS, 2 * LANES)) == rows
    depth = bottom.astype(jnp.float32)
    side_ref[...] = side
    side_ref[0:ROWS] = jnp.where(spot, depth[:, 0:1], side[0:ROWS])
    side_ref[ROWS : 2 * ROWS] = jnp.where(spot, depth[:, LANES - 1 :], side[ROWS : 2 * ROWS])


def mixed(masked_ref, kappa_ref, start, level, levels):
    def at(index):
        return masked_ref[start + index * ROWS : start + (index + 1) * ROWS]

    masked = at(level)
    below = at(level + 1) if level + 1 < levels else jnp.zeros_like(masked)
    above = at(level - 1) if level > 0 else jnp.zeros_like(masked)
    kappa_above = kappa_ref[level * ROWS : (level + 1) * ROWS]
    kappa_below = kappa_ref[(level + 1) * ROWS : (level + 2) * ROWS]
    return masked + kappa_below * (below - masked) + kappa_above * (above - masked)


def edges_kernel(
    offset_ref, piece_ref, side_ref, pick_ref, outer_ref, inner_ref, column_ref
):
    tile = lax.axis_index("lon")
    band = lax.axis_index("lat")
    holders, _, pieces, _ = piece_ref.shape
    levels = pieces // FIELDS
    column_ref[...] = jnp.zeros_like(column_ref)
    for at, step in enumerate(STEP_ORDER):
        offset = offset_ref[step, band, tile]
        chunks = [piece_ref[lax.rem(row + offset, holders), at] for row in range(ROWS)]
        column_ref[EDGE_STATE[at] : EDGE_STATE[at] + pieces] = jnp.dot(
            jnp.concatenate(chunks, axis=1), pick_ref[...], preferred_element_type=jnp.float32
        )
    state = jnp.transpose(column_ref[...])
    lane = lanes_of((ROWS, 2 * LANES))
    sides = []
    for at, sign in ((0, 1.0), (1, -1.0)):
        edge = state[at * ROWS : (at + 1) * ROWS]
        zonal = edge if at == 0 else state[3 * ROWS : 4 * ROWS]
        zonal = zonal[:, 0 : 2 * LANES]
        zonal = jnp.where(lane < levels, shift(zonal, -2 * levels, 1), shift(zonal, -levels, 1))
        masked = side_ref[at * ROWS : (at + 1) * ROWS]
        beside = side_ref[(at + 2) * ROWS : (at + 3) * ROWS]
        face = (ADVECT_HALF * zonal + sign * DIFFUSE) * (sign * (beside - masked))
        part = masked[:, LANES:] + face[:, 0:LANES]
        side = jnp.concatenate([edge, masked[:, 0:LANES], part], axis=1)
        sides.append(side.astype(jnp.bfloat16))
    to_west, to_east = sides

    @pl.when(lax.rem(tile, 2) == 0)
    def _():
        inner_ref[...] = to_east
        outer_ref[...] = to_west

    @pl.when(lax.rem(tile, 2) == 1)
    def _():
        inner_ref[...] = to_west
        outer_ref[...] = to_east


def drafts_kernel(
    offset_ref, piece_ref, masked_ref, base_ref, bottom_ref, state_ref, top_ref, bot_ref
):
    tile = lax.axis_index("lon")
    band = lax.axis_index("lat")
    levels = masked_ref.shape[0] // (2 * ROWS)
    pieces = FIELDS * levels
    holders = piece_ref.shape[0]
    for at, step in enumerate(STEP_ORDER):
        offset = offset_ref[step, band, tile]
        for row in range(ROWS):
            chunk = piece_ref[lax.rem(row + offset, holders), at]
            state_ref[pl.ds(at * pieces * ROWS + row, pieces, stride=ROWS), :] = chunk.astype(
                jnp.float32
            )
    bottom = bottom_ref[...].astype(jnp.float32)
    layout = Layout(levels)
    wide = lanes_of((levels, LANES))
    for row, inner, draft_ref in ((ROWS - 1, ROWS - 2, top_ref), (0, 1, bot_ref)):
        for at in range(2):
            begin = at * pieces * ROWS
            draft_ref[layout.tracer[at] : layout.tracer[at] + 2 * levels] = strided(
                state_ref, begin + row, 2 * levels
            )
            draft_ref[layout.merid[at] : layout.merid[at] + levels] = strided(
                state_ref, begin + 3 * levels * ROWS + row, levels
            )
        zonal = strided(state_ref, 2 * levels * ROWS + row, levels)
        merid = strided(state_ref, 3 * levels * ROWS + min(row, inner), levels)
        east_factor = ADVECT_HALF * zonal + DIFFUSE
        west_factor = ADVECT_HALF * shift(zonal, 1, 1) - DIFFUSE
        for tracer in range(2):
            begin = tracer * levels * ROWS
            masked = strided(masked_ref, begin + row, levels)
            next_row = strided(masked_ref, begin + inner, levels)
            if row > inner:
                along = (ADVECT_HALF * merid - DIFFUSE) * (masked - next_row)
            else:
                along = (ADVECT_HALF * merid + DIFFUSE) * (next_row - masked)
            east = east_factor * (shift(masked, -1, 1) - masked)
            west = west_factor * (masked - shift(masked, 1, 1))
            part = strided(base_ref, begin + row, levels) + along
            part = part + jnp.where(wide < LANES - 1, east, 0.0) + jnp.where(wide > 0, west, 0.0)
            at_masked = layout.masked + tracer * levels
            at_part = layout.part + tracer * levels
            draft_ref[at_masked : at_masked + levels] = masked
            draft_ref[at_part : at_part + levels] = part
        draft_ref[layout.corner : layout.corner + levels] = zonal
        draft_ref[layout.bottom : layout.rows] = jnp.broadcast_to(
            bottom[row : row + 1], (layout.rows - layout.bottom, LANES)
        )


def complete_kernel(
    levels,
    outer_ref,
    inner_ref,
    top_draft_ref,
    bot_draft_ref,
    far_ref,
    near_ref,
    west_ref,
    east_ref,
    pack_ref,
    edge_ref,
    column_ref,
    top_ref,
    bot_ref,
):
    layout = Layout(levels)
    odd_tile = lax.rem(lax.axis_index("lon"), 2) == 1
    odd_band = lax.rem(lax.axis_index("lat"), 2) == 1

    @pl.when(odd_tile)
    def _():
        west_ref[...] = inner_ref[...]
        east_ref[...] = outer_ref[...]

    @pl.when(jnp.logical_not(odd_tile))
    def _():
        west_ref[...] = outer_ref[...]
        east_ref[...] = inner_ref[...]

    top_ref[...] = top_draft_ref[...]
    bot_ref[...] = bot_draft_ref[...]
    edge_ref[...] = jnp.zeros_like(edge_ref)
    edge_ref[0:ROWS] = west_ref[...].astype(jnp.float32)
    edge_ref[ROWS : 2 * ROWS] = east_ref[...].astype(jnp.float32)
    column_ref[...] = jnp.transpose(edge_ref[...])
    lane = lanes_of((levels, LANES))

    def pair(start, row):
        block = column_ref[start : start + levels]
        return block[:, row : row + 1], block[:, ROWS + row : ROWS + row + 1]

    for row, draft_ref in ((ROWS - 1, top_ref), (0, bot_ref)):
        zonal = draft_ref[layout.corner : layout.corner + levels]
        zonal_west, _ = pair(EDGE_STATE[0] + 2 * levels, row)
        merid_west, merid_east = pair(EDGE_STATE[0] + 3 * levels, row)
        east_factor = ADVECT_HALF * zonal + DIFFUSE
        west_factor = ADVECT_HALF * zonal_west - DIFFUSE
        corner = jnp.where((lane == 32) | (lane == 96), merid_west, 0.0)
        corner = jnp.where((lane == 31) | (lane == 95), merid_east, corner)
        for tracer in range(2):
            west, east = pair(EDGE_MASKED + tracer * levels, row)
            at_masked = layout.masked + tracer * levels
            at_part = layout.part + tracer * levels
            masked = draft_ref[at_masked : at_masked + levels]
            face = jnp.where(lane == LANES - 1, east_factor * (east - masked), 0.0)
            face = jnp.where(lane == 0, west_factor * (masked - west), face)
            draft_ref[at_part : at_part + levels] = draft_ref[at_part : at_part + levels] + face
            corner = jnp.where(lane == (0, LANES // 2)[tracer], west, corner)
            corner = jnp.where(lane == (LANES - 1, LANES // 2 - 1)[tracer], east, corner)
        draft_ref[layout.corner : layout.corner + levels] = corner
        begin = 0 if row else levels
        pack_ref[begin : begin + levels] = corner

    @pl.when(odd_band)
    def _():
        near_ref[...] = bot_ref[...].astype(jnp.bfloat16)
        far_ref[...] = top_ref[...].astype(jnp.bfloat16)

    @pl.when(jnp.logical_not(odd_band))
    def _():
        near_ref[...] = top_ref[...].astype(jnp.bfloat16)
        far_ref[...] = bot_ref[...].astype(jnp.bfloat16)


class Tile:
    def __init__(self, levels, west_ref, east_ref, state_ref):
        self.levels = levels
        self.west_ref, self.east_ref, self.state_ref = west_ref, east_ref, state_ref
        self.shape = (ROWS, LANES)
        lane, row = lanes_of(self.shape), rows_of(self.shape)
        self.first_lane, self.last_lane = lane == 0, lane == LANES - 1
        self.bottom_row, self.top_row = row == 0, row == ROWS - 1

    def spread(self, ref, index):
        return jnp.broadcast_to(ref[:, index : index + 1].astype(jnp.float32), self.shape)

    def line(self, ref, index):
        return jnp.broadcast_to(ref[index : index + 1], self.shape)

    def side(self, index):
        return jnp.where(
            self.first_lane, self.spread(self.west_ref, index), self.spread(self.east_ref, index)
        )

    def velocities(self, at, level):
        begin = at * FIELDS * self.levels
        zonal = tile_of(self.state_ref, begin + 2 * self.levels + level)
        merid = tile_of(self.state_ref, begin + 3 * self.levels + level)
        zonal_west = jnp.where(
            self.first_lane,
            self.spread(self.west_ref, EDGE_STATE[at] + 2 * self.levels + level),
            shift(zonal, 1, 1),
        )
        return ADVECT_HALF * zonal, ADVECT_HALF * zonal_west, merid

    def tracer(self, at, level, tracer):
        field = tile_of(self.state_ref, (at * FIELDS + tracer) * self.levels + level)
        east = jnp.where(
            self.last_lane,
            self.spread(self.east_ref, EDGE_STATE[at] + tracer * self.levels + level),
            shift(field, -1, 1),
        )
        return field, east


def tile_of(ref, index):
    return ref[index * ROWS : (index + 1) * ROWS]


def first_step_kernel(
    west_ref,
    east_ref,
    state_ref,
    masked_ref,
    base_ref,
    bottom_ref,
    next_ref,
    side_ref,
    velocity_ref,
):
    levels = masked_ref.shape[0] // (2 * ROWS)
    tile = Tile(levels, west_ref, east_ref, state_ref)
    first_lane, last_lane = tile.first_lane, tile.last_lane
    top_row, bottom_row = tile.top_row, tile.bottom_row
    bottom = bottom_ref[...]
    side_bottom = tile.side(EDGE_MASKED + 2 * levels)
    for level in range(levels):
        zonal, zonal_west, merid = tile.velocities(0, level)
        north_factor = ADVECT_HALF * merid + DIFFUSE
        south_factor = ADVECT_HALF * shift(merid, 1, 0) - DIFFUSE
        side_merid = tile.side(EDGE_STATE[0] + 3 * levels + level)
        side_north = ADVECT_HALF * side_merid + DIFFUSE
        side_south = ADVECT_HALF * shift(side_merid, 1, 0) - DIFFUSE
        zonal_total = jnp.zeros(tile.shape, jnp.float32)
        merid_total = jnp.zeros(tile.shape, jnp.float32)
        for tracer in range(2):
            index = tracer * levels + level
            masked = tile_of(masked_ref, index)
            west = tile.spread(west_ref, EDGE_MASKED + index)
            east = tile.spread(east_ref, EDGE_MASKED + index)
            side = jnp.where(first_lane, west, east)
            to_east = jnp.where(last_lane, east, shift(masked, -1, 1)) - masked
            to_west = masked - jnp.where(first_lane, west, shift(masked, 1, 1))
            to_north = jnp.where(top_row, 0.0, shift(masked, -1, 0) - masked)
            to_south = jnp.where(bottom_row, 0.0, masked - shift(masked, 1, 0))
            result = (
                tile_of(base_ref, index)
                + (zonal + DIFFUSE) * to_east
                + (zonal_west - DIFFUSE) * to_west
                + north_factor * to_north
                + south_factor * to_south
            )
            next_ref[index * ROWS : (index + 1) * ROWS] = jnp.where(level < bottom, result, 0.0)
            field, field_east = tile.tracer(0, level, tracer)
            zonal_total = zonal_total + (field + field_east) * to_east
            merid_total = merid_total + (field + shift(field, -1, 0)) * to_north
            face = jnp.where(
                first_lane,
                (zonal_west + DIFFUSE) * (masked - side),
                (zonal - DIFFUSE) * (side - masked),
            )
            upper = jnp.where(top_row, 0.0, shift(side, -1, 0) - side)
            lower = jnp.where(bottom_row, 0.0, side - shift(side, 1, 0))
            result = (
                tile.side(EDGE_PART + index) + face + side_north * upper + side_south * lower
            )
            side_ref[index * ROWS : (index + 1) * ROWS] = jnp.where(
                side_bottom > level, result, 0.0
            )
        velocity_ref[level * ROWS : (level + 1) * ROWS] = ADVECT_HALF * zonal_total
        velocity_ref[(levels + level) * ROWS : (levels + level + 1) * ROWS] = (
            ADVECT_HALF * merid_total
        )


def second_step_kernel(
    far_ref,
    near_ref,
    pack_ref,
    west_ref,
    east_ref,
    state_ref,
    masked_ref,
    kappa_ref,
    bottom_ref,
    next_in_ref,
    side_in_ref,
    velocity_in_ref,
    adjoint_ref,
    velocity_ref,
    north_ref,
    south_ref,
    next_ref,
    side_ref,
    ring_ref,
):
    levels = masked_ref.shape[0] // (2 * ROWS)
    layout = Layout(levels)
    band = lax.axis_index("lat")
    odd_band = lax.rem(band, 2) == 1
    top_band = (band == lax.axis_size("lat") - 1).astype(jnp.int32)
    folded = top_band.astype(jnp.float32)
    open_south = jnp.where(band > 0, DIFFUSE, 0.0)
    square = (LANES, LANES)
    from_lane = rows_of(square)
    turned = from_lane + top_band * (LANES - 1 - 2 * from_lane)
    turn = jnp.where(lanes_of(square) == turned, 1.0, 0.0).astype(jnp.bfloat16)

    @pl.when(odd_band)
    def _():
        north_ref[...] = jnp.dot(far_ref[...], turn, preferred_element_type=jnp.float32)
        south_ref[...] = near_ref[...].astype(jnp.float32)

    @pl.when(jnp.logical_not(odd_band))
    def _():
        north_ref[...] = jnp.dot(near_ref[...], turn, preferred_element_type=jnp.float32)
        south_ref[...] = far_ref[...].astype(jnp.float32)

    next_ref[...] = next_in_ref[...]
    side_ref[...] = side_in_ref[...]
    velocity_ref[...] = velocity_in_ref[...]
    for at in range(2):
        here = slice(layout.merid[at], layout.merid[at] + levels)
        north_ref[here] = north_ref[here] * folded

    def rows_at(ref, begin):
        return ref[begin : begin + levels]

    def unpacked(packed):
        return packed, shift(packed, LANES // 2, 1), shift(packed, 96, 1)

    level_of = rows_of((levels, LANES)).astype(jnp.float32)
    left = lanes_of((levels, LANES)) < LANES // 2

    def side_depth(row):
        spot = slice(EDGE_MASKED + 2 * levels, EDGE_MASKED + 2 * levels + 1)
        west = west_ref[...].astype(jnp.float32)[row : row + 1, spot]
        east = east_ref[...].astype(jnp.float32)[row : row + 1, spot]
        return jnp.where(left, west, east)

    def add_rows(ref, begin, value):
        here = pl.ds(begin, levels, stride=ROWS)
        ref[here, :] = ref[here, :] + value

    top = ROWS - 1
    depth = bottom_ref[...].astype(jnp.float32)
    top_merid = strided(state_ref, 3 * levels * ROWS + top, levels)
    north_merid = rows_at(north_ref, layout.merid[0])
    south_merid = rows_at(south_ref, layout.merid[0])
    top_factor = ADVECT_HALF * (top_merid - north_merid) + DIFFUSE
    bottom_factor = ADVECT_HALF * south_merid - open_south
    own_top = unpacked(rows_at(pack_ref, 0))
    own_bottom = unpacked(rows_at(pack_ref, levels))
    north_corner = unpacked(rows_at(north_ref, layout.corner))
    south_corner = unpacked(rows_at(south_ref, layout.corner))
    side_top_factor = ADVECT_HALF * (own_top[2] - folded * north_corner[2]) + DIFFUSE
    side_bottom_factor = ADVECT_HALF * south_corner[2] - open_south
    merid_total = jnp.zeros((levels, LANES), jnp.float32)
    for tracer in range(2):
        start = tracer * levels * ROWS
        masked = strided(masked_ref, start + top, levels)
        beyond = rows_at(north_ref, layout.masked + tracer * levels)
        part = rows_at(north_ref, layout.part + tracer * levels)
        step = beyond - masked
        add_rows(
            next_ref, start + top, jnp.where(level_of < depth[top:], top_factor * step, 0.0)
        )
        ring = part - (ADVECT_HALF * (north_merid - top_merid) + DIFFUSE) * step
        wet = level_of < north_ref[layout.bottom : layout.bottom + 1]
        ring_ref[tracer * levels : (tracer + 1) * levels] = jnp.where(wet, ring, 0.0)
        field = strided(state_ref, start + top, levels)
        field_north = rows_at(north_ref, layout.tracer[0] + tracer * levels)
        merid_total = merid_total + (field + field_north) * step
        masked = strided(masked_ref, start, levels)
        beyond = rows_at(south_ref, layout.masked + tracer * levels)
        part = rows_at(south_ref, layout.part + tracer * levels)
        step = masked - beyond
        add_rows(
            next_ref, start, jnp.where(level_of < depth[0:1], bottom_factor * step, 0.0)
        )
        ring = part + (ADVECT_HALF * south_merid + DIFFUSE) * step
        wet = level_of < south_ref[layout.bottom : layout.bottom + 1]
        ring_ref[(2 + tracer) * levels : (3 + tracer) * levels] = jnp.where(wet, ring, 0.0)
        face = side_top_factor * (north_corner[tracer] - own_top[tracer])
        add_rows(side_ref, start + top, jnp.where(level_of < side_depth(top), face, 0.0))
        face = side_bottom_factor * (own_bottom[tracer] - south_corner[tracer])
        add_rows(side_ref, start, jnp.where(level_of < side_depth(0), face, 0.0))
    add_rows(velocity_ref, levels * ROWS + top, ADVECT_HALF * merid_total)

    tile = Tile(levels, west_ref, east_ref, state_ref)
    first_lane, last_lane = tile.first_lane, tile.last_lane
    top_row, bottom_row = tile.top_row, tile.bottom_row
    closed = (band == 0).astype(jnp.int32)
    spread_south = jnp.where(rows_of(tile.shape) >= closed, DIFFUSE, 0.0)
    for level in range(levels):
        zonal, zonal_west, merid = tile.velocities(1, level)
        merid_south = jnp.where(
            bottom_row, tile.line(south_ref, layout.merid[1] + level), shift(merid, 1, 0)
        )
        merid_net = merid - jnp.where(top_row, tile.line(north_ref, layout.merid[1] + level), 0.0)
        north_factor = ADVECT_HALF * merid_net + DIFFUSE
        south_factor = ADVECT_HALF * merid_south - spread_south
        zonal_total = jnp.zeros(tile.shape, jnp.float32)
        merid_total = jnp.zeros(tile.shape, jnp.float32)
        for tracer in range(2):
            index = tracer * levels + level
            masked = tile_of(next_ref, index)
            side = tile_of(side_ref, index)
            to_east = jnp.where(last_lane, side, shift(masked, -1, 1)) - masked
            to_west = masked - jnp.where(first_lane, side, shift(masked, 1, 1))
            to_north = jnp.where(top_row, tile.line(ring_ref, index), shift(masked, -1, 0)) - masked
            to_south = masked - jnp.where(
                bottom_row, tile.line(ring_ref, 2 * levels + index), shift(masked, 1, 0)
            )
            adjoint_ref[index * ROWS : (index + 1) * ROWS] = (
                mixed(next_ref, kappa_ref, tracer * levels * ROWS, level, levels)
                + (zonal + DIFFUSE) * to_east
                + (zonal_west - DIFFUSE) * to_west
                + north_factor * to_north
                + south_factor * to_south
            )
            field, field_east = tile.tracer(1, level, tracer)
            field_north = jnp.where(
                top_row,
                tile.line(north_ref, layout.tracer[1] + tracer * levels + level),
                shift(field, -1, 0),
            )
            zonal_total = zonal_total + (field + field_east) * to_east
            merid_total = merid_total + (field + field_north) * to_north
        for total, begin in ((zonal_total, 0), (merid_total, levels)):
            here = slice((begin + level) * ROWS, (begin + level + 1) * ROWS)
            velocity_ref[here] = velocity_ref[here] + ADVECT_HALF * total


def swaps(pairs):
    return [pair for low, high in pairs for pair in ((low, high), (high, low))]


def ring_routes(tiles):
    inner = swaps((tile, tile + 1) for tile in range(0, tiles, 2))
    outer = swaps((tile, (tile + 1) % tiles) for tile in range(1, tiles, 2))
    return inner, outer


def line_routes(tiles, bands):
    near, far = [], []
    for tile in range(tiles):
        start = tile * bands
        near += [(start + band, start + band + 1) for band in range(0, bands, 2)]
        far += [(start + band, start + band + 1) for band in range(1, bands - 1, 2)]
        if tile < tiles // 2:
            far.append((start + bands - 1, (tiles - tile) * bands - 1))
    return swaps(near), swaps(far)


def call(kernel, outputs, scratch, scalars, arrays):
    vmem = pl.BlockSpec(memory_space=pltpu.VMEM)
    smem = pl.BlockSpec(memory_space=pltpu.SMEM)
    return pl.pallas_call(
        kernel,
        out_shape=[jax.ShapeDtypeStruct(shape, dtype) for shape, dtype in outputs],
        in_specs=[smem] * len(scalars) + [vmem] * len(arrays),
        out_specs=[vmem] * len(outputs),
        scratch_shapes=[pltpu.VMEM(shape, jnp.float32) for shape in scratch],
        compiler_params=pltpu.CompilerParams(vmem_limit_bytes=32 * 1024 * 1024),
    )(*scalars, *arrays)


def shards(final_adjoint, store, holder_offset, holder_slot, bottom_level, mix_class, mix_table):
    bands = lax.axis_size("lat")
    tiles = lax.axis_size("lon")
    levels = final_adjoint.shape[1]
    slots = store.shape[2]
    steps = len(STEP_ORDER)
    pieces = FIELDS * levels
    full = levels * ROWS
    layout = Layout(levels)
    narrow, wide = jnp.bfloat16, jnp.float32
    hbm = pl.BlockSpec(memory_space=pltpu.HBM)
    request = pl.pallas_call(
        request_kernel,
        out_shape=jax.ShapeDtypeStruct((bands, steps, pieces, LANES), narrow),
        in_specs=[hbm, hbm],
        out_specs=hbm,
        scratch_shapes=[
            pltpu.SMEM(holder_slot.shape, jnp.int32),
            pltpu.VMEM((pieces * slots, LANES), narrow),
            pltpu.VMEM((pieces * slots, LANES), wide),
            pltpu.VMEM((bands, steps, pieces, LANES), narrow),
            pltpu.SemaphoreType.DMA,
            pltpu.SemaphoreType.DMA((FIELDS,)),
            pltpu.SemaphoreType.DMA((bands,)),
        ],
        compiler_params=pltpu.CompilerParams(vmem_limit_bytes=32 * 1024 * 1024),
    )(
        pltpu.with_memory_space_constraint(holder_slot, pltpu.HBM),
        pltpu.with_memory_space_constraint(store.reshape(pieces * slots, LANES), pltpu.HBM),
    )
    received = lax.all_to_all(request, "lat", split_axis=0, concat_axis=0, tiled=True)
    masked, base, kappa, side, pick = call(
        prepare_kernel,
        [
            ((2 * full, LANES), wide),
            ((2 * full, LANES), wide),
            ((full + ROWS, LANES), wide),
            ((4 * ROWS, 2 * LANES), wide),
            ((ROWS * LANES, LANES), narrow),
        ],
        [(2 * LANES, LANES)],
        [mix_table],
        [
            final_adjoint.reshape(2 * full, LANES),
            bottom_level,
            mix_class.reshape((levels - 1) * ROWS, LANES),
        ],
    )
    outer, inner = call(
        edges_kernel,
        [((ROWS, EDGE_LANES), narrow), ((ROWS, EDGE_LANES), narrow)],
        [(EDGE_MASKED, LANES)],
        [holder_offset],
        [received, side, pick],
    )
    inner_routes, outer_routes = ring_routes(tiles)
    near_routes, far_routes = line_routes(tiles, bands)
    outer = lax.ppermute(outer, "lon", outer_routes)
    inner = lax.ppermute(inner, "lon", inner_routes)
    state, top, bot = call(
        drafts_kernel,
        [
            ((steps * FIELDS * full, LANES), wide),
            ((layout.rows, LANES), wide),
            ((layout.rows, LANES), wide),
        ],
        [],
        [holder_offset],
        [received, masked, base, bottom_level],
    )
    far, near, west, east, pack = call(
        functools.partial(complete_kernel, levels),
        [
            ((layout.rows, LANES), narrow),
            ((layout.rows, LANES), narrow),
            ((ROWS, EDGE_LANES), narrow),
            ((ROWS, EDGE_LANES), narrow),
            ((2 * levels, LANES), wide),
        ],
        [(LANES, EDGE_LANES), (EDGE_LANES, LANES), (layout.rows, LANES), (layout.rows, LANES)],
        [],
        [outer, inner, top, bot],
    )
    far = lax.ppermute(far, ("lon", "lat"), far_routes)
    near = lax.ppermute(near, ("lon", "lat"), near_routes)
    following, beside, velocity = call(
        first_step_kernel,
        [((2 * full, LANES), wide)] * 3,
        [],
        [],
        [west, east, state, masked, base, bottom_level],
    )
    adjoint, velocity = call(
        second_step_kernel,
        [((2 * full, LANES), wide)] * 2,
        [
            (layout.rows, LANES),
            (layout.rows, LANES),
            (2 * full, LANES),
            (2 * full, LANES),
            (4 * levels, LANES),
        ],
        [],
        [
            far,
            near,
            pack,
            west,
            east,
            state,
            masked,
            kappa,
            bottom_level,
            following,
            beside,
            velocity,
        ],
    )
    shape = (2, levels, ROWS, LANES)
    return adjoint.reshape(shape), velocity.reshape(shape)


def solution(mesh):
    return jax.shard_map(
        shards,
        mesh=mesh,
        in_specs=(
            P(None, None, "lat", "lon"),
            P(None, None, None, "lat", "lon"),
            P(),
            P(),
            P("lat", "lon"),
            P(None, "lat", "lon"),
            P(),
        ),
        out_specs=(P(None, None, "lat", "lon"), P(None, None, "lat", "lon")),
        check_vma=False,
    )
```

time: 67.3 us -> 61.8 us (0.918)
  waiting for transfers between devices: 29.3 us -> 25.2 us
  local copies, waits for them, and re-layouts: 1.78 us -> 0.02 us
  Pallas kernels: 7.28 us -> 8.98 us
  starting transfers between devices: 27.8 us -> 26.6 us
    pallas_call x0 -> x1, Pallas kernels: none -> 2.61 us  [shards(): pl.pallas_call(request_kernel, out_shape=jax.ShapeDtypeStruct((bands, ste...]
    unnamed x14 -> x10, local copies, waits for them, and re-layouts: 1.78 us -> 0.02 us
    ppermute x1, waiting for transfers between devices: 8.66 us -> 7.22 us  [shards(): far = lax.ppermute(far, ('lon', 'lat'), far_routes)]
    ppermute x1, waiting for transfers between devices: 1.37 us -> 0.01 us  [shards(): outer = lax.ppermute(outer, 'lon', outer_routes)]
    ppermute x1, waiting for transfers between devices: 0.91 us -> 0.01 us  [shards(): near = lax.ppermute(near, ('lon', 'lat'), near_routes)]
    pallas_call x5 -> x6, Pallas kernels: 7.28 us -> 6.37 us  [call(): pl.pallas_call(kernel, out_shape=[jax.ShapeDtypeStruct(shape, dtype) for...]
    ppermute x1, starting transfers between devices: 12 us -> 11.2 us  [shards(): outer = lax.ppermute(outer, 'lon', outer_routes)]
  transfers between devices with their start and end apart: 5 -> 5, of which waited for: 4 -> 2; matrix products, arithmetic and copies ran while one was open for 0% -> 0% of each run, Pallas kernels for 1% -> 5%
where the time goes in v4:
time: 61.8 us; the launch traced here: 61.5 us
  starting transfers between devices  26.6 us (43%)
  waiting for transfers between devices  25.2 us (41%)
  Pallas kernels  8.98 us (15%)
  between operations  0.77 us (1%)
    all_to_all x1, waiting for transfers between devices, shards(): lax.all_to_all(request, 'lat', split_axis=0, concat_axis=0, tiled=True)  18 us
    ppermute x1, starting transfers between devices, shards(): outer = lax.ppermute(outer, 'lon', outer_routes)  11.2 us
    all_to_all x1, starting transfers between devices, shards(): lax.all_to_all(request, 'lat', split_axis=0, concat_axis=0, tiled=True)  8.25 us
    ppermute x1, waiting for transfers between devices, shards(): far = lax.ppermute(far, ('lon', 'lat'), far_routes)  7.22 us
    pallas_call x6, Pallas kernels, call(): pl.pallas_call(kernel, out_shape=[jax.ShapeDtypeStruct(shape, dtype) for...  6.37 us
    ppermute x1, starting transfers between devices, shards(): far = lax.ppermute(far, ('lon', 'lat'), far_routes)  2.84 us
    pallas_call x1, Pallas kernels, shards(): pl.pallas_call(request_kernel, out_shape=jax.ShapeDtypeStruct((bands, ste...  2.61 us
    ppermute x1, starting transfers between devices, shards(): near = lax.ppermute(near, ('lon', 'lat'), near_routes)  2.34 us
  transfers between devices with their start and end apart: 5, of which 2 were waited for; matrix products, arithmetic and copies ran while one was open for 0% of the time, Pallas kernels for 5%

profile of v4, /device:TPU:22, one launch (start us, length us, event | category | flops | bytes accessed | tf_op | source)
XLA Modules:
  0.0 61.5 jit_solution(1498152978418834364)
XLA Ops:
  0.6 0.0 copy-start
  0.6 0.0 copy-start.1
  0.7 0.0 copy-start.2
  0.7 0.0 copy-start.4
  0.7 2.6 %shard_map.86 = bf16[8,2,152,128]{3,2,1,0:T(8,128)(2,1)} custom-call(s32[2,8,64]{2,1,0:T(8,128)} %slot_hbm.1, bf16[2432,128]{1,0:T(8,128)(2,1)} %bitcast.7), custom_call_target="tpu_custom_call" | custom-call | tf_op jit(solution)/shard_map/pallas_call | solution.py:642
  3.3 8.2 %all-to-all-start = ((bf16[8,2,152,128]{3,2,1,0:T(8,128)(2,1)}), bf16[8,2,152,128]{3,2,1,0:T(8,128)(2,1)S(1)}, u32[]{:S(2)}, u32[]{:S(2)}) async-start(bf16[8,2,152,128]{3,2,1,0:T(8,128)(2,1)} %shard_map.86), calls=%async_computation | async-start | bytes 1245184 | tf_op jit(solution)/shard_map/all_to_all | solution.py:661
  11.6 0.0 copy-done.1
  11.6 0.0 copy-done.2
  11.6 0.0 copy-done.4
  11.6 1.0 %shard_map.87 = (f32[608,128]{1,0:T(8,128)S(1)}, f32[608,128]{1,0:T(8,128)S(1)}, f32[312,128]{1,0:T(8,128)S(1)}, f32[32,256]{1,0:T(8,128)S(1)}, bf16[1024,128]{1,0:T(8,128)(2,1)S(1)}) custom-call(f32[8]{0:T(128)S(1)} %copy-done.4, f32[608,128]{1,0:T(8,128)S(1)} %bitcast.5, s32[8,128]{1,0:T(8,128)S(1)} %copy-done.2, s32[296,128]{1,0:T(8,128)S(1)} %bitcast.6), custom_call_target="tpu_custom_call" | custom-call | tf_op jit(solution)/shard_map/pallas_call | solution.py:621
  12.6 18.0 %all-to-all-done.piece_ref = bf16[8,2,152,128]{3,2,1,0:T(8,128)(2,1)S(1)} async-done(((bf16[8,2,152,128]{3,2,1,0:T(8,128)(2,1)}), bf16[8,2,152,128]{3,2,1,0:T(8,128)(2,1)S(1)}, u32[]{:S(2)}, u32[]{:S(2)}) %all-to-all-start) | async-done | bytes 622624 | tf_op jit(solution)/shard_map/all_to_all | solution.py:661
  30.6 1.1 %shard_map.88 = (bf16[8,768]{1,0:T(8,128)(2,1)S(1)}, bf16[8,768]{1,0:T(8,128)(2,1)S(1)}) custom-call(s32[2,8,64]{2,1,0:T(8,128)S(1)} %copy-done.3, bf16[8,2,152,128]{3,2,1,0:T(8,128)(2,1)S(1)} %all-to-all-done.piece_ref, f32[32,256]{1,0:T(8,128)S(1)} %get-tuple-element.22.side_ref, bf16[1024,128]{1,0:T(8,128)(2,1)S(1)} %get-tuple-element.23.pick_ref), custom_call_target="tpu_custom_call" | custom-call | tf_op jit(solution)/shard_map/pallas_call | solution.py:621
  31.7 11.2 %collective-permute-start = (bf16[8,768]{1,0:T(8,128)(2,1)S(1)}, bf16[8,768]{1,0:T(8,128)(2,1)S(1)}, u32[]{:S(2)}, u32[]{:S(2)}) collective-permute-start(bf16[8,768]{1,0:T(8,128)(2,1)S(1)} %get-tuple-element.24), channel_id=1, source_target_pairs={{8,16},{16,8},{24,32},{32,24},{40,48},{48,40},{56,64},{64,56},{72,... | collective-permute-start | bytes 36872 | tf_op jit(solution)/shard_map/ppermute | solution.py:688
  42.9 1.9 %collective-permute-start.1 = (bf16[8,768]{1,0:T(8,128)(2,1)S(1)}, bf16[8,768]{1,0:T(8,128)(2,1)S(1)}, u32[]{:S(2)}, u32[]{:S(2)}) collective-permute-start(bf16[8,768]{1,0:T(8,128)(2,1)S(1)} %get-tuple-element.25), channel_id=1, source_target_pairs={{0,8},{8,0},{16,24},{24,16},{32,40},{40,32},{48,56},{56,48},{64,72... | collective-permute-start | bytes 36872 | tf_op jit(solution)/shard_map/ppermute | solution.py:689
  44.8 1.2 %shard_map.89 = (f32[2432,128]{1,0:T(8,128)S(1)}, f32[432,128]{1,0:T(8,128)S(1)}, f32[432,128]{1,0:T(8,128)S(1)}) custom-call(s32[2,8,64]{2,1,0:T(8,128)S(1)} %copy-done.3, bf16[8,2,152,128]{3,2,1,0:T(8,128)(2,1)S(1)} %all-to-all-done.piece_ref, f32[608,128]{1,0:T(8,128)S(1)} %get-tuple-element.26.masked_ref, f32[608,128]{1,0:T(8,128)S(1)} %get-tuple-element.27.base_ref, ...), custom_call_target="tpu_custom_call" | custom-call | tf_op jit(solution)/shard_map/pallas_call | solution.py:621
  46.0 0.0 collective-permute-done.outer_ref
  46.0 0.0 collective-permute-done.1.inner_ref
  46.0 0.3 shard_map.90
  46.4 2.8 %collective-permute-start.2 = (bf16[432,128]{1,0:T(8,128)(2,1)S(1)}, bf16[432,128]{1,0:T(8,128)(2,1)S(1)}, u32[]{:S(2)}, u32[]{:S(2)}) collective-permute-start(bf16[432,128]{1,0:T(8,128)(2,1)S(1)} %get-tuple-element.30), channel_id=1, source_target_pairs={{1,2},{2,1},{3,4},{4,3},{5,6},{6,5},{7,511},{511,7},{9,10},{10,9},... | collective-permute-start | bytes 331784 | tf_op jit(solution)/shard_map/ppermute | solution.py:714
  49.2 2.3 %collective-permute-start.3 = (bf16[432,128]{1,0:T(8,128)(2,1)S(1)}, bf16[432,128]{1,0:T(8,128)(2,1)S(1)}, u32[]{:S(2)}, u32[]{:S(2)}) collective-permute-start(bf16[432,128]{1,0:T(8,128)(2,1)S(1)} %get-tuple-element.31), channel_id=1, source_target_pairs={{0,1},{1,0},{2,3},{3,2},{4,5},{5,4},{6,7},{7,6},{8,9},{9,8},{10,11... | collective-permute-start | bytes 331784 | tf_op jit(solution)/shard_map/ppermute | solution.py:715
  51.6 0.9 %shard_map.91 = (f32[608,128]{1,0:T(8,128)S(1)}, f32[608,128]{1,0:T(8,128)S(1)}, f32[608,128]{1,0:T(8,128)S(1)}) custom-call(bf16[8,768]{1,0:T(8,128)(2,1)S(1)} %get-tuple-element.33.west_ref, bf16[8,768]{1,0:T(8,128)(2,1)S(1)} %get-tuple-element.34.east_ref, f32[2432,128]{1,0:T(8,128)S(1)} %get-tuple-element.35.state_ref, ...), custom_call_target="tpu_custom_call" | custom-call | tf_op jit(solution)/shard_map/pallas_call | solution.py:621
  52.5 7.2 %collective-permute-done.2.far_ref = bf16[432,128]{1,0:T(8,128)(2,1)S(1)} collective-permute-done((bf16[432,128]{1,0:T(8,128)(2,1)S(1)}, bf16[432,128]{1,0:T(8,128)(2,1)S(1)}, u32[]{:S(2)}, u32[]{:S(2)}) %collective-permute-start.2) | collective-permute-done | bytes 110624 | tf_op jit(solution)/shard_map/ppermute | solution.py:714
  59.7 0.0 collective-permute-done.3.near_ref
  59.7 1.8 %shard_map.92 = (f32[608,128]{1,0:T(8,128)}, f32[608,128]{1,0:T(8,128)}) custom-call(bf16[432,128]{1,0:T(8,128)(2,1)S(1)} %collective-permute-done.2.far_ref, bf16[432,128]{1,0:T(8,128)(2,1)S(1)} %collective-permute-done.3.near_ref, f32[76,128]{1,0:T(8,128)S(1)} %get-tuple-element.32.pack_ref, bf16[8,768]{1,0:T(8,128)(2,1)S(1)} %get-tuple-element.33.west_ref, ...), custom_call_target="tpu_custom_call" | custom-call | tf_op jit(solution)/shard_map/pallas_call | solution.py:621
  (3 shorter events, 0.0 us)
Async XLA Ops:
  0.6 10.9 %copy-start = (f32[2,38,8,128]{3,2,1,0:T(8,128)S(1)}, f32[2,38,8,128]{3,2,1,0:T(8,128)}, u32[]{:S(2)}) copy-start(f32[2,38,8,128]{3,2,1,0:T(8,128)} %param.7) | copy-start | bytes 933892
  0.6 10.9 %copy-start.1 = (s32[37,8,128]{2,1,0:T(8,128)S(1)}, s32[37,8,128]{2,1,0:T(8,128)}, u32[]{:S(2)}) copy-start(s32[37,8,128]{2,1,0:T(8,128)} %param.12) | copy-start | bytes 454660
  0.7 10.9 %copy-start.2 = (s32[8,128]{1,0:T(8,128)S(1)}, s32[8,128]{1,0:T(8,128)}, u32[]{:S(2)}) copy-start(s32[8,128]{1,0:T(8,128)} %bottom_ref.7) | copy-start | bytes 12292
  0.7 10.9 %copy-start.4 = (f32[8]{0:T(128)S(1)}, f32[8]{0:T(128)}, u32[]{:S(2)}) copy-start(f32[8]{0:T(128)} %table_ref.1) | copy-start | bytes 100
  0.7 29.9 %copy-start.3 = (s32[2,8,64]{2,1,0:T(8,128)S(1)}, s32[2,8,64]{2,1,0:T(8,128)}, u32[]{:S(2)}) copy-start(s32[2,8,64]{2,1,0:T(8,128)} %offset_ref.3) | copy-start | bytes 12292
  3.3 27.3 %all-to-all-start = ((bf16[8,2,152,128]{3,2,1,0:T(8,128)(2,1)}), bf16[8,2,152,128]{3,2,1,0:T(8,128)(2,1)S(1)}, u32[]{:S(2)}, u32[]{:S(2)}) async-start(bf16[8,2,152,128]{3,2,1,0:T(8,128)(2,1)} %shard_map.86), calls=%async_computation | async-start | bytes 1245184 | tf_op jit(solution)/shard_map/all_to_all | solution.py:661
  31.7 14.3 %collective-permute-start = (bf16[8,768]{1,0:T(8,128)(2,1)S(1)}, bf16[8,768]{1,0:T(8,128)(2,1)S(1)}, u32[]{:S(2)}, u32[]{:S(2)}) collective-permute-start(bf16[8,768]{1,0:T(8,128)(2,1)S(1)} %get-tuple-element.24), channel_id=1, source_target_pairs={{8,16},{16,8},{24,32},{32,24},{40,48},{48,40},{56,64},{64,56},{72,... | collective-permute-start | bytes 36872 | tf_op jit(solution)/shard_map/ppermute | solution.py:688
  42.9 3.1 %collective-permute-start.1 = (bf16[8,768]{1,0:T(8,128)(2,1)S(1)}, bf16[8,768]{1,0:T(8,128)(2,1)S(1)}, u32[]{:S(2)}, u32[]{:S(2)}) collective-permute-start(bf16[8,768]{1,0:T(8,128)(2,1)S(1)} %get-tuple-element.25), channel_id=1, source_target_pairs={{0,8},{8,0},{16,24},{24,16},{32,40},{40,32},{48,56},{56,48},{64,72... | collective-permute-start | bytes 36872 | tf_op jit(solution)/shard_map/ppermute | solution.py:689
  46.4 13.4 %collective-permute-start.2 = (bf16[432,128]{1,0:T(8,128)(2,1)S(1)}, bf16[432,128]{1,0:T(8,128)(2,1)S(1)}, u32[]{:S(2)}, u32[]{:S(2)}) collective-permute-start(bf16[432,128]{1,0:T(8,128)(2,1)S(1)} %get-tuple-element.30), channel_id=1, source_target_pairs={{1,2},{2,1},{3,4},{4,3},{5,6},{6,5},{7,511},{511,7},{9,10},{10,9},... | collective-permute-start | bytes 331784 | tf_op jit(solution)/shard_map/ppermute | solution.py:714
  49.2 10.5 %collective-permute-start.3 = (bf16[432,128]{1,0:T(8,128)(2,1)S(1)}, bf16[432,128]{1,0:T(8,128)(2,1)S(1)}, u32[]{:S(2)}, u32[]{:S(2)}) collective-permute-start(bf16[432,128]{1,0:T(8,128)(2,1)S(1)} %get-tuple-element.31), channel_id=1, source_target_pairs={{0,1},{1,0},{2,3},{3,2},{4,5},{5,4},{6,7},{7,6},{8,9},{9,8},{10,11... | collective-permute-start | bytes 331784 | tf_op jit(solution)/shard_map/ppermute | solution.py:715

commit v5 on v4

--- a/solution.py
+++ b/solution.py
@@ -196,35 +196,48 @@
         outer_ref[...] = to_east
 
 
+def tiles_kernel(offset_ref, piece_ref, west_ref, state_ref):
+    tile = lax.axis_index("lon")
+    band = lax.axis_index("lat")
+    holders, _, pieces, _ = piece_ref.shape
+    for at, step in enumerate(STEP_ORDER):
+        offset = offset_ref[step, band, tile]
+        for row in range(ROWS):
+            chunk = piece_ref[lax.rem(row + offset, holders), at]
+            state_ref[pl.ds(at * pieces * ROWS + row, pieces, stride=ROWS), :] = chunk.astype(
+                jnp.float32
+            )
+
+
 def drafts_kernel(
-    offset_ref, piece_ref, masked_ref, base_ref, bottom_ref, state_ref, top_ref, bot_ref
+    offset_ref, piece_ref, masked_ref, base_ref, bottom_ref, top_ref, bot_ref, line_ref
 ):
     tile = lax.axis_index("lon")
     band = lax.axis_index("lat")
     levels = masked_ref.shape[0] // (2 * ROWS)
     pieces = FIELDS * levels
     holders = piece_ref.shape[0]
-    for at, step in enumerate(STEP_ORDER):
-        offset = offset_ref[step, band, tile]
-        for row in range(ROWS):
-            chunk = piece_ref[lax.rem(row + offset, holders), at]
-            state_ref[pl.ds(at * pieces * ROWS + row, pieces, stride=ROWS), :] = chunk.astype(
-                jnp.float32
-            )
+    for slot, (row, at) in enumerate(((ROWS - 1, 0), (ROWS - 1, 1), (0, 0), (0, 1), (ROWS - 2, 0))):
+        offset = offset_ref[STEP_ORDER[at], band, tile]
+        chunk = piece_ref[lax.rem(row + offset, holders), at]
+        line_ref[slot * pieces : (slot + 1) * pieces] = chunk.astype(jnp.float32)
     bottom = bottom_ref[...].astype(jnp.float32)
     layout = Layout(levels)
     wide = lanes_of((levels, LANES))
-    for row, inner, draft_ref in ((ROWS - 1, ROWS - 2, top_ref), (0, 1, bot_ref)):
+    for row, inner, first, facing, draft_ref in (
+        (ROWS - 1, ROWS - 2, 0, 4, top_ref),
+        (0, 1, 2, 2, bot_ref),
+    ):
         for at in range(2):
-            begin = at * pieces * ROWS
-            draft_ref[layout.tracer[at] : layout.tracer[at] + 2 * levels] = strided(
-                state_ref, begin + row, 2 * levels
-            )
-            draft_ref[layout.merid[at] : layout.merid[at] + levels] = strided(
-                state_ref, begin + 3 * levels * ROWS + row, levels
-            )
-        zonal = strided(state_ref, 2 * levels * ROWS + row, levels)
-        merid = strided(state_ref, 3 * levels * ROWS + min(row, inner), levels)
+            begin = (first + at) * pieces
+            draft_ref[layout.tracer[at] : layout.tracer[at] + 2 * levels] = line_ref[
+                begin : begin + 2 * levels
+            ]
+            draft_ref[layout.merid[at] : layout.merid[at] + levels] = line_ref[
+                begin + 3 * levels : begin + 4 * levels
+            ]
+        zonal = line_ref[first * pieces + 2 * levels : first * pieces + 3 * levels]
+        merid = line_ref[facing * pieces + 3 * levels : facing * pieces + 4 * levels]
         east_factor = ADVECT_HALF * zonal + DIFFUSE
         west_factor = ADVECT_HALF * shift(zonal, 1, 1) - DIFFUSE
         for tracer in range(2):
@@ -450,11 +463,12 @@
     velocity_in_ref,
     adjoint_ref,
     velocity_ref,
+    next_ref,
+    side_ref,
     north_ref,
     south_ref,
-    next_ref,
-    side_ref,
     ring_ref,
+    total_ref,
 ):
     levels = masked_ref.shape[0] // (2 * ROWS)
     layout = Layout(levels)
@@ -478,9 +492,6 @@
         north_ref[...] = jnp.dot(near_ref[...], turn, preferred_element_type=jnp.float32)
         south_ref[...] = far_ref[...].astype(jnp.float32)
 
-    next_ref[...] = next_in_ref[...]
-    side_ref[...] = side_in_ref[...]
-    velocity_ref[...] = velocity_in_ref[...]
     for at in range(2):
         here = slice(layout.merid[at], layout.merid[at] + levels)
         north_ref[here] = north_ref[here] * folded
@@ -547,7 +558,7 @@
         add_rows(side_ref, start + top, jnp.where(level_of < side_depth(top), face, 0.0))
         face = side_bottom_factor * (own_bottom[tracer] - south_corner[tracer])
         add_rows(side_ref, start, jnp.where(level_of < side_depth(0), face, 0.0))
-    add_rows(velocity_ref, levels * ROWS + top, ADVECT_HALF * merid_total)
+    total_ref[...] = merid_total
 
     tile = Tile(levels, west_ref, east_ref, state_ref)
     first_lane, last_lane = tile.first_lane, tile.last_lane
@@ -589,9 +600,10 @@
             )
             zonal_total = zonal_total + (field + field_east) * to_east
             merid_total = merid_total + (field + field_north) * to_north
+        merid_total = merid_total + jnp.where(top_row, tile.line(total_ref, level), 0.0)
         for total, begin in ((zonal_total, 0), (merid_total, levels)):
             here = slice((begin + level) * ROWS, (begin + level + 1) * ROWS)
-            velocity_ref[here] = velocity_ref[here] + ADVECT_HALF * total
+            velocity_ref[here] = velocity_in_ref[here] + ADVECT_HALF * total
 
 
 def swaps(pairs):
@@ -615,7 +627,7 @@
     return swaps(near), swaps(far)
 
 
-def call(kernel, outputs, scratch, scalars, arrays):
+def call(kernel, outputs, scratch, scalars, arrays, aliases=None):
     vmem = pl.BlockSpec(memory_space=pltpu.VMEM)
     smem = pl.BlockSpec(memory_space=pltpu.SMEM)
     return pl.pallas_call(
@@ -624,6 +636,7 @@
         in_specs=[smem] * len(scalars) + [vmem] * len(arrays),
         out_specs=[vmem] * len(outputs),
         scratch_shapes=[pltpu.VMEM(shape, jnp.float32) for shape in scratch],
+        input_output_aliases=aliases or {},
         compiler_params=pltpu.CompilerParams(vmem_limit_bytes=32 * 1024 * 1024),
     )(*scalars, *arrays)
 
@@ -687,14 +700,10 @@
     near_routes, far_routes = line_routes(tiles, bands)
     outer = lax.ppermute(outer, "lon", outer_routes)
     inner = lax.ppermute(inner, "lon", inner_routes)
-    state, top, bot = call(
+    top, bot = call(
         drafts_kernel,
-        [
-            ((steps * FIELDS * full, LANES), wide),
-            ((layout.rows, LANES), wide),
-            ((layout.rows, LANES), wide),
-        ],
-        [],
+        [((layout.rows, LANES), wide), ((layout.rows, LANES), wide)],
+        [(5 * pieces, LANES)],
         [holder_offset],
         [received, masked, base, bottom_level],
     )
@@ -713,6 +722,13 @@
     )
     far = lax.ppermute(far, ("lon", "lat"), far_routes)
     near = lax.ppermute(near, ("lon", "lat"), near_routes)
+    (state,) = call(
+        tiles_kernel,
+        [((steps * FIELDS * full, LANES), wide)],
+        [],
+        [holder_offset],
+        [received, west],
+    )
     following, beside, velocity = call(
         first_step_kernel,
         [((2 * full, LANES), wide)] * 3,
@@ -720,15 +736,14 @@
         [],
         [west, east, state, masked, base, bottom_level],
     )
-    adjoint, velocity = call(
+    adjoint, velocity, _, _ = call(
         second_step_kernel,
-        [((2 * full, LANES), wide)] * 2,
+        [((2 * full, LANES), wide)] * 4,
         [
             (layout.rows, LANES),
             (layout.rows, LANES),
-            (2 * full, LANES),
-            (2 * full, LANES),
             (4 * levels, LANES),
+            (levels, LANES),
         ],
         [],
         [
@@ -745,6 +760,7 @@
             beside,
             velocity,
         ],
+        {9: 2, 10: 3},
     )
     shape = (2, levels, ROWS, LANES)
     return adjoint.reshape(shape), velocity.reshape(shape)

time: 61.8 us -> 61.5 us (level)
  waiting for transfers between devices: 25.2 us -> 24.2 us
  Pallas kernels: 8.98 us -> 9.63 us
    ppermute x1, waiting for transfers between devices: 7.22 us -> 5.92 us  [shards(): far = lax.ppermute(far, ('lon', 'lat'), far_routes)]
    pallas_call x6 -> x7, Pallas kernels: 6.37 us -> 7.02 us  [call(): pl.pallas_call(kernel, out_shape=[jax.ShapeDtypeStruct(shape, dtype) for...]
  transfers between devices with their start and end apart: 5 -> 5, of which waited for: 2 -> 3; matrix products, arithmetic and copies ran while one was open for 0% -> 0% of each run, Pallas kernels for 5% -> 6%
where the time goes in v5:
time: 61.5 us; the launch traced here: 61.2 us
  starting transfers between devices  26.6 us (43%)
  waiting for transfers between devices  24.2 us (39%)
  Pallas kernels  9.63 us (16%)
  between operations  0.77 us (1%)
    all_to_all x1, waiting for transfers between devices, shards(): lax.all_to_all(request, 'lat', split_axis=0, concat_axis=0, tiled=True)  18 us
    ppermute x1, starting transfers between devices, shards(): outer = lax.ppermute(outer, 'lon', outer_routes)  11.2 us
    all_to_all x1, starting transfers between devices, shards(): lax.all_to_all(request, 'lat', split_axis=0, concat_axis=0, tiled=True)  8.25 us
    pallas_call x7, Pallas kernels, call(): pl.pallas_call(kernel, out_shape=[jax.ShapeDtypeStruct(shape, dtype) for...  7.02 us
    ppermute x1, waiting for transfers between devices, shards(): far = lax.ppermute(far, ('lon', 'lat'), far_routes)  5.92 us
    ppermute x1, starting transfers between devices, shards(): far = lax.ppermute(far, ('lon', 'lat'), far_routes)  2.84 us
    pallas_call x1, Pallas kernels, shards(): pl.pallas_call(request_kernel, out_shape=jax.ShapeDtypeStruct((bands, ste...  2.61 us
    ppermute x1, starting transfers between devices, shards(): near = lax.ppermute(near, ('lon', 'lat'), near_routes)  2.34 us
  transfers between devices with their start and end apart: 5, of which 3 were waited for; matrix products, arithmetic and copies ran while one was open for 0% of the time, Pallas kernels for 6%

profile of v5, /device:TPU:22, one launch (start us, length us, event | category | flops | bytes accessed | tf_op | source)
XLA Modules:
  0.0 61.2 jit_solution(2857016879359769067)
XLA Ops:
  0.6 0.0 copy-start
  0.6 0.0 copy-start.1
  0.7 0.0 copy-start.3
  0.7 0.0 copy-start.4
  0.7 0.0 copy-start.2
  0.7 2.6 %shard_map.86 = bf16[8,2,152,128]{3,2,1,0:T(8,128)(2,1)} custom-call(s32[2,8,64]{2,1,0:T(8,128)} %slot_hbm.1, bf16[2432,128]{1,0:T(8,128)(2,1)} %bitcast.7), custom_call_target="tpu_custom_call" | custom-call | tf_op jit(solution)/shard_map/pallas_call | solution.py:655
  3.3 8.2 %all-to-all-start = ((bf16[8,2,152,128]{3,2,1,0:T(8,128)(2,1)}), bf16[8,2,152,128]{3,2,1,0:T(8,128)(2,1)S(1)}, u32[]{:S(2)}, u32[]{:S(2)}) async-start(bf16[8,2,152,128]{3,2,1,0:T(8,128)(2,1)} %shard_map.86), calls=%async_computation | async-start | bytes 1245184 | tf_op jit(solution)/shard_map/all_to_all | solution.py:674
  11.5 0.0 copy-done
  11.6 1.0 %shard_map.87 = (f32[608,128]{1,0:T(8,128)S(1)}, f32[608,128]{1,0:T(8,128)S(1)}, f32[312,128]{1,0:T(8,128)S(1)}, f32[32,256]{1,0:T(8,128)S(1)}, bf16[1024,128]{1,0:T(8,128)(2,1)S(1)}) custom-call(f32[8]{0:T(128)S(1)} %copy-done.4, f32[608,128]{1,0:T(8,128)S(1)} %bitcast.5, s32[8,128]{1,0:T(8,128)S(1)} %copy-done.3, s32[296,128]{1,0:T(8,128)S(1)} %bitcast.6), custom_call_target="tpu_custom_call" | custom-call | tf_op jit(solution)/shard_map/pallas_call | solution.py:633
  12.6 18.0 %all-to-all-done.piece_ref = bf16[8,2,152,128]{3,2,1,0:T(8,128)(2,1)S(1)} async-done(((bf16[8,2,152,128]{3,2,1,0:T(8,128)(2,1)}), bf16[8,2,152,128]{3,2,1,0:T(8,128)(2,1)S(1)}, u32[]{:S(2)}, u32[]{:S(2)}) %all-to-all-start) | async-done | bytes 622624 | tf_op jit(solution)/shard_map/all_to_all | solution.py:674
  30.6 1.1 %shard_map.88 = (bf16[8,768]{1,0:T(8,128)(2,1)S(1)}, bf16[8,768]{1,0:T(8,128)(2,1)S(1)}) custom-call(s32[2,8,64]{2,1,0:T(8,128)S(1)} %copy-done.2, bf16[8,2,152,128]{3,2,1,0:T(8,128)(2,1)S(1)} %all-to-all-done.piece_ref, f32[32,256]{1,0:T(8,128)S(1)} %get-tuple-element.21.side_ref, bf16[1024,128]{1,0:T(8,128)(2,1)S(1)} %get-tuple-element.22.pick_ref), custom_call_target="tpu_custom_call" | custom-call | tf_op jit(solution)/shard_map/pallas_call | solution.py:633
  31.7 11.2 %collective-permute-start = (bf16[8,768]{1,0:T(8,128)(2,1)S(1)}, bf16[8,768]{1,0:T(8,128)(2,1)S(1)}, u32[]{:S(2)}, u32[]{:S(2)}) collective-permute-start(bf16[8,768]{1,0:T(8,128)(2,1)S(1)} %get-tuple-element.23), channel_id=1, source_target_pairs={{8,16},{16,8},{24,32},{32,24},{40,48},{48,40},{56,64},{64,56},{72,... | collective-permute-start | bytes 36872 | tf_op jit(solution)/shard_map/ppermute | solution.py:701
  42.9 1.9 %collective-permute-start.1 = (bf16[8,768]{1,0:T(8,128)(2,1)S(1)}, bf16[8,768]{1,0:T(8,128)(2,1)S(1)}, u32[]{:S(2)}, u32[]{:S(2)}) collective-permute-start(bf16[8,768]{1,0:T(8,128)(2,1)S(1)} %get-tuple-element.24), channel_id=1, source_target_pairs={{0,8},{8,0},{16,24},{24,16},{32,40},{40,32},{48,56},{56,48},{64,72... | collective-permute-start | bytes 36872 | tf_op jit(solution)/shard_map/ppermute | solution.py:702
  44.8 0.8 %shard_map.89 = (f32[432,128]{1,0:T(8,128)S(1)}, f32[432,128]{1,0:T(8,128)S(1)}) custom-call(s32[2,8,64]{2,1,0:T(8,128)S(1)} %copy-done.2, bf16[8,2,152,128]{3,2,1,0:T(8,128)(2,1)S(1)} %all-to-all-done.piece_ref, f32[608,128]{1,0:T(8,128)S(1)} %get-tuple-element.25.masked_ref, f32[608,128]{1,0:T(8,128)S(1)} %get-tuple-element.26.base_ref, s32[8,128]{1,0:T(8,128)S(1)} %copy-done.3), custom_call_target="tpu_custom_call" | custom-call | tf_op jit(solution)/shard_map/pallas_call | solution.py:633
  45.7 0.0 collective-permute-done.outer_ref
  45.7 0.3 collective-permute-done.1.inner_ref
  46.0 0.3 shard_map.90
  46.3 2.8 %collective-permute-start.2 = (bf16[432,128]{1,0:T(8,128)(2,1)S(1)}, bf16[432,128]{1,0:T(8,128)(2,1)S(1)}, u32[]{:S(2)}, u32[]{:S(2)}) collective-permute-start(bf16[432,128]{1,0:T(8,128)(2,1)S(1)} %get-tuple-element.29), channel_id=1, source_target_pairs={{1,2},{2,1},{3,4},{4,3},{5,6},{6,5},{7,511},{511,7},{9,10},{10,9},... | collective-permute-start | bytes 331784 | tf_op jit(solution)/shard_map/ppermute | solution.py:723
  49.2 2.3 %collective-permute-start.3 = (bf16[432,128]{1,0:T(8,128)(2,1)S(1)}, bf16[432,128]{1,0:T(8,128)(2,1)S(1)}, u32[]{:S(2)}, u32[]{:S(2)}) collective-permute-start(bf16[432,128]{1,0:T(8,128)(2,1)S(1)} %get-tuple-element.30), channel_id=1, source_target_pairs={{0,1},{1,0},{2,3},{3,2},{4,5},{5,4},{6,7},{7,6},{8,9},{9,8},{10,11... | collective-permute-start | bytes 331784 | tf_op jit(solution)/shard_map/ppermute | solution.py:724
  51.5 1.0 %shard_map.91.state_ref = f32[2432,128]{1,0:T(8,128)S(1)} custom-call(s32[2,8,64]{2,1,0:T(8,128)S(1)} %copy-done.2, bf16[8,2,152,128]{3,2,1,0:T(8,128)(2,1)S(1)} %all-to-all-done.piece_ref, bf16[8,768]{1,0:T(8,128)(2,1)S(1)} %get-tuple-element.32.west_ref), custom_call_target="tpu_custom_call" | custom-call | tf_op jit(solution)/shard_map/pallas_call | solution.py:633
  52.5 1.0 %shard_map.92 = (f32[608,128]{1,0:T(8,128)S(1)}, f32[608,128]{1,0:T(8,128)S(1)}, f32[608,128]{1,0:T(8,128)S(1)}) custom-call(bf16[8,768]{1,0:T(8,128)(2,1)S(1)} %get-tuple-element.32.west_ref, bf16[8,768]{1,0:T(8,128)(2,1)S(1)} %get-tuple-element.33.east_ref, f32[2432,128]{1,0:T(8,128)S(1)} %shard_map.91.state_ref, ...), custom_call_target="tpu_custom_call" | custom-call | tf_op jit(solution)/shard_map/pallas_call | solution.py:633
  53.5 5.9 %collective-permute-done.2.far_ref = bf16[432,128]{1,0:T(8,128)(2,1)S(1)} collective-permute-done((bf16[432,128]{1,0:T(8,128)(2,1)S(1)}, bf16[432,128]{1,0:T(8,128)(2,1)S(1)}, u32[]{:S(2)}, u32[]{:S(2)}) %collective-permute-start.2) | collective-permute-done | bytes 110624 | tf_op jit(solution)/shard_map/ppermute | solution.py:723
  59.4 0.0 collective-permute-done.3.near_ref
  59.4 1.8 %shard_map.93 = (f32[608,128]{1,0:T(8,128)}, f32[608,128]{1,0:T(8,128)}, f32[608,128]{1,0:T(8,128)S(1)}, f32[608,128]{1,0:T(8,128)S(1)}) custom-call(bf16[432,128]{1,0:T(8,128)(2,1)S(1)} %collective-permute-done.2.far_ref, bf16[432,128]{1,0:T(8,128)(2,1)S(1)} %collective-permute-done.3.near_ref, ...), custom_call_target="tpu_custom_call", output_to_operand_aliasing={{2}: (9, {}), {3}: (10, {})} | custom-call | tf_op jit(solution)/shard_map/pallas_call | solution.py:633
  (4 shorter events, 0.0 us)
Async XLA Ops:
  0.6 10.9 %copy-start = (f32[2,38,8,128]{3,2,1,0:T(8,128)S(1)}, f32[2,38,8,128]{3,2,1,0:T(8,128)}, u32[]{:S(2)}) copy-start(f32[2,38,8,128]{3,2,1,0:T(8,128)} %param.7) | copy-start | bytes 933892
  0.6 10.9 %copy-start.1 = (s32[37,8,128]{2,1,0:T(8,128)S(1)}, s32[37,8,128]{2,1,0:T(8,128)}, u32[]{:S(2)}) copy-start(s32[37,8,128]{2,1,0:T(8,128)} %param.12) | copy-start | bytes 454660
  0.7 10.9 %copy-start.3 = (s32[8,128]{1,0:T(8,128)S(1)}, s32[8,128]{1,0:T(8,128)}, u32[]{:S(2)}) copy-start(s32[8,128]{1,0:T(8,128)} %bottom_ref.7) | copy-start | bytes 12292
  0.7 10.9 %copy-start.4 = (f32[8]{0:T(128)S(1)}, f32[8]{0:T(128)}, u32[]{:S(2)}) copy-start(f32[8]{0:T(128)} %table_ref.1) | copy-start | bytes 100
  0.7 29.9 %copy-start.2 = (s32[2,8,64]{2,1,0:T(8,128)S(1)}, s32[2,8,64]{2,1,0:T(8,128)}, u32[]{:S(2)}) copy-start(s32[2,8,64]{2,1,0:T(8,128)} %offset_ref.5) | copy-start | bytes 12292
  3.3 27.3 %all-to-all-start = ((bf16[8,2,152,128]{3,2,1,0:T(8,128)(2,1)}), bf16[8,2,152,128]{3,2,1,0:T(8,128)(2,1)S(1)}, u32[]{:S(2)}, u32[]{:S(2)}) async-start(bf16[8,2,152,128]{3,2,1,0:T(8,128)(2,1)} %shard_map.86), calls=%async_computation | async-start | bytes 1245184 | tf_op jit(solution)/shard_map/all_to_all | solution.py:674
  31.7 14.0 %collective-permute-start = (bf16[8,768]{1,0:T(8,128)(2,1)S(1)}, bf16[8,768]{1,0:T(8,128)(2,1)S(1)}, u32[]{:S(2)}, u32[]{:S(2)}) collective-permute-start(bf16[8,768]{1,0:T(8,128)(2,1)S(1)} %get-tuple-element.23), channel_id=1, source_target_pairs={{8,16},{16,8},{24,32},{32,24},{40,48},{48,40},{56,64},{64,56},{72,... | collective-permute-start | bytes 36872 | tf_op jit(solution)/shard_map/ppermute | solution.py:701
  42.9 3.1 %collective-permute-start.1 = (bf16[8,768]{1,0:T(8,128)(2,1)S(1)}, bf16[8,768]{1,0:T(8,128)(2,1)S(1)}, u32[]{:S(2)}, u32[]{:S(2)}) collective-permute-start(bf16[8,768]{1,0:T(8,128)(2,1)S(1)} %get-tuple-element.24), channel_id=1, source_target_pairs={{0,8},{8,0},{16,24},{24,16},{32,40},{40,32},{48,56},{56,48},{64,72... | collective-permute-start | bytes 36872 | tf_op jit(solution)/shard_map/ppermute | solution.py:702
  46.3 13.1 %collective-permute-start.2 = (bf16[432,128]{1,0:T(8,128)(2,1)S(1)}, bf16[432,128]{1,0:T(8,128)(2,1)S(1)}, u32[]{:S(2)}, u32[]{:S(2)}) collective-permute-start(bf16[432,128]{1,0:T(8,128)(2,1)S(1)} %get-tuple-element.29), channel_id=1, source_target_pairs={{1,2},{2,1},{3,4},{4,3},{5,6},{6,5},{7,511},{511,7},{9,10},{10,9},... | collective-permute-start | bytes 331784 | tf_op jit(solution)/shard_map/ppermute | solution.py:723
  49.2 10.2 %collective-permute-start.3 = (bf16[432,128]{1,0:T(8,128)(2,1)S(1)}, bf16[432,128]{1,0:T(8,128)(2,1)S(1)}, u32[]{:S(2)}, u32[]{:S(2)}) collective-permute-start(bf16[432,128]{1,0:T(8,128)(2,1)S(1)} %get-tuple-element.30), channel_id=1, source_target_pairs={{0,1},{1,0},{2,3},{3,2},{4,5},{5,4},{6,7},{7,6},{8,9},{9,8},{10,11... | collective-permute-start | bytes 331784 | tf_op jit(solution)/shard_map/ppermute | solution.py:724

commit v6 on v5

--- a/solution.py
+++ b/solution.py
@@ -81,10 +81,10 @@
         store.wait()
 
 
-def pick_columns():
+def pick_columns(offset=0):
     place = (ROWS * LANES, LANES)
     row, source = rows_of(place) // LANES, rows_of(place) % LANES
-    order = lanes_of(place) - row
+    order = lanes_of(place) - (row + ROWS - offset) % ROWS
     chosen = (
         ((source == 0) & (order == 0))
         | ((source == LANES - 1) & (order == ROWS))
@@ -96,6 +96,7 @@
 
 def prepare_kernel(
     table_ref,
+    offset_ref,
     adjoint_ref,
     bottom_ref,
     mix_ref,
@@ -127,7 +128,8 @@
                 masked_ref, kappa_ref, start, level, levels
             )
     pick = pick_columns()
-    pick_ref[...] = pick
+    for at, step in enumerate(STEP_ORDER):
+        pick_ref[at] = pick_columns(offset_ref[step, lax.axis_index("lat"), lax.axis_index("lon")])
     column_ref[...] = jnp.zeros_like(column_ref)
     rows = 2 * levels
     for start, ref in ((0, masked_ref), (LANES, base_ref)):
@@ -155,19 +157,15 @@
     return masked + kappa_below * (below - masked) + kappa_above * (above - masked)
 
 
-def edges_kernel(
-    offset_ref, piece_ref, side_ref, pick_ref, outer_ref, inner_ref, column_ref
-):
+def edges_kernel(piece_ref, side_ref, pick_ref, outer_ref, inner_ref, column_ref):
     tile = lax.axis_index("lon")
-    band = lax.axis_index("lat")
-    holders, _, pieces, _ = piece_ref.shape
+    holders, steps, pieces, _ = piece_ref.shape
     levels = pieces // FIELDS
     column_ref[...] = jnp.zeros_like(column_ref)
-    for at, step in enumerate(STEP_ORDER):
-        offset = offset_ref[step, band, tile]
-        chunks = [piece_ref[lax.rem(row + offset, holders), at] for row in range(ROWS)]
+    for at in range(steps):
+        chunks = [piece_ref[holder, at] for holder in range(holders)]
         column_ref[EDGE_STATE[at] : EDGE_STATE[at] + pieces] = jnp.dot(
-            jnp.concatenate(chunks, axis=1), pick_ref[...], preferred_element_type=jnp.float32
+            jnp.concatenate(chunks, axis=1), pick_ref[at], preferred_element_type=jnp.float32
         )
     state = jnp.transpose(column_ref[...])
     lane = lanes_of((ROWS, 2 * LANES))
@@ -323,8 +321,16 @@
             corner = jnp.where(lane == (0, LANES // 2)[tracer], west, corner)
             corner = jnp.where(lane == (LANES - 1, LANES // 2 - 1)[tracer], east, corner)
         draft_ref[layout.corner : layout.corner + levels] = corner
-        begin = 0 if row else levels
+        begin = 0 if row else 4 * levels
         pack_ref[begin : begin + levels] = corner
+        zonal_west, _ = pair(EDGE_STATE[1] + 2 * levels, row)
+        pack_ref[begin + levels : begin + 2 * levels] = jnp.broadcast_to(
+            zonal_west, (levels, LANES)
+        )
+        for tracer in range(2):
+            _, east = pair(EDGE_STATE[1] + tracer * levels, row)
+            here = begin + (2 + tracer) * levels
+            pack_ref[here : here + levels] = jnp.broadcast_to(east, (levels, LANES))
 
     @pl.when(odd_band)
     def _():
@@ -382,16 +388,18 @@
     return ref[index * ROWS : (index + 1) * ROWS]
 
 
-def first_step_kernel(
+def steps_kernel(
     west_ref,
     east_ref,
     state_ref,
     masked_ref,
     base_ref,
+    kappa_ref,
     bottom_ref,
+    adjoint_ref,
+    velocity_ref,
     next_ref,
     side_ref,
-    velocity_ref,
 ):
     levels = masked_ref.shape[0] // (2 * ROWS)
     tile = Tile(levels, west_ref, east_ref, state_ref)
@@ -447,8 +455,36 @@
             ADVECT_HALF * merid_total
         )
 
-
-def second_step_kernel(
+    for level in range(levels):
+        zonal, zonal_west, merid = tile.velocities(1, level)
+        north_factor = ADVECT_HALF * merid + DIFFUSE
+        south_factor = ADVECT_HALF * shift(merid, 1, 0) - DIFFUSE
+        zonal_total = jnp.zeros(tile.shape, jnp.float32)
+        merid_total = jnp.zeros(tile.shape, jnp.float32)
+        for tracer in range(2):
+            index = tracer * levels + level
+            masked = tile_of(next_ref, index)
+            side = tile_of(side_ref, index)
+            to_east = jnp.where(last_lane, side, shift(masked, -1, 1)) - masked
+            to_west = masked - jnp.where(first_lane, side, shift(masked, 1, 1))
+            to_north = jnp.where(top_row, 0.0, shift(masked, -1, 0) - masked)
+            to_south = jnp.where(bottom_row, 0.0, masked - shift(masked, 1, 0))
+            adjoint_ref[index * ROWS : (index + 1) * ROWS] = (
+                mixed(next_ref, kappa_ref, tracer * levels * ROWS, level, levels)
+                + (zonal + DIFFUSE) * to_east
+                + (zonal_west - DIFFUSE) * to_west
+                + north_factor * to_north
+                + south_factor * to_south
+            )
+            field, field_east = tile.tracer(1, level, tracer)
+            zonal_total = zonal_total + (field + field_east) * to_east
+            merid_total = merid_total + (field + shift(field, -1, 0)) * to_north
+        for total, begin in ((zonal_total, 0), (merid_total, levels)):
+            here = slice((begin + level) * ROWS, (begin + level + 1) * ROWS)
+            velocity_ref[here] = velocity_ref[here] + ADVECT_HALF * total
+
+
+def finish_kernel(
     far_ref,
     near_ref,
     pack_ref,
@@ -458,20 +494,18 @@
     masked_ref,
     kappa_ref,
     bottom_ref,
-    next_in_ref,
-    side_in_ref,
+    next_ref,
+    adjoint_in_ref,
     velocity_in_ref,
     adjoint_ref,
     velocity_ref,
-    next_ref,
-    side_ref,
     north_ref,
     south_ref,
-    ring_ref,
-    total_ref,
+    guard_ref,
 ):
     levels = masked_ref.shape[0] // (2 * ROWS)
     layout = Layout(levels)
+    top = ROWS - 1
     band = lax.axis_index("lat")
     odd_band = lax.rem(band, 2) == 1
     top_band = (band == lax.axis_size("lat") - 1).astype(jnp.int32)
@@ -492,9 +526,9 @@
         north_ref[...] = jnp.dot(near_ref[...], turn, preferred_element_type=jnp.float32)
         south_ref[...] = far_ref[...].astype(jnp.float32)
 
-    for at in range(2):
-        here = slice(layout.merid[at], layout.merid[at] + levels)
-        north_ref[here] = north_ref[here] * folded
+    adjoint_ref[...] = adjoint_in_ref[...]
+    velocity_ref[...] = velocity_in_ref[...]
+    guard_ref[...] = jnp.zeros_like(guard_ref)
 
     def rows_at(ref, begin):
         return ref[begin : begin + levels]
@@ -502,108 +536,122 @@
     def unpacked(packed):
         return packed, shift(packed, LANES // 2, 1), shift(packed, 96, 1)
 
+    def state_row(at, field, row):
+        return strided(state_ref, (at * FIELDS + field) * levels * ROWS + row, levels)
+
+    def add_rows(ref, begin, value):
+        here = pl.ds(begin, levels, stride=ROWS)
+        ref[here, :] = ref[here, :] + value
+
     level_of = rows_of((levels, LANES)).astype(jnp.float32)
-    left = lanes_of((levels, LANES)) < LANES // 2
+    lane = lanes_of((levels, LANES))
+    first_lane, last_lane = lane == 0, lane == LANES - 1
 
     def side_depth(row):
         spot = slice(EDGE_MASKED + 2 * levels, EDGE_MASKED + 2 * levels + 1)
         west = west_ref[...].astype(jnp.float32)[row : row + 1, spot]
         east = east_ref[...].astype(jnp.float32)[row : row + 1, spot]
-        return jnp.where(left, west, east)
-
-    def add_rows(ref, begin, value):
-        here = pl.ds(begin, levels, stride=ROWS)
-        ref[here, :] = ref[here, :] + value
-
-    top = ROWS - 1
+        return jnp.where(lane < LANES // 2, west, east)
+
     depth = bottom_ref[...].astype(jnp.float32)
-    top_merid = strided(state_ref, 3 * levels * ROWS + top, levels)
-    north_merid = rows_at(north_ref, layout.merid[0])
+    merid_top = state_row(0, 3, top)
+    north_merid = rows_at(north_ref, layout.merid[0]) * folded
     south_merid = rows_at(south_ref, layout.merid[0])
-    top_factor = ADVECT_HALF * (top_merid - north_merid) + DIFFUSE
+    top_factor = ADVECT_HALF * (merid_top - north_merid) + DIFFUSE
     bottom_factor = ADVECT_HALF * south_merid - open_south
-    own_top = unpacked(rows_at(pack_ref, 0))
-    own_bottom = unpacked(rows_at(pack_ref, levels))
+    own_corner = (unpacked(rows_at(pack_ref, 4 * levels)), unpacked(rows_at(pack_ref, 0)))
     north_corner = unpacked(rows_at(north_ref, layout.corner))
     south_corner = unpacked(rows_at(south_ref, layout.corner))
-    side_top_factor = ADVECT_HALF * (own_top[2] - folded * north_corner[2]) + DIFFUSE
-    side_bottom_factor = ADVECT_HALF * south_corner[2] - open_south
-    merid_total = jnp.zeros((levels, LANES), jnp.float32)
+    side_top = ADVECT_HALF * (own_corner[1][2] - folded * north_corner[2]) + DIFFUSE
+    side_bottom = ADVECT_HALF * south_corner[2] - open_south
+
+    merids = {row: state_row(1, 3, row) for row in (0, top - 1, top)}
+    next_north = ADVECT_HALF * (merids[top] - folded * rows_at(north_ref, layout.merid[1])) + DIFFUSE
+    next_south = ADVECT_HALF * rows_at(south_ref, layout.merid[1]) - open_south
+    east_factors, west_factors, kappas = [], [], []
+    for row, begin in ((0, 4 * levels), (top, 0)):
+        zonal = state_row(1, 2, row)
+        zonal_west = jnp.where(first_lane, rows_at(pack_ref, begin + levels), shift(zonal, 1, 1))
+        east_factors.append(ADVECT_HALF * zonal + DIFFUSE)
+        west_factors.append(ADVECT_HALF * zonal_west - DIFFUSE)
+        kappas.append(
+            (strided(kappa_ref, row, levels), strided(kappa_ref, ROWS + row, levels))
+        )
+
+    zonal_totals = [jnp.zeros((levels, LANES), jnp.float32) for _ in range(2)]
+    merid_totals = {row: jnp.zeros((levels, LANES), jnp.float32) for row in (0, top - 1, top)}
     for tracer in range(2):
         start = tracer * levels * ROWS
-        masked = strided(masked_ref, start + top, levels)
-        beyond = rows_at(north_ref, layout.masked + tracer * levels)
-        part = rows_at(north_ref, layout.part + tracer * levels)
-        step = beyond - masked
-        add_rows(
-            next_ref, start + top, jnp.where(level_of < depth[top:], top_factor * step, 0.0)
-        )
-        ring = part - (ADVECT_HALF * (north_merid - top_merid) + DIFFUSE) * step
+        own_top = strided(masked_ref, start + top, levels)
+        own_bottom = strided(masked_ref, start, levels)
+        north = rows_at(north_ref, layout.masked + tracer * levels)
+        south = rows_at(south_ref, layout.masked + tracer * levels)
+        north_step, south_step = north - own_top, own_bottom - south
         wet = level_of < north_ref[layout.bottom : layout.bottom + 1]
-        ring_ref[tracer * levels : (tracer + 1) * levels] = jnp.where(wet, ring, 0.0)
-        field = strided(state_ref, start + top, levels)
-        field_north = rows_at(north_ref, layout.tracer[0] + tracer * levels)
-        merid_total = merid_total + (field + field_north) * step
-        masked = strided(masked_ref, start, levels)
-        beyond = rows_at(south_ref, layout.masked + tracer * levels)
-        part = rows_at(south_ref, layout.part + tracer * levels)
-        step = masked - beyond
-        add_rows(
-            next_ref, start, jnp.where(level_of < depth[0:1], bottom_factor * step, 0.0)
-        )
-        ring = part + (ADVECT_HALF * south_merid + DIFFUSE) * step
+        ring_north = rows_at(north_ref, layout.part + tracer * levels)
+        ring_north = ring_north - (ADVECT_HALF * (north_merid - merid_top) + DIFFUSE) * north_step
+        ring_north = jnp.where(wet, ring_north, 0.0)
         wet = level_of < south_ref[layout.bottom : layout.bottom + 1]
-        ring_ref[(2 + tracer) * levels : (3 + tracer) * levels] = jnp.where(wet, ring, 0.0)
-        face = side_top_factor * (north_corner[tracer] - own_top[tracer])
-        add_rows(side_ref, start + top, jnp.where(level_of < side_depth(top), face, 0.0))
-        face = side_bottom_factor * (own_bottom[tracer] - south_corner[tracer])
-        add_rows(side_ref, start, jnp.where(level_of < side_depth(0), face, 0.0))
-    total_ref[...] = merid_total
-
-    tile = Tile(levels, west_ref, east_ref, state_ref)
-    first_lane, last_lane = tile.first_lane, tile.last_lane
-    top_row, bottom_row = tile.top_row, tile.bottom_row
-    closed = (band == 0).astype(jnp.int32)
-    spread_south = jnp.where(rows_of(tile.shape) >= closed, DIFFUSE, 0.0)
-    for level in range(levels):
-        zonal, zonal_west, merid = tile.velocities(1, level)
-        merid_south = jnp.where(
-            bottom_row, tile.line(south_ref, layout.merid[1] + level), shift(merid, 1, 0)
-        )
-        merid_net = merid - jnp.where(top_row, tile.line(north_ref, layout.merid[1] + level), 0.0)
-        north_factor = ADVECT_HALF * merid_net + DIFFUSE
-        south_factor = ADVECT_HALF * merid_south - spread_south
-        zonal_total = jnp.zeros(tile.shape, jnp.float32)
-        merid_total = jnp.zeros(tile.shape, jnp.float32)
-        for tracer in range(2):
-            index = tracer * levels + level
-            masked = tile_of(next_ref, index)
-            side = tile_of(side_ref, index)
-            to_east = jnp.where(last_lane, side, shift(masked, -1, 1)) - masked
-            to_west = masked - jnp.where(first_lane, side, shift(masked, 1, 1))
-            to_north = jnp.where(top_row, tile.line(ring_ref, index), shift(masked, -1, 0)) - masked
-            to_south = masked - jnp.where(
-                bottom_row, tile.line(ring_ref, 2 * levels + index), shift(masked, 1, 0)
+        ring_south = rows_at(south_ref, layout.part + tracer * levels)
+        ring_south = ring_south + (ADVECT_HALF * south_merid + DIFFUSE) * south_step
+        ring_south = jnp.where(wet, ring_south, 0.0)
+        first_field = state_row(0, tracer, top) + rows_at(
+            north_ref, layout.tracer[0] + tracer * levels
+        )
+        merid_totals[top] = merid_totals[top] + first_field * north_step
+        changes = (
+            jnp.where(level_of < depth[0:1], bottom_factor * south_step, 0.0),
+            jnp.where(level_of < depth[top:], top_factor * north_step, 0.0),
+        )
+        side_changes = (
+            side_bottom * (own_corner[0][tracer] - south_corner[tracer]),
+            side_top * (north_corner[tracer] - own_corner[1][tracer]),
+        )
+        fields = {row: state_row(1, tracer, row) for row in (0, 1, top - 1, top)}
+        for at, row in enumerate((0, top)):
+            change = changes[at]
+            side = jnp.where(level_of < side_depth(row), side_changes[at], 0.0)
+            guard_ref[ROWS : ROWS + levels] = change
+            above = guard_ref[ROWS - 1 : ROWS - 1 + levels]
+            below = guard_ref[ROWS + 1 : ROWS + 1 + levels]
+            kappa_above, kappa_below = kappas[at]
+            to_east = jnp.where(last_lane, side, shift(change, -1, 1)) - change
+            to_west = change - jnp.where(first_lane, side, shift(change, 1, 1))
+            value = (
+                change
+                + kappa_below * (below - change)
+                + kappa_above * (above - change)
+                + east_factors[at] * to_east
+                + west_factors[at] * to_west
             )
-            adjoint_ref[index * ROWS : (index + 1) * ROWS] = (
-                mixed(next_ref, kappa_ref, tracer * levels * ROWS, level, levels)
-                + (zonal + DIFFUSE) * to_east
-                + (zonal_west - DIFFUSE) * to_west
-                + north_factor * to_north
-                + south_factor * to_south
+            begin = (4 * levels if row == 0 else 0) + (2 + tracer) * levels
+            field_east = jnp.where(
+                last_lane, rows_at(pack_ref, begin), shift(fields[row], -1, 1)
             )
-            field, field_east = tile.tracer(1, level, tracer)
-            field_north = jnp.where(
-                top_row,
-                tile.line(north_ref, layout.tracer[1] + tracer * levels + level),
-                shift(field, -1, 0),
-            )
-            zonal_total = zonal_total + (field + field_east) * to_east
-            merid_total = merid_total + (field + field_north) * to_north
-        merid_total = merid_total + jnp.where(top_row, tile.line(total_ref, level), 0.0)
-        for total, begin in ((zonal_total, 0), (merid_total, levels)):
-            here = slice((begin + level) * ROWS, (begin + level + 1) * ROWS)
-            velocity_ref[here] = velocity_in_ref[here] + ADVECT_HALF * total
+            zonal_totals[at] = zonal_totals[at] + (fields[row] + field_east) * to_east
+            full = strided(next_ref, start + row, levels) + change
+            if row == 0:
+                value = value - (ADVECT_HALF * merids[0] + DIFFUSE) * change
+                value = value + next_south * (full - ring_south)
+                add_rows(adjoint_ref, start + 1, -(ADVECT_HALF * merids[0] - DIFFUSE) * change)
+                merid_totals[0] = merid_totals[0] - (fields[0] + fields[1]) * change
+            else:
+                value = value + (ADVECT_HALF * merids[top - 1] - DIFFUSE) * change
+                value = value + next_north * (ring_north - full)
+                inner = (ADVECT_HALF * merids[top - 1] + DIFFUSE) * change
+                add_rows(adjoint_ref, start + top - 1, inner)
+                merid_totals[top - 1] = (
+                    merid_totals[top - 1] + (fields[top - 1] + fields[top]) * change
+                )
+                field_north = rows_at(north_ref, layout.tracer[1] + tracer * levels)
+                merid_totals[top] = merid_totals[top] + (fields[top] + field_north) * (
+                    ring_north - full
+                )
+            add_rows(adjoint_ref, start + row, value)
+    for at, row in enumerate((0, top)):
+        add_rows(velocity_ref, row, ADVECT_HALF * zonal_totals[at])
+    for row, total in merid_totals.items():
+        add_rows(velocity_ref, levels * ROWS + row, ADVECT_HALF * total)
 
 
 def swaps(pairs):
@@ -627,7 +675,7 @@
     return swaps(near), swaps(far)
 
 
-def call(kernel, outputs, scratch, scalars, arrays, aliases=None):
+def call(kernel, outputs, scratch, scalars, arrays):
     vmem = pl.BlockSpec(memory_space=pltpu.VMEM)
     smem = pl.BlockSpec(memory_space=pltpu.SMEM)
     return pl.pallas_call(
@@ -636,7 +684,6 @@
         in_specs=[smem] * len(scalars) + [vmem] * len(arrays),
         out_specs=[vmem] * len(outputs),
         scratch_shapes=[pltpu.VMEM(shape, jnp.float32) for shape in scratch],
-        input_output_aliases=aliases or {},
         compiler_params=pltpu.CompilerParams(vmem_limit_bytes=32 * 1024 * 1024),
     )(*scalars, *arrays)
 
@@ -679,10 +726,10 @@
             ((2 * full, LANES), wide),
             ((full + ROWS, LANES), wide),
             ((4 * ROWS, 2 * LANES), wide),
-            ((ROWS * LANES, LANES), narrow),
+            ((steps, ROWS * LANES, LANES), narrow),
         ],
         [(2 * LANES, LANES)],
-        [mix_table],
+        [mix_table, holder_offset],
         [
             final_adjoint.reshape(2 * full, LANES),
             bottom_level,
@@ -693,7 +740,7 @@
         edges_kernel,
         [((ROWS, EDGE_LANES), narrow), ((ROWS, EDGE_LANES), narrow)],
         [(EDGE_MASKED, LANES)],
-        [holder_offset],
+        [],
         [received, side, pick],
     )
     inner_routes, outer_routes = ring_routes(tiles)
@@ -714,7 +761,7 @@
             ((layout.rows, LANES), narrow),
             ((ROWS, EDGE_LANES), narrow),
             ((ROWS, EDGE_LANES), narrow),
-            ((2 * levels, LANES), wide),
+            ((8 * levels, LANES), wide),
         ],
         [(LANES, EDGE_LANES), (EDGE_LANES, LANES), (layout.rows, LANES), (layout.rows, LANES)],
         [],
@@ -729,21 +776,20 @@
         [holder_offset],
         [received, west],
     )
-    following, beside, velocity = call(
-        first_step_kernel,
+    adjoint, velocity, following = call(
+        steps_kernel,
         [((2 * full, LANES), wide)] * 3,
+        [(2 * full, LANES)],
         [],
-        [],
-        [west, east, state, masked, base, bottom_level],
-    )
-    adjoint, velocity, _, _ = call(
-        second_step_kernel,
-        [((2 * full, LANES), wide)] * 4,
+        [west, east, state, masked, base, kappa, bottom_level],
+    )
+    adjoint, velocity = call(
+        finish_kernel,
+        [((2 * full, LANES), wide)] * 2,
         [
             (layout.rows, LANES),
             (layout.rows, LANES),
-            (4 * levels, LANES),
-            (levels, LANES),
+            ((levels + 2 * ROWS + ROWS - 1) // ROWS * ROWS, LANES),
         ],
         [],
         [
@@ -757,10 +803,9 @@
             kappa,
             bottom_level,
             following,
-            beside,
+            adjoint,
             velocity,
         ],
-        {9: 2, 10: 3},
     )
     shape = (2, levels, ROWS, LANES)
     return adjoint.reshape(shape), velocity.reshape(shape)

time: 61.5 us -> 60.5 us (0.984)
  waiting for transfers between devices: 24.2 us -> 23.4 us
  transfers between devices with their start and end apart: 5 -> 5, of which waited for: 3 -> 3; matrix products, arithmetic and copies ran while one was open for 0% -> 0% of each run, Pallas kernels for 6% -> 8%
where the time goes in v6:
time: 60.5 us; the launch traced here: 60.2 us
  starting transfers between devices  26.6 us (44%)
  waiting for transfers between devices  23.4 us (39%)
  Pallas kernels  9.35 us (15%)
  between operations  0.78 us (1%)
    all_to_all x1, waiting for transfers between devices, shards(): lax.all_to_all(request, 'lat', split_axis=0, concat_axis=0, tiled=True)  17.7 us
    ppermute x1, starting transfers between devices, shards(): outer = lax.ppermute(outer, 'lon', outer_routes)  11.2 us
    all_to_all x1, starting transfers between devices, shards(): lax.all_to_all(request, 'lat', split_axis=0, concat_axis=0, tiled=True)  8.25 us
    pallas_call x7, Pallas kernels, call(): pl.pallas_call(kernel, out_shape=[jax.ShapeDtypeStruct(shape, dtype) for...  6.74 us
    ppermute x1, waiting for transfers between devices, shards(): far = lax.ppermute(far, ('lon', 'lat'), far_routes)  5.37 us
    ppermute x1, starting transfers between devices, shards(): far = lax.ppermute(far, ('lon', 'lat'), far_routes)  2.82 us
    pallas_call x1, Pallas kernels, shards(): pl.pallas_call(request_kernel, out_shape=jax.ShapeDtypeStruct((bands, ste...  2.61 us
    ppermute x1, starting transfers between devices, shards(): near = lax.ppermute(near, ('lon', 'lat'), near_routes)  2.42 us
  transfers between devices with their start and end apart: 5, of which 3 were waited for; matrix products, arithmetic and copies ran while one was open for 0% of the time, Pallas kernels for 8%

profile of v6, /device:TPU:22, one launch (start us, length us, event | category | flops | bytes accessed | tf_op | source)
XLA Modules:
  0.0 60.2 jit_solution(6418572896482491040)
XLA Ops:
  0.6 0.0 copy-start
  0.6 0.0 copy-start.1
  0.7 0.0 copy-start.2
  0.7 0.0 copy-start.3
  0.7 0.0 copy-start.4
  0.7 2.6 %shard_map.86 = bf16[8,2,152,128]{3,2,1,0:T(8,128)(2,1)} custom-call(s32[2,8,64]{2,1,0:T(8,128)} %slot_hbm.1, bf16[2432,128]{1,0:T(8,128)(2,1)} %bitcast.7), custom_call_target="tpu_custom_call" | custom-call | tf_op jit(solution)/shard_map/pallas_call | solution.py:702
  3.3 8.2 %all-to-all-start = ((bf16[8,2,152,128]{3,2,1,0:T(8,128)(2,1)}), bf16[8,2,152,128]{3,2,1,0:T(8,128)(2,1)S(1)}, u32[]{:S(2)}, u32[]{:S(2)}) async-start(bf16[8,2,152,128]{3,2,1,0:T(8,128)(2,1)} %shard_map.86), calls=%async_computation | async-start | bytes 1245184 | tf_op jit(solution)/shard_map/all_to_all | solution.py:721
  11.5 0.0 copy-done
  11.6 1.3 %shard_map.87 = (f32[608,128]{1,0:T(8,128)S(1)}, f32[608,128]{1,0:T(8,128)S(1)}, f32[312,128]{1,0:T(8,128)S(1)}, f32[32,256]{1,0:T(8,128)S(1)}, bf16[2,1024,128]{2,1,0:T(8,128)(2,1)S(1)}) custom-call(f32[8]{0:T(128)S(1)} %copy-done.4, s32[2,8,64]{2,1,0:T(8,128)S(1)} %copy-done.2, f32[608,128]{1,0:T(8,128)S(1)} %bitcast.5, s32[8,128]{1,0:T(8,128)S(1)} %copy-done.3, ...), custom_call_target="tpu_custom_call" | custom-call | tf_op jit(solution)/shard_map/pallas_call | solution.py:681
  12.9 17.7 %all-to-all-done.piece_ref = bf16[8,2,152,128]{3,2,1,0:T(8,128)(2,1)S(1)} async-done(((bf16[8,2,152,128]{3,2,1,0:T(8,128)(2,1)}), bf16[8,2,152,128]{3,2,1,0:T(8,128)(2,1)S(1)}, u32[]{:S(2)}, u32[]{:S(2)}) %all-to-all-start) | async-done | bytes 622624 | tf_op jit(solution)/shard_map/all_to_all | solution.py:721
  30.6 0.4 shard_map.88
  31.0 11.2 %collective-permute-start = (bf16[8,768]{1,0:T(8,128)(2,1)S(1)}, bf16[8,768]{1,0:T(8,128)(2,1)S(1)}, u32[]{:S(2)}, u32[]{:S(2)}) collective-permute-start(bf16[8,768]{1,0:T(8,128)(2,1)S(1)} %get-tuple-element.23), channel_id=1, source_target_pairs={{8,16},{16,8},{24,32},{32,24},{40,48},{48,40},{56,64},{64,56},{72,... | collective-permute-start | bytes 36872 | tf_op jit(solution)/shard_map/ppermute | solution.py:748
  42.3 1.9 %collective-permute-start.1 = (bf16[8,768]{1,0:T(8,128)(2,1)S(1)}, bf16[8,768]{1,0:T(8,128)(2,1)S(1)}, u32[]{:S(2)}, u32[]{:S(2)}) collective-permute-start(bf16[8,768]{1,0:T(8,128)(2,1)S(1)} %get-tuple-element.24), channel_id=1, source_target_pairs={{0,8},{8,0},{16,24},{24,16},{32,40},{40,32},{48,56},{56,48},{64,72... | collective-permute-start | bytes 36872 | tf_op jit(solution)/shard_map/ppermute | solution.py:749
  44.2 0.8 %shard_map.89 = (f32[432,128]{1,0:T(8,128)S(1)}, f32[432,128]{1,0:T(8,128)S(1)}) custom-call(s32[2,8,64]{2,1,0:T(8,128)S(1)} %copy-done.2, bf16[8,2,152,128]{3,2,1,0:T(8,128)(2,1)S(1)} %all-to-all-done.piece_ref, f32[608,128]{1,0:T(8,128)S(1)} %get-tuple-element.25.masked_ref, f32[608,128]{1,0:T(8,128)S(1)} %get-tuple-element.26.base_ref, s32[8,128]{1,0:T(8,128)S(1)} %copy-done.3), custom_call_target="tpu_custom_call" | custom-call | tf_op jit(solution)/shard_map/pallas_call | solution.py:681
  45.0 0.0 collective-permute-done.outer_ref
  45.0 0.3 collective-permute-done.1.inner_ref
  45.3 0.3 shard_map.90
  45.7 2.8 %collective-permute-start.2 = (bf16[432,128]{1,0:T(8,128)(2,1)S(1)}, bf16[432,128]{1,0:T(8,128)(2,1)S(1)}, u32[]{:S(2)}, u32[]{:S(2)}) collective-permute-start(bf16[432,128]{1,0:T(8,128)(2,1)S(1)} %get-tuple-element.29), channel_id=1, source_target_pairs={{1,2},{2,1},{3,4},{4,3},{5,6},{6,5},{7,511},{511,7},{9,10},{10,9},... | collective-permute-start | bytes 331784 | tf_op jit(solution)/shard_map/ppermute | solution.py:770
  48.5 2.4 %collective-permute-start.3 = (bf16[432,128]{1,0:T(8,128)(2,1)S(1)}, bf16[432,128]{1,0:T(8,128)(2,1)S(1)}, u32[]{:S(2)}, u32[]{:S(2)}) collective-permute-start(bf16[432,128]{1,0:T(8,128)(2,1)S(1)} %get-tuple-element.30), channel_id=1, source_target_pairs={{0,1},{1,0},{2,3},{3,2},{4,5},{5,4},{6,7},{7,6},{8,9},{9,8},{10,11... | collective-permute-start | bytes 331784 | tf_op jit(solution)/shard_map/ppermute | solution.py:771
  50.9 1.0 %shard_map.91.state_ref = f32[2432,128]{1,0:T(8,128)S(1)} custom-call(s32[2,8,64]{2,1,0:T(8,128)S(1)} %copy-done.2, bf16[8,2,152,128]{3,2,1,0:T(8,128)(2,1)S(1)} %all-to-all-done.piece_ref, bf16[8,768]{1,0:T(8,128)(2,1)S(1)} %get-tuple-element.32.west_ref), custom_call_target="tpu_custom_call" | custom-call | tf_op jit(solution)/shard_map/pallas_call | solution.py:681
  51.9 1.5 %shard_map.92 = (f32[608,128]{1,0:T(8,128)S(1)}, f32[608,128]{1,0:T(8,128)S(1)}, f32[608,128]{1,0:T(8,128)S(1)}) custom-call(bf16[8,768]{1,0:T(8,128)(2,1)S(1)} %get-tuple-element.32.west_ref, bf16[8,768]{1,0:T(8,128)(2,1)S(1)} %get-tuple-element.33.east_ref, f32[2432,128]{1,0:T(8,128)S(1)} %shard_map.91.state_ref, ...), custom_call_target="tpu_custom_call" | custom-call | tf_op jit(solution)/shard_map/pallas_call | solution.py:681
  53.4 5.4 %collective-permute-done.2.far_ref = bf16[432,128]{1,0:T(8,128)(2,1)S(1)} collective-permute-done((bf16[432,128]{1,0:T(8,128)(2,1)S(1)}, bf16[432,128]{1,0:T(8,128)(2,1)S(1)}, u32[]{:S(2)}, u32[]{:S(2)}) %collective-permute-start.2) | collective-permute-done | bytes 110624 | tf_op jit(solution)/shard_map/ppermute | solution.py:770
  58.8 0.0 collective-permute-done.3.near_ref
  58.8 1.4 %shard_map.93 = (f32[608,128]{1,0:T(8,128)}, f32[608,128]{1,0:T(8,128)}) custom-call(bf16[432,128]{1,0:T(8,128)(2,1)S(1)} %collective-permute-done.2.far_ref, bf16[432,128]{1,0:T(8,128)(2,1)S(1)} %collective-permute-done.3.near_ref, f32[304,128]{1,0:T(8,128)S(1)} %get-tuple-element.31.pack_ref, bf16[8,768]{1,0:T(8,128)(2,1)S(1)} %get-tuple-element.32.west_ref, ...), custom_call_target="tpu_custom_call" | custom-call | tf_op jit(solution)/shard_map/pallas_call | solution.py:681
  (4 shorter events, 0.0 us)
Async XLA Ops:
  0.6 10.9 %copy-start = (f32[2,38,8,128]{3,2,1,0:T(8,128)S(1)}, f32[2,38,8,128]{3,2,1,0:T(8,128)}, u32[]{:S(2)}) copy-start(f32[2,38,8,128]{3,2,1,0:T(8,128)} %param.7) | copy-start | bytes 933892
  0.6 10.9 %copy-start.1 = (s32[37,8,128]{2,1,0:T(8,128)S(1)}, s32[37,8,128]{2,1,0:T(8,128)}, u32[]{:S(2)}) copy-start(s32[37,8,128]{2,1,0:T(8,128)} %param.12) | copy-start | bytes 454660
  0.7 10.9 %copy-start.2 = (s32[2,8,64]{2,1,0:T(8,128)S(1)}, s32[2,8,64]{2,1,0:T(8,128)}, u32[]{:S(2)}) copy-start(s32[2,8,64]{2,1,0:T(8,128)} %offset_ref.5) | copy-start | bytes 12292
  0.7 10.9 %copy-start.3 = (s32[8,128]{1,0:T(8,128)S(1)}, s32[8,128]{1,0:T(8,128)}, u32[]{:S(2)}) copy-start(s32[8,128]{1,0:T(8,128)} %bottom_ref.7) | copy-start | bytes 12292
  0.7 10.9 %copy-start.4 = (f32[8]{0:T(128)S(1)}, f32[8]{0:T(128)}, u32[]{:S(2)}) copy-start(f32[8]{0:T(128)} %table_ref.1) | copy-start | bytes 100
  3.3 27.3 %all-to-all-start = ((bf16[8,2,152,128]{3,2,1,0:T(8,128)(2,1)}), bf16[8,2,152,128]{3,2,1,0:T(8,128)(2,1)S(1)}, u32[]{:S(2)}, u32[]{:S(2)}) async-start(bf16[8,2,152,128]{3,2,1,0:T(8,128)(2,1)} %shard_map.86), calls=%async_computation | async-start | bytes 1245184 | tf_op jit(solution)/shard_map/all_to_all | solution.py:721
  31.0 14.0 %collective-permute-start = (bf16[8,768]{1,0:T(8,128)(2,1)S(1)}, bf16[8,768]{1,0:T(8,128)(2,1)S(1)}, u32[]{:S(2)}, u32[]{:S(2)}) collective-permute-start(bf16[8,768]{1,0:T(8,128)(2,1)S(1)} %get-tuple-element.23), channel_id=1, source_target_pairs={{8,16},{16,8},{24,32},{32,24},{40,48},{48,40},{56,64},{64,56},{72,... | collective-permute-start | bytes 36872 | tf_op jit(solution)/shard_map/ppermute | solution.py:748
  42.3 3.1 %collective-permute-start.1 = (bf16[8,768]{1,0:T(8,128)(2,1)S(1)}, bf16[8,768]{1,0:T(8,128)(2,1)S(1)}, u32[]{:S(2)}, u32[]{:S(2)}) collective-permute-start(bf16[8,768]{1,0:T(8,128)(2,1)S(1)} %get-tuple-element.24), channel_id=1, source_target_pairs={{0,8},{8,0},{16,24},{24,16},{32,40},{40,32},{48,56},{56,48},{64,72... | collective-permute-start | bytes 36872 | tf_op jit(solution)/shard_map/ppermute | solution.py:749
  45.7 13.1 %collective-permute-start.2 = (bf16[432,128]{1,0:T(8,128)(2,1)S(1)}, bf16[432,128]{1,0:T(8,128)(2,1)S(1)}, u32[]{:S(2)}, u32[]{:S(2)}) collective-permute-start(bf16[432,128]{1,0:T(8,128)(2,1)S(1)} %get-tuple-element.29), channel_id=1, source_target_pairs={{1,2},{2,1},{3,4},{4,3},{5,6},{6,5},{7,511},{511,7},{9,10},{10,9},... | collective-permute-start | bytes 331784 | tf_op jit(solution)/shard_map/ppermute | solution.py:770
  48.5 10.3 %collective-permute-start.3 = (bf16[432,128]{1,0:T(8,128)(2,1)S(1)}, bf16[432,128]{1,0:T(8,128)(2,1)S(1)}, u32[]{:S(2)}, u32[]{:S(2)}) collective-permute-start(bf16[432,128]{1,0:T(8,128)(2,1)S(1)} %get-tuple-element.30), channel_id=1, source_target_pairs={{0,1},{1,0},{2,3},{3,2},{4,5},{5,4},{6,7},{7,6},{8,9},{9,8},{10,11... | collective-permute-start | bytes 331784 | tf_op jit(solution)/shard_map/ppermute | solution.py:771

commit v7 on v6

--- a/solution.py
+++ b/solution.py
@@ -19,6 +19,9 @@
 EDGE_MASKED = 512
 EDGE_PART = 640
 EDGE_LANES = 768
+
+
+DRAFT_ROWS = ((ROWS - 1, 0), (ROWS - 1, 1), (0, 0), (0, 1), (ROWS - 2, 0))
 
 
 class Layout:
@@ -105,6 +108,7 @@
     kappa_ref,
     side_ref,
     pick_ref,
+    holder_ref,
     column_ref,
 ):
     levels = adjoint_ref.shape[0] // (2 * ROWS)
@@ -128,8 +132,14 @@
                 masked_ref, kappa_ref, start, level, levels
             )
     pick = pick_columns()
+    offsets = []
     for at, step in enumerate(STEP_ORDER):
-        pick_ref[at] = pick_columns(offset_ref[step, lax.axis_index("lat"), lax.axis_index("lon")])
+        offset = offset_ref[step, lax.axis_index("lat"), lax.axis_index("lon")]
+        pick_ref[at] = pick_columns(offset)
+        offsets.append(offset)
+    for index, (row, at) in enumerate(DRAFT_ROWS):
+        held = rows_of((ROWS, LANES)) == lax.rem(row + offsets[at], ROWS)
+        holder_ref[index * ROWS : (index + 1) * ROWS] = jnp.where(held, 1.0, 0.0)
     column_ref[...] = jnp.zeros_like(column_ref)
     rows = 2 * levels
     for start, ref in ((0, masked_ref), (LANES, base_ref)):
@@ -208,17 +218,24 @@
 
 
 def drafts_kernel(
-    offset_ref, piece_ref, masked_ref, base_ref, bottom_ref, top_ref, bot_ref, line_ref
+    piece_ref, holder_ref, masked_ref, base_ref, bottom_ref, top_ref, bot_ref, line_ref
 ):
-    tile = lax.axis_index("lon")
-    band = lax.axis_index("lat")
     levels = masked_ref.shape[0] // (2 * ROWS)
-    pieces = FIELDS * levels
-    holders = piece_ref.shape[0]
-    for slot, (row, at) in enumerate(((ROWS - 1, 0), (ROWS - 1, 1), (0, 0), (0, 1), (ROWS - 2, 0))):
-        offset = offset_ref[STEP_ORDER[at], band, tile]
-        chunk = piece_ref[lax.rem(row + offset, holders), at]
-        line_ref[slot * pieces : (slot + 1) * pieces] = chunk.astype(jnp.float32)
+    holders, steps, pieces, _ = piece_ref.shape
+    for at in range(steps):
+        wanted = [index for index, (_, step) in enumerate(DRAFT_ROWS) if step == at]
+        found = [None] * len(wanted)
+        for holder in range(holders):
+            chunk = piece_ref[holder, at].astype(jnp.float32)
+            for place, index in enumerate(wanted):
+                if holder == 0:
+                    found[place] = chunk
+                    continue
+                here = index * ROWS + holder
+                held = jnp.broadcast_to(holder_ref[here : here + 1], chunk.shape) > 0.0
+                found[place] = jnp.where(held, chunk, found[place])
+        for place, index in enumerate(wanted):
+            line_ref[index * pieces : (index + 1) * pieces] = found[place]
     bottom = bottom_ref[...].astype(jnp.float32)
     layout = Layout(levels)
     wide = lanes_of((levels, LANES))
@@ -495,13 +512,16 @@
     kappa_ref,
     bottom_ref,
     next_ref,
-    adjoint_in_ref,
-    velocity_in_ref,
+    adjoint_in,
+    velocity_in,
+    adjoint_hbm,
+    velocity_hbm,
     adjoint_ref,
     velocity_ref,
     north_ref,
     south_ref,
     guard_ref,
+    out_sem,
 ):
     levels = masked_ref.shape[0] // (2 * ROWS)
     layout = Layout(levels)
@@ -526,8 +546,14 @@
         north_ref[...] = jnp.dot(near_ref[...], turn, preferred_element_type=jnp.float32)
         south_ref[...] = far_ref[...].astype(jnp.float32)
 
-    adjoint_ref[...] = adjoint_in_ref[...]
-    velocity_ref[...] = velocity_in_ref[...]
+    copies = []
+
+    def send(source, target, part):
+        here = pl.ds(part * levels * ROWS, levels * ROWS)
+        copy = pltpu.make_async_copy(source.at[here], target.at[here], out_sem.at[len(copies)])
+        copy.start()
+        copies.append(copy)
+
     guard_ref[...] = jnp.zeros_like(guard_ref)
 
     def rows_at(ref, begin):
@@ -648,10 +674,15 @@
                     ring_north - full
                 )
             add_rows(adjoint_ref, start + row, value)
+        send(adjoint_ref, adjoint_hbm, tracer)
     for at, row in enumerate((0, top)):
         add_rows(velocity_ref, row, ADVECT_HALF * zonal_totals[at])
+    send(velocity_ref, velocity_hbm, 0)
     for row, total in merid_totals.items():
         add_rows(velocity_ref, levels * ROWS + row, ADVECT_HALF * total)
+    send(velocity_ref, velocity_hbm, 1)
+    for copy in copies:
+        copy.wait()
 
 
 def swaps(pairs):
@@ -719,7 +750,7 @@
         pltpu.with_memory_space_constraint(store.reshape(pieces * slots, LANES), pltpu.HBM),
     )
     received = lax.all_to_all(request, "lat", split_axis=0, concat_axis=0, tiled=True)
-    masked, base, kappa, side, pick = call(
+    masked, base, kappa, side, pick, holder = call(
         prepare_kernel,
         [
             ((2 * full, LANES), wide),
@@ -727,6 +758,7 @@
             ((full + ROWS, LANES), wide),
             ((4 * ROWS, 2 * LANES), wide),
             ((steps, ROWS * LANES, LANES), narrow),
+            ((len(DRAFT_ROWS) * ROWS, LANES), wide),
         ],
         [(2 * LANES, LANES)],
         [mix_table, holder_offset],
@@ -750,9 +782,9 @@
     top, bot = call(
         drafts_kernel,
         [((layout.rows, LANES), wide), ((layout.rows, LANES), wide)],
-        [(5 * pieces, LANES)],
-        [holder_offset],
-        [received, masked, base, bottom_level],
+        [(len(DRAFT_ROWS) * pieces, LANES)],
+        [],
+        [received, holder, masked, base, bottom_level],
     )
     far, near, west, east, pack = call(
         functools.partial(complete_kernel, levels),
@@ -783,30 +815,23 @@
         [],
         [west, east, state, masked, base, kappa, bottom_level],
     )
-    adjoint, velocity = call(
+    arrays = (far, near, pack, west, east, state, masked, kappa, bottom_level, following)
+    arrays += (adjoint, velocity)
+    vmem = pl.BlockSpec(memory_space=pltpu.VMEM)
+    adjoint, velocity, _, _ = pl.pallas_call(
         finish_kernel,
-        [((2 * full, LANES), wide)] * 2,
-        [
-            (layout.rows, LANES),
-            (layout.rows, LANES),
-            ((levels + 2 * ROWS + ROWS - 1) // ROWS * ROWS, LANES),
+        out_shape=[jax.ShapeDtypeStruct((2 * full, LANES), wide)] * 4,
+        in_specs=[vmem] * len(arrays),
+        out_specs=[hbm, hbm, vmem, vmem],
+        input_output_aliases={len(arrays) - 2: 2, len(arrays) - 1: 3},
+        scratch_shapes=[
+            pltpu.VMEM((layout.rows, LANES), wide),
+            pltpu.VMEM((layout.rows, LANES), wide),
+            pltpu.VMEM(((levels + 2 * ROWS + ROWS - 1) // ROWS * ROWS, LANES), wide),
+            pltpu.SemaphoreType.DMA((4,)),
         ],
-        [],
-        [
-            far,
-            near,
-            pack,
-            west,
-            east,
-            state,
-            masked,
-            kappa,
-            bottom_level,
-            following,
-            adjoint,
-            velocity,
-        ],
-    )
+        compiler_params=pltpu.CompilerParams(vmem_limit_bytes=32 * 1024 * 1024),
+    )(*arrays)
     shape = (2, levels, ROWS, LANES)
     return adjoint.reshape(shape), velocity.reshape(shape)
 

time: 60.5 us -> 60.4 us (level)
  Pallas kernels: 9.35 us -> 8.69 us
    pallas_call x7 -> x6, Pallas kernels: 6.74 us -> 4.74 us  [call(): pl.pallas_call(kernel, out_shape=[jax.ShapeDtypeStruct(shape, dtype) for...]
    pallas_call x0 -> x1, Pallas kernels: none -> 1.34 us  [shards(): pl.pallas_call(finish_kernel, out_shape=[jax.ShapeDtypeStruct((2 * full,...]
  transfers between devices with their start and end apart: 5 -> 5, of which waited for: 3 -> 3; matrix products, arithmetic and copies ran while one was open for 0% -> 0% of each run, Pallas kernels for 8% -> 7%
where the time goes in v7:
time: 60.4 us; the launch traced here: 60.1 us
  starting transfers between devices  26.6 us (44%)
  waiting for transfers between devices  24 us (40%)
  Pallas kernels  8.69 us (14%)
  between operations  0.78 us (1%)
    all_to_all x1, waiting for transfers between devices, shards(): lax.all_to_all(request, 'lat', split_axis=0, concat_axis=0, tiled=True)  17.7 us
    ppermute x1, starting transfers between devices, shards(): outer = lax.ppermute(outer, 'lon', outer_routes)  11.2 us
    all_to_all x1, starting transfers between devices, shards(): lax.all_to_all(request, 'lat', split_axis=0, concat_axis=0, tiled=True)  8.25 us
    ppermute x1, waiting for transfers between devices, shards(): far = lax.ppermute(far, ('lon', 'lat'), far_routes)  5.32 us
    pallas_call x6, Pallas kernels, call(): pl.pallas_call(kernel, out_shape=[jax.ShapeDtypeStruct(shape, dtype) for...  4.74 us
    ppermute x1, starting transfers between devices, shards(): far = lax.ppermute(far, ('lon', 'lat'), far_routes)  2.81 us
    pallas_call x1, Pallas kernels, shards(): pl.pallas_call(request_kernel, out_shape=jax.ShapeDtypeStruct((bands, ste...  2.61 us
    ppermute x1, starting transfers between devices, shards(): near = lax.ppermute(near, ('lon', 'lat'), near_routes)  2.42 us
  transfers between devices with their start and end apart: 5, of which 3 were waited for; matrix products, arithmetic and copies ran while one was open for 0% of the time, Pallas kernels for 7%

profile of v7, /device:TPU:22, one launch (start us, length us, event | category | flops | bytes accessed | tf_op | source)
XLA Modules:
  0.0 60.1 jit_solution(2189606561247402601)
XLA Ops:
  0.6 0.0 copy-start
  0.6 0.0 copy-start.1
  0.7 0.0 copy-start.2
  0.7 0.0 copy-start.3
  0.7 0.0 copy-start.4
  0.7 2.6 %shard_map.86 = bf16[8,2,152,128]{3,2,1,0:T(8,128)(2,1)} custom-call(s32[2,8,64]{2,1,0:T(8,128)} %slot_hbm.1, bf16[2432,128]{1,0:T(8,128)(2,1)} %bitcast.7), custom_call_target="tpu_custom_call" | custom-call | tf_op jit(solution)/shard_map/pallas_call | solution.py:733
  3.3 8.2 %all-to-all-start = ((bf16[8,2,152,128]{3,2,1,0:T(8,128)(2,1)}), bf16[8,2,152,128]{3,2,1,0:T(8,128)(2,1)S(1)}, u32[]{:S(2)}, u32[]{:S(2)}) async-start(bf16[8,2,152,128]{3,2,1,0:T(8,128)(2,1)} %shard_map.86), calls=%async_computation | async-start | bytes 1245184 | tf_op jit(solution)/shard_map/all_to_all | solution.py:752
  11.5 0.0 copy-done
  11.6 1.3 %shard_map.87 = (f32[608,128]{1,0:T(8,128)S(1)}, f32[608,128]{1,0:T(8,128)S(1)}, f32[312,128]{1,0:T(8,128)S(1)}, f32[32,256]{1,0:T(8,128)S(1)}, bf16[2,1024,128]...) custom-call(f32[8]{0:T(128)S(1)} %copy-done.4, s32[2,8,64]{2,1,0:T(8,128)S(1)} %copy-done.3, f32[608,128]{1,0:T(8,128)S(1)} %bitcast.5, ...), custom_call_target="tpu_custom_call" | custom-call | tf_op jit(solution)/shard_map/pallas_call | solution.py:712
  12.9 17.7 %all-to-all-done.piece_ref = bf16[8,2,152,128]{3,2,1,0:T(8,128)(2,1)S(1)} async-done(((bf16[8,2,152,128]{3,2,1,0:T(8,128)(2,1)}), bf16[8,2,152,128]{3,2,1,0:T(8,128)(2,1)S(1)}, u32[]{:S(2)}, u32[]{:S(2)}) %all-to-all-start) | async-done | bytes 622624 | tf_op jit(solution)/shard_map/all_to_all | solution.py:752
  30.6 0.4 shard_map.88
  31.0 11.2 %collective-permute-start = (bf16[8,768]{1,0:T(8,128)(2,1)S(1)}, bf16[8,768]{1,0:T(8,128)(2,1)S(1)}, u32[]{:S(2)}, u32[]{:S(2)}) collective-permute-start(bf16[8,768]{1,0:T(8,128)(2,1)S(1)} %get-tuple-element.24), channel_id=1, source_target_pairs={{8,16},{16,8},{24,32},{32,24},{40,48},{48,40},{56,64},{64,56},{72,... | collective-permute-start | bytes 36872 | tf_op jit(solution)/shard_map/ppermute | solution.py:780
  42.3 1.9 %collective-permute-start.1 = (bf16[8,768]{1,0:T(8,128)(2,1)S(1)}, bf16[8,768]{1,0:T(8,128)(2,1)S(1)}, u32[]{:S(2)}, u32[]{:S(2)}) collective-permute-start(bf16[8,768]{1,0:T(8,128)(2,1)S(1)} %get-tuple-element.25), channel_id=1, source_target_pairs={{0,8},{8,0},{16,24},{24,16},{32,40},{40,32},{48,56},{56,48},{64,72... | collective-permute-start | bytes 36872 | tf_op jit(solution)/shard_map/ppermute | solution.py:781
  44.2 0.2 shard_map.89
  44.4 0.0 collective-permute-done.outer_ref
  44.5 0.9 %collective-permute-done.1.inner_ref = bf16[8,768]{1,0:T(8,128)(2,1)S(1)} collective-permute-done((bf16[8,768]{1,0:T(8,128)(2,1)S(1)}, bf16[8,768]{1,0:T(8,128)(2,1)S(1)}, u32[]{:S(2)}, u32[]{:S(2)}) %collective-permute-start.1) | collective-permute-done | bytes 12320 | tf_op jit(solution)/shard_map/ppermute | solution.py:781
  45.3 0.3 shard_map.90
  45.7 2.8 %collective-permute-start.2 = (bf16[432,128]{1,0:T(8,128)(2,1)S(1)}, bf16[432,128]{1,0:T(8,128)(2,1)S(1)}, u32[]{:S(2)}, u32[]{:S(2)}) collective-permute-start(bf16[432,128]{1,0:T(8,128)(2,1)S(1)} %get-tuple-element.31), channel_id=1, source_target_pairs={{1,2},{2,1},{3,4},{4,3},{5,6},{6,5},{7,511},{511,7},{9,10},{10,9},... | collective-permute-start | bytes 331784 | tf_op jit(solution)/shard_map/ppermute | solution.py:802
  48.5 2.4 %collective-permute-start.3 = (bf16[432,128]{1,0:T(8,128)(2,1)S(1)}, bf16[432,128]{1,0:T(8,128)(2,1)S(1)}, u32[]{:S(2)}, u32[]{:S(2)}) collective-permute-start(bf16[432,128]{1,0:T(8,128)(2,1)S(1)} %get-tuple-element.32), channel_id=1, source_target_pairs={{0,1},{1,0},{2,3},{3,2},{4,5},{5,4},{6,7},{7,6},{8,9},{9,8},{10,11... | collective-permute-start | bytes 331784 | tf_op jit(solution)/shard_map/ppermute | solution.py:803
  50.9 1.0 %shard_map.91.state_ref = f32[2432,128]{1,0:T(8,128)S(1)} custom-call(s32[2,8,64]{2,1,0:T(8,128)S(1)} %copy-done.3, bf16[8,2,152,128]{3,2,1,0:T(8,128)(2,1)S(1)} %all-to-all-done.piece_ref, bf16[8,768]{1,0:T(8,128)(2,1)S(1)} %get-tuple-element.34.west_ref), custom_call_target="tpu_custom_call" | custom-call | tf_op jit(solution)/shard_map/pallas_call | solution.py:712
  51.9 1.5 %shard_map.92 = (f32[608,128]{1,0:T(8,128)S(1)}, f32[608,128]{1,0:T(8,128)S(1)}, f32[608,128]{1,0:T(8,128)S(1)}) custom-call(bf16[8,768]{1,0:T(8,128)(2,1)S(1)} %get-tuple-element.34.west_ref, bf16[8,768]{1,0:T(8,128)(2,1)S(1)} %get-tuple-element.35.east_ref, f32[2432,128]{1,0:T(8,128)S(1)} %shard_map.91.state_ref, ...), custom_call_target="tpu_custom_call" | custom-call | tf_op jit(solution)/shard_map/pallas_call | solution.py:712
  53.4 5.3 %collective-permute-done.2.far_ref = bf16[432,128]{1,0:T(8,128)(2,1)S(1)} collective-permute-done((bf16[432,128]{1,0:T(8,128)(2,1)S(1)}, bf16[432,128]{1,0:T(8,128)(2,1)S(1)}, u32[]{:S(2)}, u32[]{:S(2)}) %collective-permute-start.2) | collective-permute-done | bytes 110624 | tf_op jit(solution)/shard_map/ppermute | solution.py:802
  58.7 0.0 collective-permute-done.3.near_ref
  58.7 1.3 %shard_map.93 = (f32[608,128]{1,0:T(8,128)}, f32[608,128]{1,0:T(8,128)}, f32[608,128]{1,0:T(8,128)S(1)}, f32[608,128]{1,0:T(8,128)S(1)}) custom-call(bf16[432,128]{1,0:T(8,128)(2,1)S(1)} %collective-permute-done.2.far_ref, bf16[432,128]{1,0:T(8,128)(2,1)S(1)} %collective-permute-done.3.near_ref, ...), custom_call_target="tpu_custom_call", output_to_operand_aliasing={{2}: (10, {}), {3}: (11, {})} | custom-call | tf_op jit(solution)/shard_map/pallas_call | solution.py:821
  (4 shorter events, 0.0 us)
Async XLA Ops:
  0.6 10.9 %copy-start = (f32[2,38,8,128]{3,2,1,0:T(8,128)S(1)}, f32[2,38,8,128]{3,2,1,0:T(8,128)}, u32[]{:S(2)}) copy-start(f32[2,38,8,128]{3,2,1,0:T(8,128)} %param.7) | copy-start | bytes 933892
  0.6 10.9 %copy-start.1 = (s32[37,8,128]{2,1,0:T(8,128)S(1)}, s32[37,8,128]{2,1,0:T(8,128)}, u32[]{:S(2)}) copy-start(s32[37,8,128]{2,1,0:T(8,128)} %param.12) | copy-start | bytes 454660
  0.7 10.9 %copy-start.2 = (s32[8,128]{1,0:T(8,128)S(1)}, s32[8,128]{1,0:T(8,128)}, u32[]{:S(2)}) copy-start(s32[8,128]{1,0:T(8,128)} %bottom_ref.7) | copy-start | bytes 12292
  0.7 10.9 %copy-start.3 = (s32[2,8,64]{2,1,0:T(8,128)S(1)}, s32[2,8,64]{2,1,0:T(8,128)}, u32[]{:S(2)}) copy-start(s32[2,8,64]{2,1,0:T(8,128)} %offset_ref.3) | copy-start | bytes 12292
  0.7 10.9 %copy-start.4 = (f32[8]{0:T(128)S(1)}, f32[8]{0:T(128)}, u32[]{:S(2)}) copy-start(f32[8]{0:T(128)} %table_ref.1) | copy-start | bytes 100
  3.3 27.3 %all-to-all-start = ((bf16[8,2,152,128]{3,2,1,0:T(8,128)(2,1)}), bf16[8,2,152,128]{3,2,1,0:T(8,128)(2,1)S(1)}, u32[]{:S(2)}, u32[]{:S(2)}) async-start(bf16[8,2,152,128]{3,2,1,0:T(8,128)(2,1)} %shard_map.86), calls=%async_computation | async-start | bytes 1245184 | tf_op jit(solution)/shard_map/all_to_all | solution.py:752
  31.0 13.4 %collective-permute-start = (bf16[8,768]{1,0:T(8,128)(2,1)S(1)}, bf16[8,768]{1,0:T(8,128)(2,1)S(1)}, u32[]{:S(2)}, u32[]{:S(2)}) collective-permute-start(bf16[8,768]{1,0:T(8,128)(2,1)S(1)} %get-tuple-element.24), channel_id=1, source_target_pairs={{8,16},{16,8},{24,32},{32,24},{40,48},{48,40},{56,64},{64,56},{72,... | collective-permute-start | bytes 36872 | tf_op jit(solution)/shard_map/ppermute | solution.py:780
  42.3 3.1 %collective-permute-start.1 = (bf16[8,768]{1,0:T(8,128)(2,1)S(1)}, bf16[8,768]{1,0:T(8,128)(2,1)S(1)}, u32[]{:S(2)}, u32[]{:S(2)}) collective-permute-start(bf16[8,768]{1,0:T(8,128)(2,1)S(1)} %get-tuple-element.25), channel_id=1, source_target_pairs={{0,8},{8,0},{16,24},{24,16},{32,40},{40,32},{48,56},{56,48},{64,72... | collective-permute-start | bytes 36872 | tf_op jit(solution)/shard_map/ppermute | solution.py:781
  45.7 13.0 %collective-permute-start.2 = (bf16[432,128]{1,0:T(8,128)(2,1)S(1)}, bf16[432,128]{1,0:T(8,128)(2,1)S(1)}, u32[]{:S(2)}, u32[]{:S(2)}) collective-permute-start(bf16[432,128]{1,0:T(8,128)(2,1)S(1)} %get-tuple-element.31), channel_id=1, source_target_pairs={{1,2},{2,1},{3,4},{4,3},{5,6},{6,5},{7,511},{511,7},{9,10},{10,9},... | collective-permute-start | bytes 331784 | tf_op jit(solution)/shard_map/ppermute | solution.py:802
  48.5 10.2 %collective-permute-start.3 = (bf16[432,128]{1,0:T(8,128)(2,1)S(1)}, bf16[432,128]{1,0:T(8,128)(2,1)S(1)}, u32[]{:S(2)}, u32[]{:S(2)}) collective-permute-start(bf16[432,128]{1,0:T(8,128)(2,1)S(1)} %get-tuple-element.32), channel_id=1, source_target_pairs={{0,1},{1,0},{2,3},{3,2},{4,5},{5,4},{6,7},{7,6},{8,9},{9,8},{10,11... | collective-permute-start | bytes 331784 | tf_op jit(solution)/shard_map/ppermute | solution.py:803

commit v8 on v7

--- a/solution.py
+++ b/solution.py
@@ -279,8 +279,8 @@
 
 def complete_kernel(
     levels,
+    inner_ref,
     outer_ref,
-    inner_ref,
     top_draft_ref,
     bot_draft_ref,
     far_ref,
@@ -797,7 +797,7 @@
         ],
         [(LANES, EDGE_LANES), (EDGE_LANES, LANES), (layout.rows, LANES), (layout.rows, LANES)],
         [],
-        [outer, inner, top, bot],
+        [inner, outer, top, bot],
     )
     far = lax.ppermute(far, ("lon", "lat"), far_routes)
     near = lax.ppermute(near, ("lon", "lat"), near_routes)

time: 60.4 us -> 61 us (level)
  starting transfers between devices: 26.6 us -> 27.3 us
    ppermute x1, waiting for transfers between devices: 0.01 us -> 1.13 us  [shards(): outer = lax.ppermute(outer, 'lon', outer_routes)]
    ppermute x1, waiting for transfers between devices: 0.9 us -> 0.01 us  [shards(): inner = lax.ppermute(inner, 'lon', inner_routes)]
    ppermute x1, starting transfers between devices: 11.2 us -> 12 us  [shards(): outer = lax.ppermute(outer, 'lon', outer_routes)]
where the time goes in v8:
time: 61 us; the launch traced here: 60.7 us
  starting transfers between devices  27.3 us (45%)
  waiting for transfers between devices  23.9 us (39%)
  Pallas kernels  8.69 us (14%)
  between operations  0.78 us (1%)
    all_to_all x1, waiting for transfers between devices, shards(): lax.all_to_all(request, 'lat', split_axis=0, concat_axis=0, tiled=True)  17.7 us
    ppermute x1, starting transfers between devices, shards(): outer = lax.ppermute(outer, 'lon', outer_routes)  12 us
    all_to_all x1, starting transfers between devices, shards(): lax.all_to_all(request, 'lat', split_axis=0, concat_axis=0, tiled=True)  8.25 us
    ppermute x1, waiting for transfers between devices, shards(): far = lax.ppermute(far, ('lon', 'lat'), far_routes)  5.01 us
    pallas_call x6, Pallas kernels, call(): pl.pallas_call(kernel, out_shape=[jax.ShapeDtypeStruct(shape, dtype) for...  4.74 us
    ppermute x1, starting transfers between devices, shards(): far = lax.ppermute(far, ('lon', 'lat'), far_routes)  3.24 us
    pallas_call x1, Pallas kernels, shards(): pl.pallas_call(request_kernel, out_shape=jax.ShapeDtypeStruct((bands, ste...  2.61 us
    ppermute x1, starting transfers between devices, shards(): inner = lax.ppermute(inner, 'lon', inner_routes)  1.93 us
  transfers between devices with their start and end apart: 5, of which 3 were waited for; matrix products, arithmetic and copies ran while one was open for 0% of the time, Pallas kernels for 7%

profile of v8, /device:TPU:22, one launch (start us, length us, event | category | flops | bytes accessed | tf_op | source)
XLA Modules:
  0.0 60.7 jit_solution(7308792410283429633)
XLA Ops:
  0.6 0.0 copy-start
  0.6 0.0 copy-start.1
  0.7 2.6 %shard_map.86 = bf16[8,2,152,128]{3,2,1,0:T(8,128)(2,1)} custom-call(s32[2,8,64]{2,1,0:T(8,128)} %slot_hbm.1, bf16[2432,128]{1,0:T(8,128)(2,1)} %bitcast.7), custom_call_target="tpu_custom_call" | custom-call | tf_op jit(solution)/shard_map/pallas_call | solution.py:733
  3.3 8.2 %all-to-all-start = ((bf16[8,2,152,128]{3,2,1,0:T(8,128)(2,1)}), bf16[8,2,152,128]{3,2,1,0:T(8,128)(2,1)S(1)}, u32[]{:S(2)}, u32[]{:S(2)}) async-start(bf16[8,2,152,128]{3,2,1,0:T(8,128)(2,1)} %shard_map.86), calls=%async_computation | async-start | bytes 1245184 | tf_op jit(solution)/shard_map/all_to_all | solution.py:752
  11.6 0.0 copy-done.1
  11.6 0.0 copy-done.2
  11.6 0.0 copy-done.3
  11.6 0.0 copy-done.4
  11.6 1.3 %shard_map.87 = (f32[608,128]{1,0:T(8,128)S(1)}, f32[608,128]{1,0:T(8,128)S(1)}, f32[312,128]{1,0:T(8,128)S(1)}, f32[32,256]{1,0:T(8,128)S(1)}, bf16[2,1024,128]...) custom-call(f32[8]{0:T(128)S(1)} %copy-done.4, s32[2,8,64]{2,1,0:T(8,128)S(1)} %copy-done.3, f32[608,128]{1,0:T(8,128)S(1)} %bitcast.5, ...), custom_call_target="tpu_custom_call" | custom-call | tf_op jit(solution)/shard_map/pallas_call | solution.py:712
  12.9 17.7 %all-to-all-done.piece_ref = bf16[8,2,152,128]{3,2,1,0:T(8,128)(2,1)S(1)} async-done(((bf16[8,2,152,128]{3,2,1,0:T(8,128)(2,1)}), bf16[8,2,152,128]{3,2,1,0:T(8,128)(2,1)S(1)}, u32[]{:S(2)}, u32[]{:S(2)}) %all-to-all-start) | async-done | bytes 622624 | tf_op jit(solution)/shard_map/all_to_all | solution.py:752
  30.6 0.4 shard_map.88
  31.0 1.9 %collective-permute-start = (bf16[8,768]{1,0:T(8,128)(2,1)S(1)}, bf16[8,768]{1,0:T(8,128)(2,1)S(1)}, u32[]{:S(2)}, u32[]{:S(2)}) collective-permute-start(bf16[8,768]{1,0:T(8,128)(2,1)S(1)} %get-tuple-element.24), channel_id=1, source_target_pairs={{0,8},{8,0},{16,24},{24,16},{32,40},{40,32},{48,56},{56,48},{64,72... | collective-permute-start | bytes 36872 | tf_op jit(solution)/shard_map/ppermute | solution.py:781
  33.0 12.0 %collective-permute-start.1 = (bf16[8,768]{1,0:T(8,128)(2,1)S(1)}, bf16[8,768]{1,0:T(8,128)(2,1)S(1)}, u32[]{:S(2)}, u32[]{:S(2)}) collective-permute-start(bf16[8,768]{1,0:T(8,128)(2,1)S(1)} %get-tuple-element.25), channel_id=1, source_target_pairs={{8,16},{16,8},{24,32},{32,24},{40,48},{48,40},{56,64},{64,56},{72,... | collective-permute-start | bytes 36872 | tf_op jit(solution)/shard_map/ppermute | solution.py:780
  44.9 0.2 shard_map.89
  45.2 0.0 collective-permute-done.inner_ref
  45.2 1.1 %collective-permute-done.1.outer_ref = bf16[8,768]{1,0:T(8,128)(2,1)S(1)} collective-permute-done((bf16[8,768]{1,0:T(8,128)(2,1)S(1)}, bf16[8,768]{1,0:T(8,128)(2,1)S(1)}, u32[]{:S(2)}, u32[]{:S(2)}) %collective-permute-start.1) | collective-permute-done | bytes 12320 | tf_op jit(solution)/shard_map/ppermute | solution.py:780
  46.3 0.3 shard_map.90
  46.7 3.2 %collective-permute-start.2 = (bf16[432,128]{1,0:T(8,128)(2,1)S(1)}, bf16[432,128]{1,0:T(8,128)(2,1)S(1)}, u32[]{:S(2)}, u32[]{:S(2)}) collective-permute-start(bf16[432,128]{1,0:T(8,128)(2,1)S(1)} %get-tuple-element.31), channel_id=1, source_target_pairs={{1,2},{2,1},{3,4},{4,3},{5,6},{6,5},{7,511},{511,7},{9,10},{10,9},... | collective-permute-start | bytes 331784 | tf_op jit(solution)/shard_map/ppermute | solution.py:802
  49.9 1.9 %collective-permute-start.3 = (bf16[432,128]{1,0:T(8,128)(2,1)S(1)}, bf16[432,128]{1,0:T(8,128)(2,1)S(1)}, u32[]{:S(2)}, u32[]{:S(2)}) collective-permute-start(bf16[432,128]{1,0:T(8,128)(2,1)S(1)} %get-tuple-element.32), channel_id=1, source_target_pairs={{0,1},{1,0},{2,3},{3,2},{4,5},{5,4},{6,7},{7,6},{8,9},{9,8},{10,11... | collective-permute-start | bytes 331784 | tf_op jit(solution)/shard_map/ppermute | solution.py:803
  51.8 1.0 %shard_map.91.state_ref = f32[2432,128]{1,0:T(8,128)S(1)} custom-call(s32[2,8,64]{2,1,0:T(8,128)S(1)} %copy-done.3, bf16[8,2,152,128]{3,2,1,0:T(8,128)(2,1)S(1)} %all-to-all-done.piece_ref, bf16[8,768]{1,0:T(8,128)(2,1)S(1)} %get-tuple-element.34.west_ref), custom_call_target="tpu_custom_call" | custom-call | tf_op jit(solution)/shard_map/pallas_call | solution.py:712
  52.8 1.5 %shard_map.92 = (f32[608,128]{1,0:T(8,128)S(1)}, f32[608,128]{1,0:T(8,128)S(1)}, f32[608,128]{1,0:T(8,128)S(1)}) custom-call(bf16[8,768]{1,0:T(8,128)(2,1)S(1)} %get-tuple-element.34.west_ref, bf16[8,768]{1,0:T(8,128)(2,1)S(1)} %get-tuple-element.35.east_ref, f32[2432,128]{1,0:T(8,128)S(1)} %shard_map.91.state_ref, ...), custom_call_target="tpu_custom_call" | custom-call | tf_op jit(solution)/shard_map/pallas_call | solution.py:712
  54.3 5.0 %collective-permute-done.2.far_ref = bf16[432,128]{1,0:T(8,128)(2,1)S(1)} collective-permute-done((bf16[432,128]{1,0:T(8,128)(2,1)S(1)}, bf16[432,128]{1,0:T(8,128)(2,1)S(1)}, u32[]{:S(2)}, u32[]{:S(2)}) %collective-permute-start.2) | collective-permute-done | bytes 110624 | tf_op jit(solution)/shard_map/ppermute | solution.py:802
  59.3 0.0 collective-permute-done.3.near_ref
  59.3 1.3 %shard_map.93 = (f32[608,128]{1,0:T(8,128)}, f32[608,128]{1,0:T(8,128)}, f32[608,128]{1,0:T(8,128)S(1)}, f32[608,128]{1,0:T(8,128)S(1)}) custom-call(bf16[432,128]{1,0:T(8,128)(2,1)S(1)} %collective-permute-done.2.far_ref, bf16[432,128]{1,0:T(8,128)(2,1)S(1)} %collective-permute-done.3.near_ref, ...), custom_call_target="tpu_custom_call", output_to_operand_aliasing={{2}: (10, {}), {3}: (11, {})} | custom-call | tf_op jit(solution)/shard_map/pallas_call | solution.py:821
  (4 shorter events, 0.0 us)
Async XLA Ops:
  0.6 10.9 %copy-start = (f32[2,38,8,128]{3,2,1,0:T(8,128)S(1)}, f32[2,38,8,128]{3,2,1,0:T(8,128)}, u32[]{:S(2)}) copy-start(f32[2,38,8,128]{3,2,1,0:T(8,128)} %param.7) | copy-start | bytes 933892
  0.6 10.9 %copy-start.1 = (s32[37,8,128]{2,1,0:T(8,128)S(1)}, s32[37,8,128]{2,1,0:T(8,128)}, u32[]{:S(2)}) copy-start(s32[37,8,128]{2,1,0:T(8,128)} %param.12) | copy-start | bytes 454660
  0.7 10.9 %copy-start.2 = (s32[8,128]{1,0:T(8,128)S(1)}, s32[8,128]{1,0:T(8,128)}, u32[]{:S(2)}) copy-start(s32[8,128]{1,0:T(8,128)} %bottom_ref.7) | copy-start | bytes 12292
  0.7 10.9 %copy-start.3 = (s32[2,8,64]{2,1,0:T(8,128)S(1)}, s32[2,8,64]{2,1,0:T(8,128)}, u32[]{:S(2)}) copy-start(s32[2,8,64]{2,1,0:T(8,128)} %offset_ref.3) | copy-start | bytes 12292
  0.7 10.9 %copy-start.4 = (f32[8]{0:T(128)S(1)}, f32[8]{0:T(128)}, u32[]{:S(2)}) copy-start(f32[8]{0:T(128)} %table_ref.1) | copy-start | bytes 100
  3.3 27.3 %all-to-all-start = ((bf16[8,2,152,128]{3,2,1,0:T(8,128)(2,1)}), bf16[8,2,152,128]{3,2,1,0:T(8,128)(2,1)S(1)}, u32[]{:S(2)}, u32[]{:S(2)}) async-start(bf16[8,2,152,128]{3,2,1,0:T(8,128)(2,1)} %shard_map.86), calls=%async_computation | async-start | bytes 1245184 | tf_op jit(solution)/shard_map/all_to_all | solution.py:752
  31.0 14.1 %collective-permute-start = (bf16[8,768]{1,0:T(8,128)(2,1)S(1)}, bf16[8,768]{1,0:T(8,128)(2,1)S(1)}, u32[]{:S(2)}, u32[]{:S(2)}) collective-permute-start(bf16[8,768]{1,0:T(8,128)(2,1)S(1)} %get-tuple-element.24), channel_id=1, source_target_pairs={{0,8},{8,0},{16,24},{24,16},{32,40},{40,32},{48,56},{56,48},{64,72... | collective-permute-start | bytes 36872 | tf_op jit(solution)/shard_map/ppermute | solution.py:781
  33.0 13.3 %collective-permute-start.1 = (bf16[8,768]{1,0:T(8,128)(2,1)S(1)}, bf16[8,768]{1,0:T(8,128)(2,1)S(1)}, u32[]{:S(2)}, u32[]{:S(2)}) collective-permute-start(bf16[8,768]{1,0:T(8,128)(2,1)S(1)} %get-tuple-element.25), channel_id=1, source_target_pairs={{8,16},{16,8},{24,32},{32,24},{40,48},{48,40},{56,64},{64,56},{72,... | collective-permute-start | bytes 36872 | tf_op jit(solution)/shard_map/ppermute | solution.py:780
  46.7 12.7 %collective-permute-start.2 = (bf16[432,128]{1,0:T(8,128)(2,1)S(1)}, bf16[432,128]{1,0:T(8,128)(2,1)S(1)}, u32[]{:S(2)}, u32[]{:S(2)}) collective-permute-start(bf16[432,128]{1,0:T(8,128)(2,1)S(1)} %get-tuple-element.31), channel_id=1, source_target_pairs={{1,2},{2,1},{3,4},{4,3},{5,6},{6,5},{7,511},{511,7},{9,10},{10,9},... | collective-permute-start | bytes 331784 | tf_op jit(solution)/shard_map/ppermute | solution.py:802
  49.9 9.4 %collective-permute-start.3 = (bf16[432,128]{1,0:T(8,128)(2,1)S(1)}, bf16[432,128]{1,0:T(8,128)(2,1)S(1)}, u32[]{:S(2)}, u32[]{:S(2)}) collective-permute-start(bf16[432,128]{1,0:T(8,128)(2,1)S(1)} %get-tuple-element.32), channel_id=1, source_target_pairs={{0,1},{1,0},{2,3},{3,2},{4,5},{5,4},{6,7},{7,6},{8,9},{9,8},{10,11... | collective-permute-start | bytes 331784 | tf_op jit(solution)/shard_map/ppermute | solution.py:803

commit v9 on v7

--- a/solution.py
+++ b/solution.py
@@ -531,19 +531,25 @@
     top_band = (band == lax.axis_size("lat") - 1).astype(jnp.int32)
     folded = top_band.astype(jnp.float32)
     open_south = jnp.where(band > 0, DIFFUSE, 0.0)
-    square = (LANES, LANES)
-    from_lane = rows_of(square)
-    turned = from_lane + top_band * (LANES - 1 - 2 * from_lane)
-    turn = jnp.where(lanes_of(square) == turned, 1.0, 0.0).astype(jnp.bfloat16)
+
+    @pl.when(odd_band & (top_band == 0))
+    def _():
+        north_ref[...] = far_ref[...].astype(jnp.float32)
+
+    @pl.when(odd_band & (top_band == 1))
+    def _():
+        square = (LANES, LANES)
+        turn = lanes_of(square) + rows_of(square) == LANES - 1
+        turn = jnp.where(turn, 1.0, 0.0).astype(jnp.bfloat16)
+        north_ref[...] = jnp.dot(far_ref[...], turn, preferred_element_type=jnp.float32)
 
     @pl.when(odd_band)
     def _():
-        north_ref[...] = jnp.dot(far_ref[...], turn, preferred_element_type=jnp.float32)
         south_ref[...] = near_ref[...].astype(jnp.float32)
 
     @pl.when(jnp.logical_not(odd_band))
     def _():
-        north_ref[...] = jnp.dot(near_ref[...], turn, preferred_element_type=jnp.float32)
+        north_ref[...] = near_ref[...].astype(jnp.float32)
         south_ref[...] = far_ref[...].astype(jnp.float32)
 
     copies = []

time: 60.4 us -> 60.2 us (level)
  no operation moved by 1% of the time
where the time goes in v9:
time: 60.2 us; the launch traced here: 59.9 us
  starting transfers between devices  26.6 us (44%)
  waiting for transfers between devices  24 us (40%)
  Pallas kernels  8.5 us (14%)
  between operations  0.78 us (1%)
    all_to_all x1, waiting for transfers between devices, shards(): lax.all_to_all(request, 'lat', split_axis=0, concat_axis=0, tiled=True)  17.7 us
    ppermute x1, starting transfers between devices, shards(): outer = lax.ppermute(outer, 'lon', outer_routes)  11.2 us
    all_to_all x1, starting transfers between devices, shards(): lax.all_to_all(request, 'lat', split_axis=0, concat_axis=0, tiled=True)  8.25 us
    ppermute x1, waiting for transfers between devices, shards(): far = lax.ppermute(far, ('lon', 'lat'), far_routes)  5.32 us
    pallas_call x6, Pallas kernels, call(): pl.pallas_call(kernel, out_shape=[jax.ShapeDtypeStruct(shape, dtype) for...  4.74 us
    ppermute x1, starting transfers between devices, shards(): far = lax.ppermute(far, ('lon', 'lat'), far_routes)  2.81 us
    pallas_call x1, Pallas kernels, shards(): pl.pallas_call(request_kernel, out_shape=jax.ShapeDtypeStruct((bands, ste...  2.61 us
    ppermute x1, starting transfers between devices, shards(): near = lax.ppermute(near, ('lon', 'lat'), near_routes)  2.42 us
  transfers between devices with their start and end apart: 5, of which 3 were waited for; matrix products, arithmetic and copies ran while one was open for 0% of the time, Pallas kernels for 7%

profile of v9, /device:TPU:22, one launch (start us, length us, event | category | flops | bytes accessed | tf_op | source)
XLA Modules:
  0.0 59.9 jit_solution(15085864781851447400)
XLA Ops:
  0.6 0.0 copy-start
  0.6 0.0 copy-start.1
  0.7 0.0 copy-start.2
  0.7 0.0 copy-start.3
  0.7 0.0 copy-start.4
  0.7 2.6 %shard_map.86 = bf16[8,2,152,128]{3,2,1,0:T(8,128)(2,1)} custom-call(s32[2,8,64]{2,1,0:T(8,128)} %slot_hbm.1, bf16[2432,128]{1,0:T(8,128)(2,1)} %bitcast.7), custom_call_target="tpu_custom_call" | custom-call | tf_op jit(solution)/shard_map/pallas_call | solution.py:739
  3.3 8.2 %all-to-all-start = ((bf16[8,2,152,128]{3,2,1,0:T(8,128)(2,1)}), bf16[8,2,152,128]{3,2,1,0:T(8,128)(2,1)S(1)}, u32[]{:S(2)}, u32[]{:S(2)}) async-start(bf16[8,2,152,128]{3,2,1,0:T(8,128)(2,1)} %shard_map.86), calls=%async_computation | async-start | bytes 1245184 | tf_op jit(solution)/shard_map/all_to_all | solution.py:758
  11.5 0.0 copy-done
  11.6 1.3 %shard_map.87 = (f32[608,128]{1,0:T(8,128)S(1)}, f32[608,128]{1,0:T(8,128)S(1)}, f32[312,128]{1,0:T(8,128)S(1)}, f32[32,256]{1,0:T(8,128)S(1)}, bf16[2,1024,128]...) custom-call(f32[8]{0:T(128)S(1)} %copy-done.4, s32[2,8,64]{2,1,0:T(8,128)S(1)} %copy-done.3, f32[608,128]{1,0:T(8,128)S(1)} %bitcast.5, ...), custom_call_target="tpu_custom_call" | custom-call | tf_op jit(solution)/shard_map/pallas_call | solution.py:718
  12.9 17.7 %all-to-all-done.piece_ref = bf16[8,2,152,128]{3,2,1,0:T(8,128)(2,1)S(1)} async-done(((bf16[8,2,152,128]{3,2,1,0:T(8,128)(2,1)}), bf16[8,2,152,128]{3,2,1,0:T(8,128)(2,1)S(1)}, u32[]{:S(2)}, u32[]{:S(2)}) %all-to-all-start) | async-done | bytes 622624 | tf_op jit(solution)/shard_map/all_to_all | solution.py:758
  30.6 0.4 shard_map.88
  31.0 11.2 %collective-permute-start = (bf16[8,768]{1,0:T(8,128)(2,1)S(1)}, bf16[8,768]{1,0:T(8,128)(2,1)S(1)}, u32[]{:S(2)}, u32[]{:S(2)}) collective-permute-start(bf16[8,768]{1,0:T(8,128)(2,1)S(1)} %get-tuple-element.24), channel_id=1, source_target_pairs={{8,16},{16,8},{24,32},{32,24},{40,48},{48,40},{56,64},{64,56},{72,... | collective-permute-start | bytes 36872 | tf_op jit(solution)/shard_map/ppermute | solution.py:786
  42.3 1.9 %collective-permute-start.1 = (bf16[8,768]{1,0:T(8,128)(2,1)S(1)}, bf16[8,768]{1,0:T(8,128)(2,1)S(1)}, u32[]{:S(2)}, u32[]{:S(2)}) collective-permute-start(bf16[8,768]{1,0:T(8,128)(2,1)S(1)} %get-tuple-element.25), channel_id=1, source_target_pairs={{0,8},{8,0},{16,24},{24,16},{32,40},{40,32},{48,56},{56,48},{64,72... | collective-permute-start | bytes 36872 | tf_op jit(solution)/shard_map/ppermute | solution.py:787
  44.2 0.2 shard_map.89
  44.4 0.0 collective-permute-done.outer_ref
  44.5 0.9 %collective-permute-done.1.inner_ref = bf16[8,768]{1,0:T(8,128)(2,1)S(1)} collective-permute-done((bf16[8,768]{1,0:T(8,128)(2,1)S(1)}, bf16[8,768]{1,0:T(8,128)(2,1)S(1)}, u32[]{:S(2)}, u32[]{:S(2)}) %collective-permute-start.1) | collective-permute-done | bytes 12320 | tf_op jit(solution)/shard_map/ppermute | solution.py:787
  45.3 0.3 shard_map.90
  45.7 2.8 %collective-permute-start.2 = (bf16[432,128]{1,0:T(8,128)(2,1)S(1)}, bf16[432,128]{1,0:T(8,128)(2,1)S(1)}, u32[]{:S(2)}, u32[]{:S(2)}) collective-permute-start(bf16[432,128]{1,0:T(8,128)(2,1)S(1)} %get-tuple-element.31), channel_id=1, source_target_pairs={{1,2},{2,1},{3,4},{4,3},{5,6},{6,5},{7,511},{511,7},{9,10},{10,9},... | collective-permute-start | bytes 331784 | tf_op jit(solution)/shard_map/ppermute | solution.py:808
  48.5 2.4 %collective-permute-start.3 = (bf16[432,128]{1,0:T(8,128)(2,1)S(1)}, bf16[432,128]{1,0:T(8,128)(2,1)S(1)}, u32[]{:S(2)}, u32[]{:S(2)}) collective-permute-start(bf16[432,128]{1,0:T(8,128)(2,1)S(1)} %get-tuple-element.32), channel_id=1, source_target_pairs={{0,1},{1,0},{2,3},{3,2},{4,5},{5,4},{6,7},{7,6},{8,9},{9,8},{10,11... | collective-permute-start | bytes 331784 | tf_op jit(solution)/shard_map/ppermute | solution.py:809
  50.9 1.0 %shard_map.91.state_ref = f32[2432,128]{1,0:T(8,128)S(1)} custom-call(s32[2,8,64]{2,1,0:T(8,128)S(1)} %copy-done.3, bf16[8,2,152,128]{3,2,1,0:T(8,128)(2,1)S(1)} %all-to-all-done.piece_ref, bf16[8,768]{1,0:T(8,128)(2,1)S(1)} %get-tuple-element.34.west_ref), custom_call_target="tpu_custom_call" | custom-call | tf_op jit(solution)/shard_map/pallas_call | solution.py:718
  51.9 1.5 %shard_map.92 = (f32[608,128]{1,0:T(8,128)S(1)}, f32[608,128]{1,0:T(8,128)S(1)}, f32[608,128]{1,0:T(8,128)S(1)}) custom-call(bf16[8,768]{1,0:T(8,128)(2,1)S(1)} %get-tuple-element.34.west_ref, bf16[8,768]{1,0:T(8,128)(2,1)S(1)} %get-tuple-element.35.east_ref, f32[2432,128]{1,0:T(8,128)S(1)} %shard_map.91.state_ref, ...), custom_call_target="tpu_custom_call" | custom-call | tf_op jit(solution)/shard_map/pallas_call | solution.py:718
  53.4 5.3 %collective-permute-done.2.far_ref = bf16[432,128]{1,0:T(8,128)(2,1)S(1)} collective-permute-done((bf16[432,128]{1,0:T(8,128)(2,1)S(1)}, bf16[432,128]{1,0:T(8,128)(2,1)S(1)}, u32[]{:S(2)}, u32[]{:S(2)}) %collective-permute-start.2) | collective-permute-done | bytes 110624 | tf_op jit(solution)/shard_map/ppermute | solution.py:808
  58.7 0.0 collective-permute-done.3.near_ref
  58.7 1.1 %shard_map.93 = (f32[608,128]{1,0:T(8,128)}, f32[608,128]{1,0:T(8,128)}, f32[608,128]{1,0:T(8,128)S(1)}, f32[608,128]{1,0:T(8,128)S(1)}) custom-call(bf16[432,128]{1,0:T(8,128)(2,1)S(1)} %collective-permute-done.2.far_ref, bf16[432,128]{1,0:T(8,128)(2,1)S(1)} %collective-permute-done.3.near_ref, ...), custom_call_target="tpu_custom_call", output_to_operand_aliasing={{2}: (10, {}), {3}: (11, {})} | custom-call | tf_op jit(solution)/shard_map/pallas_call | solution.py:827
  (4 shorter events, 0.0 us)
Async XLA Ops:
  0.6 10.9 %copy-start = (f32[2,38,8,128]{3,2,1,0:T(8,128)S(1)}, f32[2,38,8,128]{3,2,1,0:T(8,128)}, u32[]{:S(2)}) copy-start(f32[2,38,8,128]{3,2,1,0:T(8,128)} %param.7) | copy-start | bytes 933892
  0.6 10.9 %copy-start.1 = (s32[37,8,128]{2,1,0:T(8,128)S(1)}, s32[37,8,128]{2,1,0:T(8,128)}, u32[]{:S(2)}) copy-start(s32[37,8,128]{2,1,0:T(8,128)} %param.12) | copy-start | bytes 454660
  0.7 10.9 %copy-start.2 = (s32[8,128]{1,0:T(8,128)S(1)}, s32[8,128]{1,0:T(8,128)}, u32[]{:S(2)}) copy-start(s32[8,128]{1,0:T(8,128)} %bottom_ref.7) | copy-start | bytes 12292
  0.7 10.9 %copy-start.3 = (s32[2,8,64]{2,1,0:T(8,128)S(1)}, s32[2,8,64]{2,1,0:T(8,128)}, u32[]{:S(2)}) copy-start(s32[2,8,64]{2,1,0:T(8,128)} %offset_ref.3) | copy-start | bytes 12292
  0.7 10.9 %copy-start.4 = (f32[8]{0:T(128)S(1)}, f32[8]{0:T(128)}, u32[]{:S(2)}) copy-start(f32[8]{0:T(128)} %table_ref.1) | copy-start | bytes 100
  3.3 27.3 %all-to-all-start = ((bf16[8,2,152,128]{3,2,1,0:T(8,128)(2,1)}), bf16[8,2,152,128]{3,2,1,0:T(8,128)(2,1)S(1)}, u32[]{:S(2)}, u32[]{:S(2)}) async-start(bf16[8,2,152,128]{3,2,1,0:T(8,128)(2,1)} %shard_map.86), calls=%async_computation | async-start | bytes 1245184 | tf_op jit(solution)/shard_map/all_to_all | solution.py:758
  31.0 13.4 %collective-permute-start = (bf16[8,768]{1,0:T(8,128)(2,1)S(1)}, bf16[8,768]{1,0:T(8,128)(2,1)S(1)}, u32[]{:S(2)}, u32[]{:S(2)}) collective-permute-start(bf16[8,768]{1,0:T(8,128)(2,1)S(1)} %get-tuple-element.24), channel_id=1, source_target_pairs={{8,16},{16,8},{24,32},{32,24},{40,48},{48,40},{56,64},{64,56},{72,... | collective-permute-start | bytes 36872 | tf_op jit(solution)/shard_map/ppermute | solution.py:786
  42.3 3.1 %collective-permute-start.1 = (bf16[8,768]{1,0:T(8,128)(2,1)S(1)}, bf16[8,768]{1,0:T(8,128)(2,1)S(1)}, u32[]{:S(2)}, u32[]{:S(2)}) collective-permute-start(bf16[8,768]{1,0:T(8,128)(2,1)S(1)} %get-tuple-element.25), channel_id=1, source_target_pairs={{0,8},{8,0},{16,24},{24,16},{32,40},{40,32},{48,56},{56,48},{64,72... | collective-permute-start | bytes 36872 | tf_op jit(solution)/shard_map/ppermute | solution.py:787
  45.7 13.0 %collective-permute-start.2 = (bf16[432,128]{1,0:T(8,128)(2,1)S(1)}, bf16[432,128]{1,0:T(8,128)(2,1)S(1)}, u32[]{:S(2)}, u32[]{:S(2)}) collective-permute-start(bf16[432,128]{1,0:T(8,128)(2,1)S(1)} %get-tuple-element.31), channel_id=1, source_target_pairs={{1,2},{2,1},{3,4},{4,3},{5,6},{6,5},{7,511},{511,7},{9,10},{10,9},... | collective-permute-start | bytes 331784 | tf_op jit(solution)/shard_map/ppermute | solution.py:808
  48.5 10.2 %collective-permute-start.3 = (bf16[432,128]{1,0:T(8,128)(2,1)S(1)}, bf16[432,128]{1,0:T(8,128)(2,1)S(1)}, u32[]{:S(2)}, u32[]{:S(2)}) collective-permute-start(bf16[432,128]{1,0:T(8,128)(2,1)S(1)} %get-tuple-element.32), channel_id=1, source_target_pairs={{0,1},{1,0},{2,3},{3,2},{4,5},{5,4},{6,7},{7,6},{8,9},{9,8},{10,11... | collective-permute-start | bytes 331784 | tf_op jit(solution)/shard_map/ppermute | solution.py:809

commit v10 on v9

--- a/solution.py
+++ b/solution.py
@@ -57,18 +57,19 @@
     tile = lax.axis_index("lon")
     bands, steps, pieces, lanes = pack_ref.shape
     slots = store_ref.shape[0] // pieces
-    length = store_ref.shape[0] // FIELDS
+    parts = 2 * FIELDS
+    length = store_ref.shape[0] // parts
     table = pltpu.make_async_copy(slot_hbm, slot_ref, slot_sem)
     table.start()
     loads = []
-    for field in range(FIELDS):
-        here = pl.ds(field * length, length)
-        load = pltpu.make_async_copy(store_hbm.at[here], store_ref.at[here], in_sem.at[field])
+    for part in range(parts):
+        here = pl.ds(part * length, length)
+        load = pltpu.make_async_copy(store_hbm.at[here], store_ref.at[here], in_sem.at[part])
         load.start()
         loads.append(load)
-    for field, load in enumerate(loads):
+    for part, load in enumerate(loads):
         load.wait()
-        here = slice(field * length, (field + 1) * length)
+        here = slice(part * length, (part + 1) * length)
         wide_ref[here] = store_ref[here].astype(jnp.float32)
     table.wait()
     stores = []
@@ -309,7 +310,6 @@
 
     top_ref[...] = top_draft_ref[...]
     bot_ref[...] = bot_draft_ref[...]
-    edge_ref[...] = jnp.zeros_like(edge_ref)
     edge_ref[0:ROWS] = west_ref[...].astype(jnp.float32)
     edge_ref[ROWS : 2 * ROWS] = east_ref[...].astype(jnp.float32)
     column_ref[...] = jnp.transpose(edge_ref[...])
@@ -747,7 +747,7 @@
             pltpu.VMEM((pieces * slots, LANES), wide),
             pltpu.VMEM((bands, steps, pieces, LANES), narrow),
             pltpu.SemaphoreType.DMA,
-            pltpu.SemaphoreType.DMA((FIELDS,)),
+            pltpu.SemaphoreType.DMA((2 * FIELDS,)),
             pltpu.SemaphoreType.DMA((bands,)),
         ],
         compiler_params=pltpu.CompilerParams(vmem_limit_bytes=32 * 1024 * 1024),

time: 60.2 us -> 60.2 us (level)
  no operation moved by 1% of the time
where the time goes in v10:
time: 60.2 us; the launch traced here: 59.9 us
  starting transfers between devices  26.6 us (44%)
  waiting for transfers between devices  24 us (40%)
  Pallas kernels  8.53 us (14%)
  between operations  0.78 us (1%)
    all_to_all x1, waiting for transfers between devices, shards(): lax.all_to_all(request, 'lat', split_axis=0, concat_axis=0, tiled=True)  17.7 us
    ppermute x1, starting transfers between devices, shards(): outer = lax.ppermute(outer, 'lon', outer_routes)  11.2 us
    all_to_all x1, starting transfers between devices, shards(): lax.all_to_all(request, 'lat', split_axis=0, concat_axis=0, tiled=True)  8.25 us
    ppermute x1, waiting for transfers between devices, shards(): far = lax.ppermute(far, ('lon', 'lat'), far_routes)  5.32 us
    pallas_call x6, Pallas kernels, call(): pl.pallas_call(kernel, out_shape=[jax.ShapeDtypeStruct(shape, dtype) for...  4.74 us
    ppermute x1, starting transfers between devices, shards(): far = lax.ppermute(far, ('lon', 'lat'), far_routes)  2.82 us
    pallas_call x1, Pallas kernels, shards(): pl.pallas_call(request_kernel, out_shape=jax.ShapeDtypeStruct((bands, ste...  2.64 us
    ppermute x1, starting transfers between devices, shards(): near = lax.ppermute(near, ('lon', 'lat'), near_routes)  2.4 us
  transfers between devices with their start and end apart: 5, of which 3 were waited for; matrix products, arithmetic and copies ran while one was open for 0% of the time, Pallas kernels for 7%

profile of v10, /device:TPU:22, one launch (start us, length us, event | category | flops | bytes accessed | tf_op | source)
XLA Modules:
  0.0 59.9 jit_solution(7693656085945393137)
XLA Ops:
  0.6 0.0 copy-start
  0.6 0.0 copy-start.1
  0.7 0.0 copy-start.2
  0.7 0.0 copy-start.3
  0.7 0.0 copy-start.4
  0.7 2.6 %shard_map.86 = bf16[8,2,152,128]{3,2,1,0:T(8,128)(2,1)} custom-call(s32[2,8,64]{2,1,0:T(8,128)} %slot_hbm.1, bf16[2432,128]{1,0:T(8,128)(2,1)} %bitcast.7), custom_call_target="tpu_custom_call" | custom-call | tf_op jit(solution)/shard_map/pallas_call | solution.py:739
  3.3 8.2 %all-to-all-start = ((bf16[8,2,152,128]{3,2,1,0:T(8,128)(2,1)}), bf16[8,2,152,128]{3,2,1,0:T(8,128)(2,1)S(1)}, u32[]{:S(2)}, u32[]{:S(2)}) async-start(bf16[8,2,152,128]{3,2,1,0:T(8,128)(2,1)} %shard_map.86), calls=%async_computation | async-start | bytes 1245184 | tf_op jit(solution)/shard_map/all_to_all | solution.py:758
  11.6 0.0 copy-done
  11.6 1.3 %shard_map.87 = (f32[608,128]{1,0:T(8,128)S(1)}, f32[608,128]{1,0:T(8,128)S(1)}, f32[312,128]{1,0:T(8,128)S(1)}, f32[32,256]{1,0:T(8,128)S(1)}, bf16[2,1024,128]...) custom-call(f32[8]{0:T(128)S(1)} %copy-done.4, s32[2,8,64]{2,1,0:T(8,128)S(1)} %copy-done.3, f32[608,128]{1,0:T(8,128)S(1)} %bitcast.5, ...), custom_call_target="tpu_custom_call" | custom-call | tf_op jit(solution)/shard_map/pallas_call | solution.py:718
  12.9 17.7 %all-to-all-done.piece_ref = bf16[8,2,152,128]{3,2,1,0:T(8,128)(2,1)S(1)} async-done(((bf16[8,2,152,128]{3,2,1,0:T(8,128)(2,1)}), bf16[8,2,152,128]{3,2,1,0:T(8,128)(2,1)S(1)}, u32[]{:S(2)}, u32[]{:S(2)}) %all-to-all-start) | async-done | bytes 622624 | tf_op jit(solution)/shard_map/all_to_all | solution.py:758
  30.6 0.4 shard_map.88
  31.1 11.2 %collective-permute-start = (bf16[8,768]{1,0:T(8,128)(2,1)S(1)}, bf16[8,768]{1,0:T(8,128)(2,1)S(1)}, u32[]{:S(2)}, u32[]{:S(2)}) collective-permute-start(bf16[8,768]{1,0:T(8,128)(2,1)S(1)} %get-tuple-element.24), channel_id=1, source_target_pairs={{8,16},{16,8},{24,32},{32,24},{40,48},{48,40},{56,64},{64,56},{72,... | collective-permute-start | bytes 36872 | tf_op jit(solution)/shard_map/ppermute | solution.py:786
  42.3 1.9 %collective-permute-start.1 = (bf16[8,768]{1,0:T(8,128)(2,1)S(1)}, bf16[8,768]{1,0:T(8,128)(2,1)S(1)}, u32[]{:S(2)}, u32[]{:S(2)}) collective-permute-start(bf16[8,768]{1,0:T(8,128)(2,1)S(1)} %get-tuple-element.25), channel_id=1, source_target_pairs={{0,8},{8,0},{16,24},{24,16},{32,40},{40,32},{48,56},{56,48},{64,72... | collective-permute-start | bytes 36872 | tf_op jit(solution)/shard_map/ppermute | solution.py:787
  44.2 0.2 shard_map.89
  44.5 0.0 collective-permute-done.outer_ref
  44.5 0.9 %collective-permute-done.1.inner_ref = bf16[8,768]{1,0:T(8,128)(2,1)S(1)} collective-permute-done((bf16[8,768]{1,0:T(8,128)(2,1)S(1)}, bf16[8,768]{1,0:T(8,128)(2,1)S(1)}, u32[]{:S(2)}, u32[]{:S(2)}) %collective-permute-start.1) | collective-permute-done | bytes 12320 | tf_op jit(solution)/shard_map/ppermute | solution.py:787
  45.4 0.3 shard_map.90
  45.7 2.8 %collective-permute-start.2 = (bf16[432,128]{1,0:T(8,128)(2,1)S(1)}, bf16[432,128]{1,0:T(8,128)(2,1)S(1)}, u32[]{:S(2)}, u32[]{:S(2)}) collective-permute-start(bf16[432,128]{1,0:T(8,128)(2,1)S(1)} %get-tuple-element.31), channel_id=1, source_target_pairs={{1,2},{2,1},{3,4},{4,3},{5,6},{6,5},{7,511},{511,7},{9,10},{10,9},... | collective-permute-start | bytes 331784 | tf_op jit(solution)/shard_map/ppermute | solution.py:808
  48.6 2.4 %collective-permute-start.3 = (bf16[432,128]{1,0:T(8,128)(2,1)S(1)}, bf16[432,128]{1,0:T(8,128)(2,1)S(1)}, u32[]{:S(2)}, u32[]{:S(2)}) collective-permute-start(bf16[432,128]{1,0:T(8,128)(2,1)S(1)} %get-tuple-element.32), channel_id=1, source_target_pairs={{0,1},{1,0},{2,3},{3,2},{4,5},{5,4},{6,7},{7,6},{8,9},{9,8},{10,11... | collective-permute-start | bytes 331784 | tf_op jit(solution)/shard_map/ppermute | solution.py:809
  51.0 1.0 %shard_map.91.state_ref = f32[2432,128]{1,0:T(8,128)S(1)} custom-call(s32[2,8,64]{2,1,0:T(8,128)S(1)} %copy-done.3, bf16[8,2,152,128]{3,2,1,0:T(8,128)(2,1)S(1)} %all-to-all-done.piece_ref, bf16[8,768]{1,0:T(8,128)(2,1)S(1)} %get-tuple-element.34.west_ref), custom_call_target="tpu_custom_call" | custom-call | tf_op jit(solution)/shard_map/pallas_call | solution.py:718
  52.0 1.5 %shard_map.92 = (f32[608,128]{1,0:T(8,128)S(1)}, f32[608,128]{1,0:T(8,128)S(1)}, f32[608,128]{1,0:T(8,128)S(1)}) custom-call(bf16[8,768]{1,0:T(8,128)(2,1)S(1)} %get-tuple-element.34.west_ref, bf16[8,768]{1,0:T(8,128)(2,1)S(1)} %get-tuple-element.35.east_ref, f32[2432,128]{1,0:T(8,128)S(1)} %shard_map.91.state_ref, ...), custom_call_target="tpu_custom_call" | custom-call | tf_op jit(solution)/shard_map/pallas_call | solution.py:718
  53.4 5.3 %collective-permute-done.2.far_ref = bf16[432,128]{1,0:T(8,128)(2,1)S(1)} collective-permute-done((bf16[432,128]{1,0:T(8,128)(2,1)S(1)}, bf16[432,128]{1,0:T(8,128)(2,1)S(1)}, u32[]{:S(2)}, u32[]{:S(2)}) %collective-permute-start.2) | collective-permute-done | bytes 110624 | tf_op jit(solution)/shard_map/ppermute | solution.py:808
  58.8 0.0 collective-permute-done.3.near_ref
  58.8 1.1 %shard_map.93 = (f32[608,128]{1,0:T(8,128)}, f32[608,128]{1,0:T(8,128)}, f32[608,128]{1,0:T(8,128)S(1)}, f32[608,128]{1,0:T(8,128)S(1)}) custom-call(bf16[432,128]{1,0:T(8,128)(2,1)S(1)} %collective-permute-done.2.far_ref, bf16[432,128]{1,0:T(8,128)(2,1)S(1)} %collective-permute-done.3.near_ref, ...), custom_call_target="tpu_custom_call", output_to_operand_aliasing={{2}: (10, {}), {3}: (11, {})} | custom-call | tf_op jit(solution)/shard_map/pallas_call | solution.py:827
  (4 shorter events, 0.0 us)
Async XLA Ops:
  0.6 11.0 %copy-start = (f32[2,38,8,128]{3,2,1,0:T(8,128)S(1)}, f32[2,38,8,128]{3,2,1,0:T(8,128)}, u32[]{:S(2)}) copy-start(f32[2,38,8,128]{3,2,1,0:T(8,128)} %param.7) | copy-start | bytes 933892
  0.6 10.9 %copy-start.1 = (s32[37,8,128]{2,1,0:T(8,128)S(1)}, s32[37,8,128]{2,1,0:T(8,128)}, u32[]{:S(2)}) copy-start(s32[37,8,128]{2,1,0:T(8,128)} %param.12) | copy-start | bytes 454660
  0.7 10.9 %copy-start.2 = (s32[8,128]{1,0:T(8,128)S(1)}, s32[8,128]{1,0:T(8,128)}, u32[]{:S(2)}) copy-start(s32[8,128]{1,0:T(8,128)} %bottom_ref.7) | copy-start | bytes 12292
  0.7 10.9 %copy-start.3 = (s32[2,8,64]{2,1,0:T(8,128)S(1)}, s32[2,8,64]{2,1,0:T(8,128)}, u32[]{:S(2)}) copy-start(s32[2,8,64]{2,1,0:T(8,128)} %offset_ref.3) | copy-start | bytes 12292
  0.7 10.9 %copy-start.4 = (f32[8]{0:T(128)S(1)}, f32[8]{0:T(128)}, u32[]{:S(2)}) copy-start(f32[8]{0:T(128)} %table_ref.1) | copy-start | bytes 100
  3.3 27.3 %all-to-all-start = ((bf16[8,2,152,128]{3,2,1,0:T(8,128)(2,1)}), bf16[8,2,152,128]{3,2,1,0:T(8,128)(2,1)S(1)}, u32[]{:S(2)}, u32[]{:S(2)}) async-start(bf16[8,2,152,128]{3,2,1,0:T(8,128)(2,1)} %shard_map.86), calls=%async_computation | async-start | bytes 1245184 | tf_op jit(solution)/shard_map/all_to_all | solution.py:758
  31.1 13.4 %collective-permute-start = (bf16[8,768]{1,0:T(8,128)(2,1)S(1)}, bf16[8,768]{1,0:T(8,128)(2,1)S(1)}, u32[]{:S(2)}, u32[]{:S(2)}) collective-permute-start(bf16[8,768]{1,0:T(8,128)(2,1)S(1)} %get-tuple-element.24), channel_id=1, source_target_pairs={{8,16},{16,8},{24,32},{32,24},{40,48},{48,40},{56,64},{64,56},{72,... | collective-permute-start | bytes 36872 | tf_op jit(solution)/shard_map/ppermute | solution.py:786
  42.3 3.1 %collective-permute-start.1 = (bf16[8,768]{1,0:T(8,128)(2,1)S(1)}, bf16[8,768]{1,0:T(8,128)(2,1)S(1)}, u32[]{:S(2)}, u32[]{:S(2)}) collective-permute-start(bf16[8,768]{1,0:T(8,128)(2,1)S(1)} %get-tuple-element.25), channel_id=1, source_target_pairs={{0,8},{8,0},{16,24},{24,16},{32,40},{40,32},{48,56},{56,48},{64,72... | collective-permute-start | bytes 36872 | tf_op jit(solution)/shard_map/ppermute | solution.py:787
  45.7 13.0 %collective-permute-start.2 = (bf16[432,128]{1,0:T(8,128)(2,1)S(1)}, bf16[432,128]{1,0:T(8,128)(2,1)S(1)}, u32[]{:S(2)}, u32[]{:S(2)}) collective-permute-start(bf16[432,128]{1,0:T(8,128)(2,1)S(1)} %get-tuple-element.31), channel_id=1, source_target_pairs={{1,2},{2,1},{3,4},{4,3},{5,6},{6,5},{7,511},{511,7},{9,10},{10,9},... | collective-permute-start | bytes 331784 | tf_op jit(solution)/shard_map/ppermute | solution.py:808
  48.6 10.2 %collective-permute-start.3 = (bf16[432,128]{1,0:T(8,128)(2,1)S(1)}, bf16[432,128]{1,0:T(8,128)(2,1)S(1)}, u32[]{:S(2)}, u32[]{:S(2)}) collective-permute-start(bf16[432,128]{1,0:T(8,128)(2,1)S(1)} %get-tuple-element.32), channel_id=1, source_target_pairs={{0,1},{1,0},{2,3},{3,2},{4,5},{5,4},{6,7},{7,6},{8,9},{9,8},{10,11... | collective-permute-start | bytes 331784 | tf_op jit(solution)/shard_map/ppermute | solution.py:809
